TPU v7x, 512 devices: a whole 4x4x16 slice. The times are simulated.
512 devices in a mesh: src: 64 (over z_hi, x, y), tile: 8 (over z_lo, core).
Axes of the slice: x: 4, y: 4, z: 16 (z_hi: 4, z_lo: 4; z = z_hi * 4 + z_lo), core: 2. Of those that a mesh axis runs over, the one named last changes fastest.
Arguments:
- target: bfloat16 [128, 512, 256], P('src', 'tile'), may hold values from -6 to 6
- sources: bfloat16 [4096, 256], P('src'), may hold values from -6 to 6
- kernel_one: bfloat16 [6, 6, 1, 16], replicated, may hold values from -1 to 1
- first_conv_bias: float32 [16], replicated, may hold values from -3 to 3
- kernel_two: bfloat16 [6, 6, 16, 32], replicated, may hold values from -0.25 to 0.25
- shift_two: float32 [32], replicated, may hold values from -3 to 3
- kernel_three: bfloat16 [6, 6, 32, 64], replicated, may hold values from -0.1875 to 0.1875
- shift_three: float32 [64], replicated, may hold values from -3 to 3
- latents: float32 [8, 128], replicated, may hold values from -6 to 6
- pos_key: float32 [16, 64, 128], P(None, 'tile'), may hold values from -6 to 6
- w_key: float32 [64, 128], replicated, may hold values from -0.5 to 0.5
- value_weight: float32 [64, 128], replicated, may hold values from -0.75 to 0.75
Outputs:
- tokens: float32 [4096, 8, 128], P('src')
All inputs are finite; a program needn't handle non-finite values.
Results may differ from a plain program's by a relative error of at most 0.003.
Values may be sent and summed in bfloat16 or wider, within the bound.
No kernel may reach another device: no remote copies, remote signals or barrier semaphores. Data moves between devices by JAX's collectives and lax.ppermute only.
A program may use at most 64 MiB of HBM per device.

v0:
```python
import math

import jax
import jax.numpy as jnp
from jax import lax
from jax.sharding import PartitionSpec as P

highest_precision = lax.Precision.HIGHEST
conv_layout = ("HWCN", "HWIO", "HWCN")


def extended(array, sides, width):
    for axis, dim in sides:
        peers, length = (lax.axis_size(axis), array.shape[dim])
        up = [(i, (i + 1) % peers) for i in range(peers - 1)]
        down = [(j, i) for i, j in up]
        last = lax.slice_in_dim(array, length - width, length, axis=dim)
        first = lax.slice_in_dim(array, 0, width, axis=dim)
        before = lax.ppermute(last, axis, up)
        after = lax.ppermute(first, axis, down)
        array = jnp.concatenate([before, array, after], axis=dim)
    return array


def correlation_volume(target_rows, sources):
    corr_scale = 1.0 / math.sqrt(sources.shape[1])
    values = jnp.einsum("rwc,sc->rws", target_rows, sources, preferred_element_type=jnp.float32)
    return (values * corr_scale).astype(jnp.bfloat16)


def convolve(in_field, kernel_weights, bias_term):
    result = lax.conv_general_dilated(
        in_field,
        kernel_weights,
        (2, 2),
        "VALID",
        dimension_numbers=conv_layout,
        preferred_element_type=jnp.float32,
    )
    return result + bias_term[None, None, :, None]


def on_device(
    target,
    sources,
    kernel_one,
    first_conv_bias,
    kernel_two,
    shift_two,
    kernel_three,
    shift_three,
    latents,
    pos_key,
    w_key,
    value_weight,
):
    border = 7 * (kernel_one.shape[0] - 2) // 2
    padded = extended(target, (("tile", 1),), border)
    cost_map = correlation_volume(lax.all_gather(padded, "src", axis=0, tiled=True), sources)
    cost_map = jnp.pad(cost_map, ((border, border), (0, 0), (0, 0)))
    hidden_one = jax.nn.gelu(convolve(cost_map[:, :, None, :], kernel_one, first_conv_bias)).astype(
        jnp.bfloat16
    )
    hidden_two = jax.nn.gelu(convolve(hidden_one, kernel_two, shift_two)).astype(jnp.bfloat16)
    feature_maps = convolve(hidden_two, kernel_three, shift_three).astype(jnp.bfloat16)
    key_scale = 1.0 / math.sqrt(latents.shape[1])
    query_feat = jnp.dot(
        latents, w_key.T, precision=highest_precision, preferred_element_type=jnp.float32
    ).astype(jnp.bfloat16)
    pos_score = jnp.einsum("ld,hwd->lhw", latents, pos_key, precision=highest_precision)
    scores = jnp.einsum(
        "hwcs,lc->lhws", feature_maps, query_feat, preferred_element_type=jnp.float32
    )
    scores = (scores + pos_score[..., None]) * key_scale
    local_peak = jnp.max(scores, axis=(1, 2))
    feature_wide = feature_maps.astype(jnp.float32)
    peak_value = lax.pmax(local_peak, "tile")
    weights = jnp.exp(scores - peak_value[:, None, None, :])
    local_totals = jnp.sum(weights, axis=(1, 2))
    local_weighted = jnp.einsum(
        "lhws,hwcs->lcs", weights, feature_wide, precision=highest_precision
    )
    totals, weighted = lax.psum((local_totals, local_weighted), "tile")
    attended_latents = weighted / totals[:, None, :]
    return jnp.einsum("wnx,nj->xwj", attended_latents, value_weight, precision=highest_precision)


def solution(mesh):
    return jax.shard_map(
        on_device,
        mesh=mesh,
        in_specs=(
            P("src", "tile", None),
            P("src", None),
            P(),
            P(),
            P(),
            P(),
            P(),
            P(),
            P(),
            P(None, "tile", None),
            P(),
            P(),
        ),
        out_specs=P("src", None, None),
        check_vma=False,
    )
```

profile of v0, /device:TPU:1, one launch (start us, length us, event | category | flops | bytes accessed | tf_op | source)
XLA Modules:
  0.0 402.5 jit_solution(11853535515872133691)
XLA Ops:
  6.5 0.0 copy-start
  6.5 0.0 all-gather.2.cloned.1.call-start
  6.5 0.8 fusion.46
  7.3 4.9 %collective-permute-start = (bf16[2,14,256]{2,1,0:T(8,128)(2,1)S(1)}, bf16[2,14,256]{2,1,0:T(8,128)(2,1)S(1)}, u32[]{:S(2)}, u32[]{:S(2)}) collective-permute-start(bf16[2,14,256]{2,1,0:T(8,128)(2,1)S(1)} %get-tuple-element.7), channel_id=1, source_target_pairs={{0,1},{1,2},{2,3},{3,4},{4,5},{5,6},{6,7},{8,9},{9,10},{10,11},{11... | collective-permute-start | bytes 43016 | tf_op jit(solution)/shard_map/ppermute | solution.py:19
  12.3 5.1 %collective-permute-start.1 = (bf16[2,14,256]{2,1,0:T(8,128)(2,1)S(1)}, bf16[2,14,256]{2,1,0:T(8,128)(2,1)S(1)}, u32[]{:S(2)}, u32[]{:S(2)}) collective-permute-start(bf16[2,14,256]{2,1,0:T(8,128)(2,1)S(1)} %get-tuple-element.8), channel_id=1, source_target_pairs={{1,0},{2,1},{3,2},{4,3},{5,4},{6,5},{7,6},{9,8},{10,9},{11,10},{12... | collective-permute-start | bytes 43016 | tf_op jit(solution)/shard_map/ppermute | solution.py:20
  17.4 0.0 collective-permute-done
  17.4 0.8 collective-permute-done.1
  18.2 1.5 pad_maximum_fusion
  19.7 0.0 all-gather.2.cloned.1.call-update
  19.8 0.0 all-reduce.3.cloned.1.call-start
  19.8 0.9 fusion.27
  20.7 1.1 fusion.35
  21.8 165.6 %all-gather.2.cloned.1.call-done = bf16[128,92,256]{2,1,0:T(8,128)(2,1)} async-done(((bf16[2,92,256]{2,1,0:T(8,128)(2,1)}), bf16[128,92,256]{2,1,0:T(8,128)(2,1)}) %all-gather.2.cloned.1.call-update) | async-done | bytes 6029328 | tf_op jit(solution)/shard_map/all_gather | solution.py:59
  187.4 7.2 %fusion.31 = f32[128,92,64]{1,2,0:T(8,128)} fusion(bf16[128,92,256]{2,1,0:T(8,128)(2,1)} %all-gather.2.cloned.1.call-done, bf16[64,256]{1,0:T(8,128)(2,1)} %param.13), kind=kOutput, calls=%fused_computation.37 | convolution fusion | flops 385875968 | bytes 9076736 | tf_op jit(solution)/shard_map/rwc,sc->rws/dot_general | solution.py:27
  194.6 4.0 copy.30
  198.6 0.4 multiply_convert_fusion
  199.0 0.0 copy-start.2
  199.0 0.0 copy-start.4
  199.0 0.0 copy-start.5
  199.0 1.1 pad_bitcast_fusion
  200.1 12.4 %copy.23 = bf16[156,92,1,64]{3,2,1,0:T(2,128)(2,1)} copy(bf16[156,92,1,64]{0,3,1,2:T(8,128)(2,1)S(1)} %pad_bitcast_fusion) | data formatting | bytes 3674112 | tf_op jit(solution)/shard_map/broadcast_in_dim | solution.py:61
  212.6 0.0 copy-done.2
  212.6 0.0 copy-done.4
  212.6 0.0 copy-done.5
  212.6 0.0 copy-start.6
  212.6 0.0 copy-start.7
  212.6 66.3 %fusion.8 = f32[36,20,32,64]{3,2,1,0:T(8,128)} fusion(bf16[6,6,16,32]{3,2,1,0:T(8,128)(2,1)S(1)} %copy-done.2, f32[16]{0:T(128)S(1)} %copy-done.5, bf16[156,92,1,64]{3,2,1,0:T(2,128)(2,1)} %copy.23, bf16[6,6,1,16]{3,1,2,0:T(8,128)(2,1)S(1)} %copy-done.4), kind=kOutput, calls=%fused_computation.10 | convolution fusion | flops 1979482112 | bytes 7773376 | tf_op jit(solution)/shard_map/conv_general_dilated | solution.py:32
  278.9 0.0 copy-done
  278.9 0.0 copy-done.6
  278.9 0.0 copy-done.7
  278.9 15.5 %add_convert_fusion = bf16[16,8,64,64]{2,3,1,0:T(8,128)(2,1)S(1)} fusion(f32[64]{0:T(128)S(1)} %copy-done.6, bf16[6,6,32,64]{3,2,1,0:T(8,128)(2,1)S(1)} %copy-done, f32[36,20,32,64]{3,2,1,0:T(8,128)} %fusion.8, f32[32]{0:T(128)S(1)} %copy-done.7), kind=kOutput, calls=%fused_computation.21 | convolution fusion | flops 1223753728 | bytes 7094656 | tf_op jit(solution)/shard_map/conv_general_dilated | solution.py:32
  294.4 0.0 copy-start.1
  294.4 1.3 copy-done.1
  295.8 0.0 copy-start.3
  295.8 1.7 fusion.47
  297.5 13.6 %pmax.7 = f32[8,64]{1,0:T(8,128)S(1)} all-reduce(f32[8,64]{1,0:T(8,128)S(1)} %get-tuple-element.9), channel_id=1, replica_groups=mesh['src'=64,'tile'=8] {'tile'}, use_global_device_ids=true, to_apply=%region_1.2 | all-reduce | flops 512 | bytes 4096 | tf_op jit(solution)/shard_map/pmax | solution.py:77
  311.1 0.1 fusion.45
  311.2 1.9 copy.36
  313.1 4.9 %fusion.22 = f32[64,64,8,1]{1,2,3,0:T(8,128)S(1)} fusion(f32[8,16,8,64]{1,0,2,3:T(8,128)S(1)} %copy.36, bf16[16,8,64,64]{2,3,1,0:T(8,128)(2,1)} %copy-done.1), kind=kOutput, calls=%fused_computation.24 | convolution fusion | flops 50331648 | bytes 1441792 | tf_op jit(solution)/shard_map/lhws,hwcs->lcs/dot_general | solution.py:80
  318.0 0.8 copy.44
  318.7 0.0 all-reduce.3.cloned.1.call-update
  318.8 13.7 %psum.15 = f32[8,64]{1,0:T(8,128)S(1)} all-reduce(f32[8,64]{1,0:T(8,128)S(1)} %get-tuple-element.5), channel_id=1, replica_groups=mesh['src'=64,'tile'=8] {'tile'}, use_global_device_ids=true, to_apply=%region_4.5 | all-reduce | flops 512 | bytes 4096 | tf_op jit(solution)/shard_map/psum | solution.py:83
  332.5 60.7 %all-reduce.3.cloned.1.call-done = f32[8,64,64]{1,2,0:T(8,128)} async-done(((f32[8,64,64]{1,2,0:T(8,128)}), f32[8,64,64]{1,2,0:T(8,128)}) %all-reduce.3.cloned.1.call-update) | async-done | bytes 131088 | tf_op jit(solution)/shard_map/psum | solution.py:83
  393.2 0.0 copy-done.3
  393.2 1.4 convolution_bitcast_fusion
  394.6 0.9 copy.28
Async XLA Ops:
  6.5 272.4 %copy-start = (bf16[6,6,32,64]{3,2,1,0:T(8,128)(2,1)S(1)}, bf16[6,6,32,64]{3,2,1,0:T(8,128)(2,1)}, u32[]{:S(2)}) copy-start(bf16[6,6,32,64]{3,2,1,0:T(8,128)(2,1)} %param.18) | copy-start | bytes 442372
  6.5 180.9 %all-gather.2.cloned.1.call-start = ((), (), s32[]{:S(2)}) async-start(), calls=%async_computation | async-start | bytes 6389760 | tf_op jit(solution)/shard_map/all_gather | solution.py:59
  7.3 10.1 %collective-permute-start = (bf16[2,14,256]{2,1,0:T(8,128)(2,1)S(1)}, bf16[2,14,256]{2,1,0:T(8,128)(2,1)S(1)}, u32[]{:S(2)}, u32[]{:S(2)}) collective-permute-start(bf16[2,14,256]{2,1,0:T(8,128)(2,1)S(1)} %get-tuple-element.7), channel_id=1, source_target_pairs={{0,1},{1,2},{2,3},{3,4},{4,5},{5,6},{6,7},{8,9},{9,10},{10,11},{11... | collective-permute-start | bytes 43016 | tf_op jit(solution)/shard_map/ppermute | solution.py:19
  12.3 6.0 %collective-permute-start.1 = (bf16[2,14,256]{2,1,0:T(8,128)(2,1)S(1)}, bf16[2,14,256]{2,1,0:T(8,128)(2,1)S(1)}, u32[]{:S(2)}, u32[]{:S(2)}) collective-permute-start(bf16[2,14,256]{2,1,0:T(8,128)(2,1)S(1)} %get-tuple-element.8), channel_id=1, source_target_pairs={{1,0},{2,1},{3,2},{4,3},{5,4},{6,5},{7,6},{9,8},{10,9},{11,10},{12... | collective-permute-start | bytes 43016 | tf_op jit(solution)/shard_map/ppermute | solution.py:20
  19.8 373.4 %all-reduce.3.cloned.1.call-start = ((), (), s32[]{:S(2)}) async-start(), calls=%async_computation.1 | async-start | bytes 524288 | tf_op jit(solution)/shard_map/psum | solution.py:83
  199.0 13.6 %copy-start.2 = (bf16[6,6,16,32]{3,2,1,0:T(8,128)(2,1)S(1)}, bf16[6,6,16,32]{3,2,1,0:T(8,128)(2,1)}, u32[]{:S(2)}) copy-start(bf16[6,6,16,32]{3,2,1,0:T(8,128)(2,1)} %param.16) | copy-start | bytes 110596
  199.0 13.6 %copy-start.4 = (bf16[6,6,1,16]{3,1,2,0:T(8,128)(2,1)S(1)}, bf16[6,6,1,16]{3,1,2,0:T(8,128)(2,1)}, u32[]{:S(2)}) copy-start(bf16[6,6,1,16]{3,1,2,0:T(8,128)(2,1)} %param.14) | copy-start | bytes 3460
  199.0 13.6 %copy-start.5 = (f32[16]{0:T(128)S(1)}, f32[16]{0:T(128)}, u32[]{:S(2)}) copy-start(f32[16]{0:T(128)} %param.15) | copy-start | bytes 196
  212.6 66.3 %copy-start.6 = (f32[64]{0:T(128)S(1)}, f32[64]{0:T(128)}, u32[]{:S(2)}) copy-start(f32[64]{0:T(128)} %param.19) | copy-start | bytes 772
  212.6 66.3 %copy-start.7 = (f32[32]{0:T(128)S(1)}, f32[32]{0:T(128)}, u32[]{:S(2)}) copy-start(f32[32]{0:T(128)} %param.17) | copy-start | bytes 388
  294.4 1.3 copy-start.1
  295.8 97.4 %copy-start.3 = (f32[64,128]{1,0:T(8,128)S(1)}, f32[64,128]{1,0:T(8,128)}, u32[]{:S(2)}) copy-start(f32[64,128]{1,0:T(8,128)} %param.23) | copy-start | bytes 98308
Sparse Core Ops, SparseCore 0:
  19.9 167.5 all-gather.1
  318.9 74.2 all-reduce.2
where the time goes:
time: 408 us; the launch traced here: 403 us
  waiting for transfers between devices  227 us (56%)
  matrix products  98.9 us (24%)
  blocking collectives  27.3 us (7%)
  local copies, waits for them, and re-layouts  23.1 us (6%)
  between operations  13.8 us (3%)
  starting transfers between devices  10.1 us (2%)
    all_gather x1, waiting for transfers between devices, on_device(): lax.all_gather(padded, 'src', axis=0, tiled=True)  166 us
    conv_general_dilated x2, matrix products, convolve(): lax.conv_general_dilated(in_field, kernel_weights, (2, 2), 'VALID', dimen...  81.8 us
    psum x1, waiting for transfers between devices, on_device(): totals, weighted = lax.psum((local_totals, local_weighted), 'tile')  60.7 us
    psum x1, blocking collectives, on_device(): totals, weighted = lax.psum((local_totals, local_weighted), 'tile')  13.7 us
    pmax x1, blocking collectives, on_device(): peak_value = lax.pmax(local_peak, 'tile')  13.6 us
    broadcast_in_dim x2, local copies, waits for them, and re-layouts, on_device(): cost_map[:, :, None, :]  13.6 us
  transfers between devices with their start and end apart: 4, of which 3 were waited for; matrix products, arithmetic and copies ran while one was open for 0% of the time, Pallas kernels for 0%

commit v1 on v0

v1 whole, which is shorter than its diff:
```python
import functools
import math

import jax
import jax.numpy as jnp
from jax import lax
from jax.experimental import pallas as pl
from jax.experimental.pallas import tpu as pltpu
from jax.sharding import Mesh, PartitionSpec as P

exact = lax.Precision.HIGHEST
f32 = jnp.float32
bf16 = jnp.bfloat16

GROUP = 16
HALO = 16
WIDE = 96
PAIRS = 64
EDGE = 7
VMEM = 56 * 1024 * 1024


def params():
    return pltpu.CompilerParams(vmem_limit_bytes=VMEM)


def gelu(x):
    inner = x * (math.sqrt(2.0 / math.pi) + (math.sqrt(2.0 / math.pi) * 0.044715) * (x * x))
    half = 0.5 * x
    return half + half * jnp.tanh(inner)


def nt_dot(a, b):
    return lax.dot_general(a, b, (((1,), (1,)), ((), ())), preferred_element_type=f32)


def mm(a, b):
    return jnp.dot(a, b, preferred_element_type=f32)


def cost_body(rows_ref, left_ref, right_ref, sources_ref, out_ref):
    parts = []
    for z in range(rows_ref.shape[0]):
        for r in range(2):
            parts += [left_ref[z, r], rows_ref[z, r], right_ref[z, r]]
    window = jnp.concatenate(parts, axis=0)
    scale = 1.0 / math.sqrt(sources_ref.shape[-1])

    def one(i, _):
        out_ref[i] = (nt_dot(sources_ref[i], window) * scale).astype(bf16)
        return 0

    lax.fori_loop(0, sources_ref.shape[0], one, 0, unroll=4)


def cost_maps(rows, left, right, sources):
    groups, count, _ = sources.shape
    return pl.pallas_call(
        cost_body,
        out_shape=jax.ShapeDtypeStruct((groups, count, 2 * WIDE * rows.shape[0]), bf16),
        compiler_params=params(),
        name="cost_maps",
    )(rows, left, right, sources)


def band(kernel_ref, out_ref, step, block):
    _, depth, lanes = kernel_ref.shape
    rows = out_ref.shape[0] // 6
    for t in range(lanes // 128):
        lane = lax.broadcasted_iota(jnp.int32, (depth, 128), 1) // block
        for kh in range(6):
            tile = kernel_ref[kh, :, 128 * t : 128 * (t + 1)].astype(f32)
            total = jnp.zeros((rows, 128), f32)
            for b in range(128 // block):
                top = step * (b + t * (128 // block))
                piece = [jnp.where(lane == b, tile, 0.0)]
                if top:
                    piece = [jnp.zeros((top, 128), f32)] + piece
                if rows - top - depth:
                    piece = piece + [jnp.zeros((rows - top - depth, 128), f32)]
                total = total + jnp.concatenate(piece, axis=0)
            out_ref[kh * rows : (kh + 1) * rows, 128 * t : 128 * (t + 1)] = total.astype(bf16)


def band_body(one_ref, two_ref, three_ref, out_one, out_two, out_three):
    lanes = one_ref.shape[-1]
    row = lax.broadcasted_iota(jnp.int32, (WIDE, lanes), 0)
    tap = row - 2 - 2 * (lax.broadcasted_iota(jnp.int32, (WIDE, lanes), 1) // 16)
    for j in range(3):
        for q in range(2):
            total = jnp.zeros((WIDE, lanes), f32)
            for kw in range(6):
                line = one_ref[2 * j + q, kw : kw + 1, :].astype(f32)
                total = jnp.where(tap == kw, line, total)
            out_one[256 * j + WIDE * q : 256 * j + WIDE * (q + 1), :] = total.astype(bf16)
        out_one[256 * j + 2 * WIDE : 256 * (j + 1), :] = jnp.zeros((256 - 2 * WIDE, lanes), bf16)
    band(two_ref, out_two, 32, 32)
    band(three_ref, out_three, 64, 64)


def bands(kernel_one, kernel_two, kernel_three):
    one = jnp.tile(kernel_one.reshape(6, 6, 16), (1, 1, 48))
    two = jnp.tile(kernel_two.reshape(6, 96, 32), (1, 1, 8))
    three = jnp.tile(kernel_three.reshape(6, 192, 64), (1, 1, 4))
    return pl.pallas_call(
        band_body,
        out_shape=(
            jax.ShapeDtypeStruct((768, 768), bf16),
            jax.ShapeDtypeStruct((2304, 256), bf16),
            jax.ShapeDtypeStruct((2304, 256), bf16),
        ),
        compiler_params=params(),
        name="bands",
    )(one, two, three)


def encode_body(
    cost_ref,
    one_ref,
    two_ref,
    three_ref,
    bias_one,
    bias_two,
    bias_three,
    query_ref,
    pos_ref,
    spread_ref,
    out_ref,
    pairs,
    hidden_one,
    hidden_two,
    features,
    score_ref,
):
    count = cost_ref.shape[1]
    blank = jnp.zeros((EDGE, count, 256), bf16)
    pairs[0:EDGE] = blank
    pairs[EDGE + PAIRS :] = blank

    def place(i, _):
        for z in range(4):
            start = 384 * (z // 2) + 128 * (z % 2)
            value = cost_ref[i, :, start : start + 256]
            if z % 2:
                value = jnp.concatenate([value[:, 64:], value[:, :64]], axis=1)
            pairs[EDGE + z * GROUP + i] = value
        return 0

    lax.fori_loop(0, GROUP, place, 0, unroll=2)

    step = 4
    flat = step * count

    def first(i, _):
        h = i * step
        left = jnp.concatenate(
            [pairs[pl.ds(h + j, step)].reshape(flat, 256) for j in range(3)], axis=1
        )
        for n in range(3):
            lanes = slice(256 * n, 256 * (n + 1))
            value = gelu(mm(left, one_ref[:, lanes]) + bias_one[:, lanes])
            hidden_one[pl.ds(i * (step // 2), step // 2), :, :, lanes] = value.astype(bf16).reshape(
                step // 2, 2, count, 256
            )
        return 0

    lax.fori_loop(0, 76 // step, first, 0)

    def second(i, _):
        h = i * step

        def left(lanes):
            return jnp.concatenate(
                [
                    hidden_one[pl.ds(h + k // 2, step), k % 2, :, lanes].reshape(flat, -1)
                    for k in range(6)
                ],
                axis=1,
            )

        def save(value, lanes):
            hidden_two[pl.ds(i * (step // 2), step // 2), :, :, lanes] = value.astype(bf16).reshape(
                step // 2, 2, count, -1
            )

        for n in range(2):
            value = mm(left(slice(256 * n, 256 * n + 384)), two_ref[...])
            save(gelu(value + bias_two[...]), slice(256 * n, 256 * (n + 1)))
        short = jnp.concatenate([two_ref[384 * k : 384 * k + 256, :128] for k in range(6)], axis=0)
        value = mm(left(slice(512, 768)), short)
        save(gelu(value + bias_two[:, :128]), slice(512, 640))
        return 0

    lax.fori_loop(0, 36 // step, second, 0)

    def third(i, _):
        h = i * step
        for n in range(2):
            left = jnp.concatenate(
                [
                    hidden_two[
                        pl.ds(h + k // 2, step), k % 2, :, 256 * n : 256 * n + 384
                    ].reshape(flat, 384)
                    for k in range(6)
                ],
                axis=1,
            )
            value = mm(left, three_ref[...]) + bias_three[...]
            features[pl.ds(h, step), :, 256 * n : 256 * (n + 1)] = value.astype(bf16).reshape(
                step, count, 256
            )
        return 0

    lax.fori_loop(0, 16 // step, third, 0)

    scale = 1.0 / math.sqrt(128)

    def score(h, peak):
        value = (mm(features[h], query_ref[...]) + pos_ref[pl.ds(h, 1), :]) * scale
        score_ref[h] = value
        return jnp.maximum(peak, value)

    peak = lax.fori_loop(0, 16, score, jnp.full((count, 128), -jnp.inf, f32), unroll=2)
    for k in (8, 16, 32):
        peak = jnp.maximum(peak, pltpu.roll(peak, k, 1))
    low = lax.broadcasted_iota(jnp.int32, (count, 128), 1) < 64

    def weigh(h, total):
        value = jnp.exp(score_ref[h] - peak)
        head = value.astype(bf16).astype(f32)
        score_ref[h] = jnp.where(low, head, value - head)
        return total + value

    total = lax.fori_loop(0, 16, weigh, jnp.zeros((count, 128), f32), unroll=2)
    for k in (8, 16, 32):
        total = total + pltpu.roll(total, k, 1)

    def gather(latent):
        spread = spread_ref[:, 512 * latent : 512 * (latent + 1)]

        def one(h, acc):
            value = mm(score_ref[h].astype(bf16), spread)
            return acc + value * features[h].astype(f32)

        acc = lax.fori_loop(0, 16, one, jnp.zeros((count, 512), f32), unroll=2)
        acc = (acc[:, :128] + acc[:, 128:256]) + (acc[:, 256:384] + acc[:, 384:])
        return acc + pltpu.roll(acc, 64, 1)

    for k in range(4):
        out_ref[:, 128 * k : 128 * (k + 1)] = jnp.where(low, gather(2 * k), gather(2 * k + 1))
    out_ref[:, 512:] = jnp.where(low, peak, total)


def encode(cost, banded, biases, query, pos, spread):
    count = cost.shape[1]
    return pl.pallas_call(
        encode_body,
        out_shape=jax.ShapeDtypeStruct((count, 640), f32),
        scratch_shapes=[
            pltpu.VMEM((PAIRS + 2 * EDGE, count, 256), bf16),
            pltpu.VMEM((38, 2, count, 768), bf16),
            pltpu.VMEM((18, 2, count, 640), bf16),
            pltpu.VMEM((16, count, 512), bf16),
            pltpu.VMEM((16, count, 128), f32),
        ],
        compiler_params=params(),
        name="encode",
    )(cost, *banded, *biases, query, pos, spread)


def combine_body(parts_ref, value_ref, spread_ref, out_ref):
    tiles, count, _ = parts_ref.shape
    low = lax.broadcasted_iota(jnp.int32, (count, 128), 1) < 64
    stats = [parts_ref[t, :, 512:] for t in range(tiles)]
    peak = functools.reduce(jnp.maximum, stats)
    total = jnp.zeros((count, 128), f32)
    weighted = jnp.zeros((count, 512), f32)
    for t in range(tiles):
        factor = jnp.where(low, jnp.exp(stats[t] - peak), 0.0)
        total = total + factor * pltpu.roll(stats[t], 64, 1)
        wide = jnp.dot(factor, spread_ref[...], precision=exact, preferred_element_type=f32)
        weighted = weighted + wide * parts_ref[t, :, :512]
    total = jnp.where(low, total, 1.0)
    share = jnp.where(low, 1.0 / total, 0.0)
    attended = weighted * jnp.dot(share, spread_ref[...], precision=exact, preferred_element_type=f32)
    for latent in range(8):
        part = attended[:, 128 * (latent // 2) : 128 * (latent // 2 + 1)]
        part = jnp.where(low == (latent % 2 == 0), part, 0.0)
        out_ref[:, latent, :] = jnp.dot(
            part, value_ref[...], precision=exact, preferred_element_type=f32
        )


def combine(parts, value_weight):
    lane = jnp.arange(128)[:, None]
    spread = (lane == jnp.arange(512)[None, :] // 64).astype(f32)
    return pl.pallas_call(
        combine_body,
        out_shape=jax.ShapeDtypeStruct((parts.shape[1], 8, 128), f32),
        compiler_params=params(),
        name="combine",
    )(parts, jnp.concatenate([value_weight, value_weight], axis=0), spread)


def spread_to(array, axis):
    peers = lax.axis_size(axis)
    return lax.all_to_all(jnp.broadcast_to(array[None], (peers,) + array.shape), axis, 0, 0)


def on_device(
    target,
    sources,
    kernel_one,
    first_conv_bias,
    kernel_two,
    shift_two,
    kernel_three,
    shift_three,
    latents,
    pos_key,
    w_key,
    value_weight,
):
    tiles = lax.axis_size("tile")
    every = spread_to(sources, "xy")
    rows = lax.all_gather(target, "zh", axis=0)
    width = rows.shape[2]
    up = [(i, i + 1) for i in range(tiles - 1)]
    down = [(j, i) for i, j in up]
    left = lax.ppermute(rows[:, :, width - HALO :], "tile", up)
    right = lax.ppermute(rows[:, :, :HALO], "tile", down)
    cost = cost_maps(rows, left, right, every)
    cost, kernel_one, kernel_two, kernel_three, latents, pos_key = lax.optimization_barrier(
        (cost, kernel_one, kernel_two, kernel_three, latents, pos_key)
    )
    cost = lax.all_to_all(cost, "xy", 0, 0)

    banded = bands(kernel_one, kernel_two, kernel_three)
    query = jnp.dot(latents, w_key.T, precision=exact, preferred_element_type=f32).astype(bf16)
    own = jnp.arange(8)[:, None] == jnp.arange(16)[None, :] % 8
    query = jnp.where(own[:, None, :, None], query.T[None, :, None, :], 0).reshape(512, 128)
    pos = jnp.einsum("ld,hwd->hwl", latents, pos_key, precision=exact).reshape(16, 64)
    pos = jnp.concatenate([pos, pos], axis=1)
    lane = jnp.arange(128)[:, None] % 64
    column = jnp.arange(8 * 512)[None, :]
    spread = (lane == (column % 512) // 64 * 8 + column // 512).astype(bf16)
    biases = (
        jnp.tile(first_conv_bias, 48)[None],
        jnp.tile(shift_two, 8)[None],
        jnp.tile(shift_three, 4)[None],
    )
    parts = encode(cost, banded, biases, query, pos, spread)
    parts = lax.all_to_all(parts.reshape(tiles, -1, parts.shape[1]), "tile", 0, 0)
    tokens = spread_to(combine(parts, value_weight), "tile")
    return tokens.reshape((-1,) + tokens.shape[2:])


def solution(mesh):
    src, tile = mesh.devices.shape
    split = Mesh(mesh.devices.reshape(src // GROUP, GROUP, tile), ("zh", "xy", "tile"))
    rows = ("zh", "xy")
    return jax.shard_map(
        on_device,
        mesh=split,
        in_specs=(
            P(rows, "tile", None),
            P(rows, None),
            P(),
            P(),
            P(),
            P(),
            P(),
            P(),
            P(),
            P(None, "tile", None),
            P(),
            P(),
        ),
        out_specs=P(rows, None, None),
        check_vma=False,
    )
```

time: 408 us -> 158 us (0.39); the launches traced: 403 us -> 157 us
  waiting for transfers between devices: 227 us -> 25.9 us
  matrix products: 98.9 us -> 0.71 us
  Pallas kernels: 0 us -> 54.4 us
  between operations: 13.8 us -> 0.2 us
  starting transfers between devices: 10.1 us -> 22 us
  blocking collectives: 27.3 us -> 38.3 us
  local copies, waits for them, and re-layouts: 23.1 us -> 12.3 us
    all_gather x1 -> x0, waiting for transfers between devices: 166 us -> none  [on_device(): lax.all_gather(padded, 'src', axis=0, tiled=True)]
    conv_general_dilated x2 -> x0, matrix products: 81.8 us -> none  [convolve(): lax.conv_general_dilated(in_field, kernel_weights, (2, 2), 'VALID', dimen...]
    psum x1 -> x0, waiting for transfers between devices: 60.7 us -> none  [on_device(): totals, weighted = lax.psum((local_totals, local_weighted), 'tile')]
    pallas_call x0 -> x4, Pallas kernels: none -> 54.4 us  [the longest x1 42.6 us: encode(): pl.pallas_call(encode_body, out_shape=jax.ShapeDtypeStruct((count, 640),...]
    all_to_all x0 -> x3, waiting for transfers between devices: none -> 25.9 us  [the longest x1 12.8 us: on_device(): cost = lax.all_to_all(cost, 'xy', 0, 0)]
    all_gather x0 -> x1, blocking collectives: none -> 25.6 us  [on_device(): rows = lax.all_gather(target, 'zh', axis=0)]
    dot_general x6 -> x2, matrix products: 17.1 us -> 0.71 us  [the longest x1 0.57 us: on_device(): jnp.einsum('ld,hwd->hwl', latents, pos_key, precision=exact).reshape(16, 64)]
    all_to_all x0 -> x3, starting transfers between devices: none -> 14.4 us  [the longest x1 6.75 us: spread_to(): lax.all_to_all(jnp.broadcast_to(array[None], (peers,) + array.shape), axi...]
  transfers between devices with their start and end apart: 4 -> 5, of which waited for: 3 -> 3; matrix products, arithmetic and copies ran while one was open for 0% -> 8% of each run, Pallas kernels for 0% -> 2%
where the time goes in v1:
time: 158 us; the launch traced here: 157 us
  Pallas kernels  54.4 us (34%)
  blocking collectives  38.3 us (24%)
  waiting for transfers between devices  25.9 us (16%)
  starting transfers between devices  22 us (14%)
  local copies, waits for them, and re-layouts  12.3 us (8%)
  other arithmetic  3.52 us (2%)
    pallas_call x1, Pallas kernels, encode(): pl.pallas_call(encode_body, out_shape=jax.ShapeDtypeStruct((count, 640),...  42.6 us
    all_gather x1, blocking collectives, on_device(): rows = lax.all_gather(target, 'zh', axis=0)  25.6 us
    all_to_all x1, waiting for transfers between devices, on_device(): cost = lax.all_to_all(cost, 'xy', 0, 0)  12.8 us
    all_to_all x1, blocking collectives, spread_to(): lax.all_to_all(jnp.broadcast_to(array[None], (peers,) + array.shape), axi...  12.7 us
    all_to_all x1, waiting for transfers between devices, spread_to(): lax.all_to_all(jnp.broadcast_to(array[None], (peers,) + array.shape), axi...  8.47 us
    all_to_all x1, starting transfers between devices, spread_to(): lax.all_to_all(jnp.broadcast_to(array[None], (peers,) + array.shape), axi...  6.75 us
    ppermute x1, starting transfers between devices, on_device(): left = lax.ppermute(rows[:, :, width - HALO:], 'tile', up)  5.66 us
    pallas_call x1, Pallas kernels, cost_maps(): pl.pallas_call(cost_body, out_shape=jax.ShapeDtypeStruct((groups, count,...  4.78 us
  transfers between devices with their start and end apart: 5, of which 3 were waited for; matrix products, arithmetic and copies ran while one was open for 8% of the time, Pallas kernels for 2%

profile of v1, /device:TPU:1, one launch (start us, length us, event | category | flops | bytes accessed | tf_op | source)
XLA Modules:
  0.0 157.3 jit_solution(7399353098799136013)
XLA Ops:
  0.0 25.6 %all-gather = bf16[8,64,256]{2,1,0:T(8,128)(2,1)S(1)} all-gather(bf16[2,64,256]{2,1,0:T(8,128)(2,1)} %param.12), channel_id=2, replica_groups=mesh['zh'=4,'xy'=16,'tile'=8] {'zh'}, dimensions={0}, use_global_device_ids=true | all-gather | bytes 327680 | tf_op jit(solution)/shard_map/all_gather | solution.py:326
  25.6 5.7 %collective-permute-start = (bf16[4,2,16,256]{3,2,1,0:T(8,128)(2,1)S(1)}, bf16[4,2,16,256]{3,2,1,0:T(8,128)(2,1)S(1)}, u32[]{:S(2)}, u32[]{:S(2)}) collective-permute-start(bf16[4,2,16,256]{3,2,1,0:T(8,128)(2,1)S(1)} %get-tuple-element.24), channel_id=1, source_target_pairs={{0,1},{1,2},{2,3},{3,4},{4,5},{5,6},{6,7},{8,9},{9,10},{10,11},{11... | collective-permute-start | bytes 196616 | tf_op jit(solution)/shard_map/ppermute | solution.py:330
  31.3 1.9 %collective-permute-start.1 = (bf16[4,2,16,256]{3,2,1,0:T(8,128)(2,1)S(1)}, bf16[4,2,16,256]{3,2,1,0:T(8,128)(2,1)S(1)}, u32[]{:S(2)}, u32[]{:S(2)}) collective-permute-start(bf16[4,2,16,256]{3,2,1,0:T(8,128)(2,1)S(1)} %get-tuple-element.23), channel_id=1, source_target_pairs={{1,0},{2,1},{3,2},{4,3},{5,4},{6,5},{7,6},{9,8},{10,9},{11,10},{12... | collective-permute-start | bytes 196616 | tf_op jit(solution)/shard_map/ppermute | solution.py:331
  33.2 1.6 %broadcast_in_dim.24 = bf16[16,64,256]{2,1,0:T(8,128)(2,1)} broadcast(bf16[64,256]{1,0:T(8,128)(2,1)} %param.13), dimensions={1,2} | broadcast | bytes 557056 | tf_op jit(solution)/shard_map/broadcast_in_dim | solution.py:307
  34.8 6.8 %all-to-all-start = ((bf16[16,64,256]{2,1,0:T(8,128)(2,1)}), bf16[16,64,256]{2,1,0:T(8,128)(2,1)S(1)}, u32[]{:S(2)}, u32[]{:S(2)}) async-start(bf16[16,64,256]{2,1,0:T(8,128)(2,1)} %broadcast_in_dim.24), calls=%async_computation | async-start | bytes 1048576 | tf_op jit(solution)/shard_map/all_to_all | solution.py:307
  41.6 0.7 broadcast_in_dim_tile.9.bias_one
  42.3 0.7 broadcast_in_dim_tile.10.bias_two
  43.0 0.7 broadcast_in_dim_tile.11.bias_three
  43.7 0.1 iota_compare_fusion.1
  43.8 0.0 collective-permute-done.left_ref
  43.8 0.0 collective-permute-done.1.right_ref
  43.8 0.0 copy-start.8
  43.8 8.5 %all-to-all-done.sources_ref = bf16[16,64,256]{2,1,0:T(8,128)(2,1)S(1)} async-done(((bf16[16,64,256]{2,1,0:T(8,128)(2,1)}), bf16[16,64,256]{2,1,0:T(8,128)(2,1)S(1)}, u32[]{:S(2)}, u32[]{:S(2)}) %all-to-all-start) | async-done | bytes 524320 | tf_op jit(solution)/shard_map/all_to_all | solution.py:307
  52.3 0.8 copy-done.2
  53.1 4.8 %cost_maps.1 = bf16[16,64,768]{2,1,0:T(8,128)(2,1)} custom-call(bf16[4,2,64,256]{3,2,1,0:T(8,128)(2,1)} %bitcast.25, bf16[4,2,16,256]{3,2,1,0:T(8,128)(2,1)} %copy-done.7, bf16[4,2,16,256]{3,2,1,0:T(8,128)(2,1)} %copy-done.8, bf16[16,64,256]{2,1,0:T(8,128)(2,1)} %copy-done.2), custom_call_target="tpu_custom_call" | custom-call | tf_op jit(solution)/shard_map/cost_maps/pallas_call | solution.py:58
  57.9 3.8 %all-to-all-start.1 = ((bf16[16,64,768]{2,1,0:T(8,128)(2,1)}), bf16[16,64,768]{2,1,0:T(8,128)(2,1)S(1)}, u32[]{:S(2)}, u32[]{:S(2)}) async-start(bf16[16,64,768]{2,1,0:T(8,128)(2,1)} %cost_maps.1), calls=%async_computation.1 | async-start | bytes 3145728 | tf_op jit(solution)/shard_map/all_to_all | solution.py:336
  61.7 0.0 copy-start.6
  61.7 0.0 copy-start.5
  61.7 1.3 compare_convert_fusion.spread_ref
  63.0 0.1 tile.49
  63.1 1.0 tile.50.one_ref
  64.1 0.1 copy.22
  64.2 0.1 tile.52
  64.3 0.9 copy.24.two_ref
  65.2 0.2 copy.23
  65.4 0.0 copy-start.9
  65.4 0.1 tile.55
  65.5 1.1 copy.25.three_ref
  66.6 0.1 fusion
  66.7 0.1 broadcast_select_fusion
  66.8 0.2 select_n.72
  67.0 0.8 copy.29.query_ref
  67.8 0.6 convolution_bitcast_fusion
  68.4 0.1 copy.27
  68.4 3.7 %bands.1 = (bf16[768,768]{1,0:T(8,128)(2,1)}, bf16[2304,256]{1,0:T(8,128)(2,1)}, bf16[2304,256]{1,0:T(8,128)(2,1)}) custom-call(bf16[6,6,768]{2,1,0:T(8,128)(2,1)} %tile.50.one_ref, bf16[6,96,256]{2,1,0:T(8,128)(2,1)} %copy.24.two_ref, bf16[6,192,256]{2,1,0:T(8,128)(2,1)} %copy.25.three_ref), custom_call_target="tpu_custom_call" | custom-call | tf_op jit(solution)/shard_map/bands/pallas_call | solution.py:105
  72.2 0.7 pad_maximum_fusion.1.pos_ref
  72.8 12.8 %all-to-all-done.1.cost_ref = bf16[16,64,768]{2,1,0:T(8,128)(2,1)S(1)} async-done(((bf16[16,64,768]{2,1,0:T(8,128)(2,1)}), bf16[16,64,768]{2,1,0:T(8,128)(2,1)S(1)}, u32[]{:S(2)}, u32[]{:S(2)}) %all-to-all-start.1) | async-done | bytes 1572896 | tf_op jit(solution)/shard_map/all_to_all | solution.py:336
  85.6 1.2 copy-done.1
  86.8 42.6 %encode.1 = f32[64,640]{1,0:T(8,128)} custom-call(bf16[16,64,768]{2,1,0:T(8,128)(2,1)} %copy-done.1, bf16[768,768]{1,0:T(8,128)(2,1)} %get-tuple-element.18.one_ref, bf16[2304,256]{1,0:T(8,128)(2,1)} %get-tuple-element.19.two_ref, bf16[2304,256]{1,0:T(8,128)(2,1)} %get-tuple-element.20.three_ref, f32[1,768]{1,0:T(1,128)} %broadcast_in_dim_tile.9.bias_one, ...), custom_call_target="tpu_custom_call" | custom-call | tf_op jit(solution)/shard_map/encode/pallas_call | solution.py:256
  129.4 3.8 %all-to-all-start.2 = ((f32[8,8,640]{2,1,0:T(8,128)}), f32[8,8,640]{2,1,0:T(8,128)S(1)}, u32[]{:S(2)}, u32[]{:S(2)}) async-start(f32[8,8,640]{2,1,0:T(8,128)} %bitcast.28), calls=%async_computation.2 | async-start | bytes 327680 | tf_op jit(solution)/shard_map/all_to_all | solution.py:353
  133.3 0.6 pad_maximum_fusion.value_ref
  133.9 0.7 fusion.1.spread_ref
  134.6 4.7 %all-to-all-done.2.parts_ref = f32[8,8,640]{2,1,0:T(8,128)S(1)} async-done(((f32[8,8,640]{2,1,0:T(8,128)}), f32[8,8,640]{2,1,0:T(8,128)S(1)}, u32[]{:S(2)}, u32[]{:S(2)}) %all-to-all-start.2) | async-done | bytes 163872 | tf_op jit(solution)/shard_map/all_to_all | solution.py:353
  139.3 0.7 copy-done.4
  139.9 3.2 %combine.1 = f32[8,8,128]{2,1,0:T(8,128)} custom-call(f32[8,8,640]{2,1,0:T(8,128)} %copy-done.4, f32[128,128]{1,0:T(8,128)} %pad_maximum_fusion.value_ref, f32[128,512]{1,0:T(8,128)} %fusion.1.spread_ref), custom_call_target="tpu_custom_call" | custom-call | tf_op jit(solution)/shard_map/combine/pallas_call | solution.py:297
  143.2 0.8 broadcast_in_dim.28
  143.9 12.7 %all_to_all.20 = f32[8,8,8,128]{3,2,1,0:T(8,128)S(1)} all-to-all(f32[8,8,8,128]{3,2,1,0:T(8,128)S(1)} %broadcast_in_dim.28), channel_id=1, replica_groups=mesh['zh'=4,'xy'=16,'tile'=8] {'tile'}, dimensions={0} | all-to-all | bytes 524288 | tf_op jit(solution)/shard_map/all_to_all | solution.py:307
  156.6 0.7 copy.35
  (33 shorter events, 0.1 us)
Async XLA Ops:
  0.0 66.6 %copy-start = (f32[64,128]{1,0:T(8,128)S(1)}, f32[64,128]{1,0:T(8,128)}, u32[]{:S(2)}) copy-start(f32[64,128]{1,0:T(8,128)} %param.22) | copy-start | bytes 98308
  0.0 41.6 %copy-start.13 = (f32[16]{0:T(128)S(1)}, f32[16]{0:T(128)}, u32[]{:S(2)}) copy-start(f32[16]{0:T(128)} %param.15) | copy-start | bytes 196
  0.0 42.3 %copy-start.14 = (f32[32]{0:T(128)S(1)}, f32[32]{0:T(128)}, u32[]{:S(2)}) copy-start(f32[32]{0:T(128)} %param.17) | copy-start | bytes 388
  0.0 43.0 %copy-start.15 = (f32[64]{0:T(128)S(1)}, f32[64]{0:T(128)}, u32[]{:S(2)}) copy-start(f32[64]{0:T(128)} %param.19) | copy-start | bytes 772
  25.6 26.6 %copy-start.3 = (bf16[8,64,256]{2,1,0:T(8,128)(2,1)}, bf16[8,64,256]{2,1,0:T(8,128)(2,1)S(1)}, u32[]{:S(2)}) copy-start(bf16[8,64,256]{2,1,0:T(8,128)(2,1)S(1)} %all-gather) | copy-start | bytes 786436
  25.6 18.1 %collective-permute-start = (bf16[4,2,16,256]{3,2,1,0:T(8,128)(2,1)S(1)}, bf16[4,2,16,256]{3,2,1,0:T(8,128)(2,1)S(1)}, u32[]{:S(2)}, u32[]{:S(2)}) collective-permute-start(bf16[4,2,16,256]{3,2,1,0:T(8,128)(2,1)S(1)} %get-tuple-element.24), channel_id=1, source_target_pairs={{0,1},{1,2},{2,3},{3,4},{4,5},{5,6},{6,7},{8,9},{9,10},{10,11},{11... | collective-permute-start | bytes 196616 | tf_op jit(solution)/shard_map/ppermute | solution.py:330
  31.3 12.5 %collective-permute-start.1 = (bf16[4,2,16,256]{3,2,1,0:T(8,128)(2,1)S(1)}, bf16[4,2,16,256]{3,2,1,0:T(8,128)(2,1)S(1)}, u32[]{:S(2)}, u32[]{:S(2)}) collective-permute-start(bf16[4,2,16,256]{3,2,1,0:T(8,128)(2,1)S(1)} %get-tuple-element.23), channel_id=1, source_target_pairs={{1,0},{2,1},{3,2},{4,3},{5,4},{6,5},{7,6},{9,8},{10,9},{11,10},{12... | collective-permute-start | bytes 196616 | tf_op jit(solution)/shard_map/ppermute | solution.py:331
  34.8 17.4 %all-to-all-start = ((bf16[16,64,256]{2,1,0:T(8,128)(2,1)}), bf16[16,64,256]{2,1,0:T(8,128)(2,1)S(1)}, u32[]{:S(2)}, u32[]{:S(2)}) async-start(bf16[16,64,256]{2,1,0:T(8,128)(2,1)} %broadcast_in_dim.24), calls=%async_computation | async-start | bytes 1048576 | tf_op jit(solution)/shard_map/all_to_all | solution.py:307
  43.8 8.5 %copy-start.7 = (bf16[4,2,16,256]{3,2,1,0:T(8,128)(2,1)}, bf16[4,2,16,256]{3,2,1,0:T(8,128)(2,1)S(1)}, u32[]{:S(2)}) copy-start(bf16[4,2,16,256]{3,2,1,0:T(8,128)(2,1)S(1)} %collective-permute-done.left_ref) | copy-start | bytes 196612
  43.8 8.5 %copy-start.8 = (bf16[4,2,16,256]{3,2,1,0:T(8,128)(2,1)}, bf16[4,2,16,256]{3,2,1,0:T(8,128)(2,1)S(1)}, u32[]{:S(2)}) copy-start(bf16[4,2,16,256]{3,2,1,0:T(8,128)(2,1)S(1)} %collective-permute-done.1.right_ref) | copy-start | bytes 196612
  52.3 0.8 copy-start.2
  57.9 5.2 %copy-start.12 = (bf16[6,6,1,16]{3,1,2,0:T(8,128)(2,1)S(1)}, bf16[6,6,1,16]{3,1,2,0:T(8,128)(2,1)}, u32[]{:S(2)}) copy-start(bf16[6,6,1,16]{3,1,2,0:T(8,128)(2,1)} %param.14) | copy-start | bytes 3460
  57.9 27.7 %all-to-all-start.1 = ((bf16[16,64,768]{2,1,0:T(8,128)(2,1)}), bf16[16,64,768]{2,1,0:T(8,128)(2,1)S(1)}, u32[]{:S(2)}, u32[]{:S(2)}) async-start(bf16[16,64,768]{2,1,0:T(8,128)(2,1)} %cost_maps.1), calls=%async_computation.1 | async-start | bytes 3145728 | tf_op jit(solution)/shard_map/all_to_all | solution.py:336
  61.7 2.4 %copy-start.6 = (bf16[6,6,16,32]{3,2,1,0:T(8,128)(2,1)S(1)}, bf16[6,6,16,32]{3,2,1,0:T(8,128)(2,1)}, u32[]{:S(2)}) copy-start(bf16[6,6,16,32]{3,2,1,0:T(8,128)(2,1)} %param.16) | copy-start | bytes 110596
  61.7 3.5 %copy-start.5 = (bf16[6,6,32,64]{3,2,1,0:T(8,128)(2,1)S(1)}, bf16[6,6,32,64]{3,2,1,0:T(8,128)(2,1)}, u32[]{:S(2)}) copy-start(bf16[6,6,32,64]{3,2,1,0:T(8,128)(2,1)} %param.18) | copy-start | bytes 442372
  65.2 1.4 copy-start.11
  65.4 2.4 %copy-start.9 = (f32[16,8,128]{2,1,0:T(8,128)S(1)}, f32[16,8,128]{2,1,0:T(8,128)}, u32[]{:S(2)}) copy-start(f32[16,8,128]{2,1,0:T(8,128)} %param.21) | copy-start | bytes 196612
  85.6 1.2 copy-start.1
  86.8 46.5 %copy-start.10 = (f32[64,128]{1,0:T(8,128)S(1)}, f32[64,128]{1,0:T(8,128)}, u32[]{:S(2)}) copy-start(f32[64,128]{1,0:T(8,128)} %param.23) | copy-start | bytes 98308
  129.4 9.9 %all-to-all-start.2 = ((f32[8,8,640]{2,1,0:T(8,128)}), f32[8,8,640]{2,1,0:T(8,128)S(1)}, u32[]{:S(2)}, u32[]{:S(2)}) async-start(f32[8,8,640]{2,1,0:T(8,128)} %bitcast.28), calls=%async_computation.2 | async-start | bytes 327680 | tf_op jit(solution)/shard_map/all_to_all | solution.py:353
  139.3 0.7 copy-start.4

commit v2 on v1

--- a/solution.py
+++ b/solution.py
@@ -3,6 +3,7 @@
 
 import jax
 import jax.numpy as jnp
+import numpy as np
 from jax import lax
 from jax.experimental import pallas as pl
 from jax.experimental.pallas import tpu as pltpu
@@ -38,26 +39,24 @@
     return jnp.dot(a, b, preferred_element_type=f32)
 
 
-def cost_body(rows_ref, left_ref, right_ref, sources_ref, out_ref):
+def cost_body(rows_ref, left_ref, right_ref, sources_ref, out_ref, *, first):
     parts = []
     for z in range(rows_ref.shape[0]):
         for r in range(2):
             parts += [left_ref[z, r], rows_ref[z, r], right_ref[z, r]]
     window = jnp.concatenate(parts, axis=0)
-    scale = 1.0 / math.sqrt(sources_ref.shape[-1])
-
-    def one(i, _):
-        out_ref[i] = (nt_dot(sources_ref[i], window) * scale).astype(bf16)
-        return 0
-
-    lax.fori_loop(0, sources_ref.shape[0], one, 0, unroll=4)
-
-
-def cost_maps(rows, left, right, sources):
-    groups, count, _ = sources.shape
+    groups, count, width = out_ref.shape
+    depth = sources_ref.shape[-1]
+    mine = sources_ref[:, first : first + count].reshape(groups * count, depth)
+    for n in range(0, width, 256):
+        value = nt_dot(mine, window[n : n + 256]) * (1.0 / math.sqrt(depth))
+        out_ref[:, :, n : n + 256] = value.astype(bf16).reshape(groups, count, 256)
+
+
+def cost_maps(rows, left, right, sources, first, count):
     return pl.pallas_call(
-        cost_body,
-        out_shape=jax.ShapeDtypeStruct((groups, count, 2 * WIDE * rows.shape[0]), bf16),
+        functools.partial(cost_body, first=first),
+        out_shape=jax.ShapeDtypeStruct((sources.shape[0], count, 2 * WIDE * rows.shape[0]), bf16),
         compiler_params=params(),
         name="cost_maps",
     )(rows, left, right, sources)
@@ -125,6 +124,7 @@
     query_ref,
     pos_ref,
     spread_ref,
+    before_ref,
     out_ref,
     pairs,
     hidden_one,
@@ -133,6 +133,7 @@
     score_ref,
 ):
     count = cost_ref.shape[1]
+    done = before_ref.shape[0] if before_ref is not None else 0
     blank = jnp.zeros((EDGE, count, 256), bf16)
     pairs[0:EDGE] = blank
     pairs[EDGE + PAIRS :] = blank
@@ -247,15 +248,25 @@
         return acc + pltpu.roll(acc, 64, 1)
 
     for k in range(4):
-        out_ref[:, 128 * k : 128 * (k + 1)] = jnp.where(low, gather(2 * k), gather(2 * k + 1))
-    out_ref[:, 512:] = jnp.where(low, peak, total)
-
-
-def encode(cost, banded, biases, query, pos, spread):
+        out_ref[done:, 128 * k : 128 * (k + 1)] = jnp.where(low, gather(2 * k), gather(2 * k + 1))
+    out_ref[done:, 512:] = jnp.where(low, peak, total)
+    if done:
+        out_ref[:done] = before_ref[...]
+
+
+def encode(cost, banded, biases, query, pos, spread, before=None):
     count = cost.shape[1]
+    whole = count + (0 if before is None else before.shape[0])
+    operands = (cost, *banded, *biases, query, pos, spread)
+
+    def body(*refs):
+        encode_body(*refs[:10], None, *refs[10:])
+
+    if before is not None:
+        body, operands = (encode_body, operands + (before,))
     return pl.pallas_call(
-        encode_body,
-        out_shape=jax.ShapeDtypeStruct((count, 640), f32),
+        body,
+        out_shape=jax.ShapeDtypeStruct((whole, 640), f32),
         scratch_shapes=[
             pltpu.VMEM((PAIRS + 2 * EDGE, count, 256), bf16),
             pltpu.VMEM((38, 2, count, 768), bf16),
@@ -265,46 +276,73 @@
         ],
         compiler_params=params(),
         name="encode",
-    )(cost, *banded, *biases, query, pos, spread)
-
-
-def combine_body(parts_ref, value_ref, spread_ref, out_ref):
+    )(*operands)
+
+
+def combine_body(parts_ref, spread_ref, out_ref):
     tiles, count, _ = parts_ref.shape
     low = lax.broadcasted_iota(jnp.int32, (count, 128), 1) < 64
     stats = [parts_ref[t, :, 512:] for t in range(tiles)]
     peak = functools.reduce(jnp.maximum, stats)
-    total = jnp.zeros((count, 128), f32)
-    weighted = jnp.zeros((count, 512), f32)
+    factors = [jnp.where(low, jnp.exp(stat - peak), 0.0) for stat in stats]
+    totals = [factor * pltpu.roll(stat, 64, 1) for factor, stat in zip(factors, stats)]
+    total = jnp.where(low, functools.reduce(jnp.add, totals), 1.0)
+    shares = jnp.concatenate([factor / total for factor in factors], axis=0)
+    wide = jnp.dot(shares, spread_ref[...], precision=exact, preferred_element_type=f32)
+    attended = jnp.zeros((count, 512), f32)
     for t in range(tiles):
-        factor = jnp.where(low, jnp.exp(stats[t] - peak), 0.0)
-        total = total + factor * pltpu.roll(stats[t], 64, 1)
-        wide = jnp.dot(factor, spread_ref[...], precision=exact, preferred_element_type=f32)
-        weighted = weighted + wide * parts_ref[t, :, :512]
-    total = jnp.where(low, total, 1.0)
-    share = jnp.where(low, 1.0 / total, 0.0)
-    attended = weighted * jnp.dot(share, spread_ref[...], precision=exact, preferred_element_type=f32)
+        attended = attended + wide[count * t : count * (t + 1)] * parts_ref[t, :, :512]
+    for t in range(tiles):
+        out_ref[t] = attended
+
+
+def combine(parts, spread):
+    return pl.pallas_call(
+        combine_body,
+        out_shape=jax.ShapeDtypeStruct(parts.shape[:2] + (512,), f32),
+        compiler_params=params(),
+        name="combine",
+    )(parts, spread)
+
+
+def value_body(attended_ref, value_ref, out_ref):
+    low = lax.broadcasted_iota(jnp.int32, (attended_ref.shape[0], 128), 1) < 64
     for latent in range(8):
-        part = attended[:, 128 * (latent // 2) : 128 * (latent // 2 + 1)]
+        part = attended_ref[:, 128 * (latent // 2) : 128 * (latent // 2 + 1)]
         part = jnp.where(low == (latent % 2 == 0), part, 0.0)
         out_ref[:, latent, :] = jnp.dot(
             part, value_ref[...], precision=exact, preferred_element_type=f32
         )
 
 
-def combine(parts, value_weight):
-    lane = jnp.arange(128)[:, None]
-    spread = (lane == jnp.arange(512)[None, :] // 64).astype(f32)
+def valued(attended, value_weight):
     return pl.pallas_call(
-        combine_body,
-        out_shape=jax.ShapeDtypeStruct((parts.shape[1], 8, 128), f32),
+        value_body,
+        out_shape=jax.ShapeDtypeStruct((attended.shape[0], 8, 128), f32),
         compiler_params=params(),
-        name="combine",
-    )(parts, jnp.concatenate([value_weight, value_weight], axis=0), spread)
-
-
-def spread_to(array, axis):
-    peers = lax.axis_size(axis)
-    return lax.all_to_all(jnp.broadcast_to(array[None], (peers,) + array.shape), axis, 0, 0)
+        name="valued",
+    )(attended, value_weight)
+
+
+def prepare(
+    kernel_one, kernel_two, kernel_three, latents, pos_key, first_conv_bias, shift_two, shift_three, w_key
+):
+    banded = bands(kernel_one, kernel_two, kernel_three)
+    query = jnp.dot(latents, w_key.T, precision=exact, preferred_element_type=f32).astype(bf16)
+    own = np.arange(8)[:, None] == np.arange(16)[None, :] % 8
+    query = query.T[None, :, None, :] * own[:, None, :, None].astype(bf16)
+    query = query.reshape(512, 128)
+    pos = jnp.einsum("ld,hwd->hwl", latents, pos_key, precision=exact).reshape(16, 64)
+    pos = jnp.concatenate([pos, pos], axis=1)
+    lane = np.arange(128)[:, None] % 64
+    column = np.arange(8 * 512)[None, :]
+    spread = jnp.asarray((lane == (column % 512) // 64 * 8 + column // 512).astype(bf16))
+    biases = (
+        jnp.tile(first_conv_bias, 48)[None],
+        jnp.tile(shift_two, 8)[None],
+        jnp.tile(shift_three, 4)[None],
+    )
+    return banded, biases, query, pos, spread
 
 
 def on_device(
@@ -322,37 +360,33 @@
     value_weight,
 ):
     tiles = lax.axis_size("tile")
-    every = spread_to(sources, "xy")
+    groups = lax.axis_size("xy")
+    copies = jnp.broadcast_to(sources[None], (groups,) + sources.shape)
+    copies, target = lax.optimization_barrier((copies, target))
+    every = lax.all_to_all(copies, "xy", 0, 0)
     rows = lax.all_gather(target, "zh", axis=0)
     width = rows.shape[2]
     up = [(i, i + 1) for i in range(tiles - 1)]
     down = [(j, i) for i, j in up]
     left = lax.ppermute(rows[:, :, width - HALO :], "tile", up)
     right = lax.ppermute(rows[:, :, :HALO], "tile", down)
-    cost = cost_maps(rows, left, right, every)
-    cost, kernel_one, kernel_two, kernel_three, latents, pos_key = lax.optimization_barrier(
-        (cost, kernel_one, kernel_two, kernel_three, latents, pos_key)
-    )
+    half = sources.shape[0] // 2
+    cost = cost_maps(rows, left, right, every, 0, half)
+    weights = (kernel_one, kernel_two, kernel_three, latents, pos_key)
+    cost, weights = lax.optimization_barrier((cost, weights))
+    prepared = prepare(*weights, first_conv_bias, shift_two, shift_three, w_key)
+    other = cost_maps(rows, left, right, every, half, half)
     cost = lax.all_to_all(cost, "xy", 0, 0)
-
-    banded = bands(kernel_one, kernel_two, kernel_three)
-    query = jnp.dot(latents, w_key.T, precision=exact, preferred_element_type=f32).astype(bf16)
-    own = jnp.arange(8)[:, None] == jnp.arange(16)[None, :] % 8
-    query = jnp.where(own[:, None, :, None], query.T[None, :, None, :], 0).reshape(512, 128)
-    pos = jnp.einsum("ld,hwd->hwl", latents, pos_key, precision=exact).reshape(16, 64)
-    pos = jnp.concatenate([pos, pos], axis=1)
-    lane = jnp.arange(128)[:, None] % 64
-    column = jnp.arange(8 * 512)[None, :]
-    spread = (lane == (column % 512) // 64 * 8 + column // 512).astype(bf16)
-    biases = (
-        jnp.tile(first_conv_bias, 48)[None],
-        jnp.tile(shift_two, 8)[None],
-        jnp.tile(shift_three, 4)[None],
-    )
-    parts = encode(cost, banded, biases, query, pos, spread)
+    other, prepared = lax.optimization_barrier((other, prepared))
+    other = lax.all_to_all(other, "xy", 0, 0)
+    parts = encode(cost, *prepared)
+    parts = encode(other, *prepared, parts)
     parts = lax.all_to_all(parts.reshape(tiles, -1, parts.shape[1]), "tile", 0, 0)
-    tokens = spread_to(combine(parts, value_weight), "tile")
-    return tokens.reshape((-1,) + tokens.shape[2:])
+    latent = np.arange(128)[:, None]
+    spread = jnp.asarray((latent == np.arange(512)[None, :] // 64).astype(np.float32))
+    attended = lax.all_to_all(combine(parts, spread), "tile", 0, 0)
+    value_weight = jnp.concatenate([value_weight, value_weight], axis=0)
+    return valued(attended.reshape(-1, attended.shape[-1]), value_weight)
 
 
 def solution(mesh):

time: 158 us -> 167 us (1.057)
  Pallas kernels: 54.4 us -> 76.7 us
  waiting for transfers between devices: 25.9 us -> 8.85 us
  starting transfers between devices: 22 us -> 33 us
  blocking collectives: 38.3 us -> 33.9 us
  other arithmetic: 3.52 us -> 1.42 us
    pallas_call x3 -> x6, Pallas kernels: 50.7 us -> 73.1 us  [the longest x2 63.9 us: encode(): pl.pallas_call(body, out_shape=jax.ShapeDtypeStruct((whole, 640), f32), s...]
    all_to_all x1, waiting for transfers between devices: 12.8 us -> 0.01 us  [on_device(): cost = lax.all_to_all(cost, 'xy', 0, 0)]
    all_to_all x2 -> x3, starting transfers between devices: 10.6 us -> 18.7 us  [the longest x1 7.58 us: on_device(): every = lax.all_to_all(copies, 'xy', 0, 0)]
    all_to_all x2 -> x3, waiting for transfers between devices: 13.1 us -> 5.21 us  [the longest x1 5.21 us: on_device(): attended = lax.all_to_all(combine(parts, spread), 'tile', 0, 0)]
    ppermute x1, waiting for transfers between devices: 0.01 us -> 3.64 us  [on_device(): right = lax.ppermute(rows[:, :, :HALO], 'tile', down)]
    all_to_all x1, blocking collectives: 12.7 us -> 9.39 us  [on_device(): lax.all_to_all(parts.reshape(tiles, -1, parts.shape[1]), 'tile', 0, 0)]
    all_to_all x1, starting transfers between devices: 3.84 us -> 6.79 us  [on_device(): cost = lax.all_to_all(cost, 'xy', 0, 0)]
    convert_element_type x2 -> x0, other arithmetic: 2.01 us -> none  [the longest x1 1.28 us: on_device(): spread = (lane == column % 512 // 64 * 8 + column // 512).astype(bf16)]
  transfers between devices with their start and end apart: 5 -> 6, of which waited for: 3 -> 2; matrix products, arithmetic and copies ran while one was open for 8% -> 5% of each run, Pallas kernels for 2% -> 23%
where the time goes in v2:
time: 167 us; the launch traced here: 166 us
  Pallas kernels  76.7 us (46%)
  blocking collectives  33.9 us (20%)
  starting transfers between devices  33 us (20%)
  local copies, waits for them, and re-layouts  11.2 us (7%)
  waiting for transfers between devices  8.85 us (5%)
    pallas_call x2, Pallas kernels, encode(): pl.pallas_call(body, out_shape=jax.ShapeDtypeStruct((whole, 640), f32), s...  63.9 us
    all_gather x1, blocking collectives, on_device(): rows = lax.all_gather(target, 'zh', axis=0)  24.5 us
    all_to_all x1, blocking collectives, on_device(): lax.all_to_all(parts.reshape(tiles, -1, parts.shape[1]), 'tile', 0, 0)  9.39 us
    all_to_all x1, starting transfers between devices, on_device(): every = lax.all_to_all(copies, 'xy', 0, 0)  7.58 us
    all_to_all x1, starting transfers between devices, on_device(): cost = lax.all_to_all(cost, 'xy', 0, 0)  6.79 us
    all_to_all x1, starting transfers between devices, on_device(): other = lax.all_to_all(other, 'xy', 0, 0)  6.65 us
    ppermute x1, starting transfers between devices, on_device(): left = lax.ppermute(rows[:, :, width - HALO:], 'tile', up)  5.53 us
    all_to_all x1, waiting for transfers between devices, on_device(): attended = lax.all_to_all(combine(parts, spread), 'tile', 0, 0)  5.21 us
  transfers between devices with their start and end apart: 6, of which 2 were waited for; matrix products, arithmetic and copies ran while one was open for 5% of the time, Pallas kernels for 23%

profile of v2, /device:TPU:1, one launch (start us, length us, event | category | flops | bytes accessed | tf_op | source)
XLA Modules:
  0.0 166.0 jit_solution(5191246741015322353)
XLA Ops:
  0.0 1.7 %broadcast_in_dim.2 = bf16[16,64,256]{2,1,0:T(8,128)(2,1)} broadcast(bf16[64,256]{1,0:T(8,128)(2,1)} %param.16), dimensions={1,2} | broadcast | bytes 557056 | tf_op jit(solution)/shard_map/broadcast_in_dim | solution.py:364
  1.7 7.6 %all-to-all-start = ((bf16[16,64,256]{2,1,0:T(8,128)(2,1)}), bf16[16,64,256]{2,1,0:T(8,128)(2,1)S(1)}, u32[]{:S(2)}, u32[]{:S(2)}) async-start(bf16[16,64,256]{2,1,0:T(8,128)(2,1)} %broadcast_in_dim.2), calls=%async_computation | async-start | bytes 1048576 | tf_op jit(solution)/shard_map/all_to_all | solution.py:366
  9.3 24.5 %all-gather = bf16[8,64,256]{2,1,0:T(8,128)(2,1)S(1)} all-gather(bf16[2,64,256]{2,1,0:T(8,128)(2,1)S(1)} %copy-done.10), channel_id=2, replica_groups=mesh['zh'=4,'xy'=16,'tile'=8] {'zh'}, dimensions={0}, use_global_device_ids=true | all-gather | bytes 327680 | tf_op jit(solution)/shard_map/all_gather | solution.py:367
  33.8 5.5 %collective-permute-start = (bf16[4,2,16,256]{3,2,1,0:T(8,128)(2,1)S(1)}, bf16[4,2,16,256]{3,2,1,0:T(8,128)(2,1)S(1)}, u32[]{:S(2)}, u32[]{:S(2)}) collective-permute-start(bf16[4,2,16,256]{3,2,1,0:T(8,128)(2,1)S(1)} %get-tuple-element.48), channel_id=1, source_target_pairs={{0,1},{1,2},{2,3},{3,4},{4,5},{5,6},{6,7},{8,9},{9,10},{10,11},{11... | collective-permute-start | bytes 196616 | tf_op jit(solution)/shard_map/ppermute | solution.py:371
  39.4 1.9 %collective-permute-start.1 = (bf16[4,2,16,256]{3,2,1,0:T(8,128)(2,1)S(1)}, bf16[4,2,16,256]{3,2,1,0:T(8,128)(2,1)S(1)}, u32[]{:S(2)}, u32[]{:S(2)}) collective-permute-start(bf16[4,2,16,256]{3,2,1,0:T(8,128)(2,1)S(1)} %get-tuple-element.47), channel_id=1, source_target_pairs={{1,0},{2,1},{3,2},{4,3},{5,4},{6,5},{7,6},{9,8},{10,9},{11,10},{12... | collective-permute-start | bytes 196616 | tf_op jit(solution)/shard_map/ppermute | solution.py:372
  41.3 0.0 collective-permute-done.left_ref
  41.3 3.6 %collective-permute-done.1.right_ref = bf16[4,2,16,256]{3,2,1,0:T(8,128)(2,1)S(1)} collective-permute-done((bf16[4,2,16,256]{3,2,1,0:T(8,128)(2,1)S(1)}, bf16[4,2,16,256]{3,2,1,0:T(8,128)(2,1)S(1)}, u32[]{:S(2)}, u32[]{:S(2)}) %collective-permute-start.1) | collective-permute-done | bytes 65568 | tf_op jit(solution)/shard_map/ppermute | solution.py:372
  44.9 0.0 all-to-all-done.sources_ref
  45.0 0.6 copy-done.8
  45.6 0.8 copy-done.1
  46.4 2.5 %cost_maps.3 = bf16[16,32,768]{2,1,0:T(8,128)(2,1)} custom-call(bf16[4,2,64,256]{3,2,1,0:T(8,128)(2,1)} %bitcast.24, bf16[4,2,16,256]{3,2,1,0:T(8,128)(2,1)} %copy-done.7, bf16[4,2,16,256]{3,2,1,0:T(8,128)(2,1)} %copy-done.8, bf16[16,64,256]{2,1,0:T(8,128)(2,1)} %copy-done.1), custom_call_target="tpu_custom_call" | custom-call | tf_op jit(solution)/shard_map/cost_maps/pallas_call | solution.py:57
  48.9 0.0 copy-start.9
  48.9 6.8 %all-to-all-start.2 = ((bf16[16,32,768]{2,1,0:T(8,128)(2,1)}), bf16[16,32,768]{2,1,0:T(8,128)(2,1)S(1)}, u32[]{:S(2)}, u32[]{:S(2)}) async-start(bf16[16,32,768]{2,1,0:T(8,128)(2,1)} %cost_maps.3), calls=%async_computation.2 | async-start | bytes 1572864 | tf_op jit(solution)/shard_map/all_to_all | solution.py:379
  55.7 0.0 copy-start.6
  55.7 0.7 broadcast_in_dim_tile.9.refs_4_.bias_one
  56.4 0.6 broadcast_in_dim_tile.10.refs_5_.bias_two
  57.0 0.6 broadcast_in_dim_tile.11.refs_6_.bias_three
  57.7 0.1 tile.49
  57.7 1.1 tile.50.one_ref
  58.8 0.1 copy.26
  58.9 0.1 tile.52
  59.0 0.9 copy.28.two_ref
  59.9 0.2 copy.27
  60.0 0.0 copy-start.13
  60.0 0.0 copy-start.15
  60.1 0.1 tile.55
  60.1 0.0 copy-start.11
  60.1 1.1 copy.29.three_ref
  61.2 0.1 fusion
  61.4 0.1 broadcast_multiply_fusion
  61.5 0.2 mul.23
  61.7 0.6 convolution_bitcast_fusion
  62.3 0.1 copy.31
  62.4 3.6 %bands.1 = (bf16[768,768]{1,0:T(8,128)(2,1)}, bf16[2304,256]{1,0:T(8,128)(2,1)}, bf16[2304,256]{1,0:T(8,128)(2,1)}) custom-call(bf16[6,6,768]{2,1,0:T(8,128)(2,1)} %tile.50.one_ref, bf16[6,96,256]{2,1,0:T(8,128)(2,1)} %copy.28.two_ref, bf16[6,192,256]{2,1,0:T(8,128)(2,1)} %copy.29.three_ref), custom_call_target="tpu_custom_call" | custom-call | tf_op jit(solution)/shard_map/bands/pallas_call | solution.py:104
  66.0 2.5 %cost_maps.2 = bf16[16,32,768]{2,1,0:T(8,128)(2,1)} custom-call(bf16[4,2,64,256]{3,2,1,0:T(8,128)(2,1)} %bitcast.25, bf16[4,2,16,256]{3,2,1,0:T(8,128)(2,1)} %copy-done.7, bf16[4,2,16,256]{3,2,1,0:T(8,128)(2,1)} %copy-done.8, bf16[16,64,256]{2,1,0:T(8,128)(2,1)} %copy-done.1), custom_call_target="tpu_custom_call" | custom-call | tf_op jit(solution)/shard_map/cost_maps/pallas_call | solution.py:57
  68.5 0.7 pad_maximum_fusion.1.refs_8_.pos_ref
  69.2 6.7 %all-to-all-start.1 = ((bf16[16,32,768]{2,1,0:T(8,128)(2,1)}), bf16[16,32,768]{2,1,0:T(8,128)(2,1)S(1)}, u32[]{:S(2)}, u32[]{:S(2)}) async-start(bf16[16,32,768]{2,1,0:T(8,128)(2,1)} %cost_maps.2), calls=%async_computation.1 | async-start | bytes 1572864 | tf_op jit(solution)/shard_map/all_to_all | solution.py:381
  75.9 0.8 copy.34.refs_7_.query_ref
  76.6 31.9 %encode.2.before_ref = f32[32,640]{1,0:T(8,128)} custom-call(bf16[16,32,768]{2,1,0:T(8,128)(2,1)} %copy-done.3, bf16[768,768]{1,0:T(8,128)(2,1)} %get-tuple-element.37.refs_1_.one_ref, bf16[2304,256]{1,0:T(8,128)(2,1)} %get-tuple-element.38.refs_2_.two_ref, bf16[2304,256]{1,0:T(8,128)(2,1)} %get-tuple-element.39.refs_3_.three_ref, ...), custom_call_target="tpu_custom_call" | custom-call | tf_op jit(solution)/shard_map/encode/pallas_call | solution.py:267
  108.6 0.9 copy-done.4
  109.4 31.9 %encode.3 = f32[64,640]{1,0:T(8,128)} custom-call(bf16[16,32,768]{2,1,0:T(8,128)(2,1)} %copy-done.4, bf16[768,768]{1,0:T(8,128)(2,1)} %get-tuple-element.37.refs_1_.one_ref, bf16[2304,256]{1,0:T(8,128)(2,1)} %get-tuple-element.38.refs_2_.two_ref, bf16[2304,256]{1,0:T(8,128)(2,1)} %get-tuple-element.39.refs_3_.three_ref, ...), custom_call_target="tpu_custom_call" | custom-call | tf_op jit(solution)/shard_map/encode/pallas_call | solution.py:267
  141.4 9.4 %all_to_all.25.parts_ref = f32[8,8,640]{2,1,0:T(8,128)} all-to-all(f32[8,8,640]{2,1,0:T(8,128)} %bitcast.28), channel_id=1, replica_groups=mesh['zh'=4,'xy'=16,'tile'=8] {'tile'}, dimensions={0} | all-to-all | bytes 327680 | tf_op jit(solution)/shard_map/all_to_all | solution.py:384
  150.8 2.0 %combine.1 = f32[8,8,512]{2,1,0:T(8,128)} custom-call(f32[8,8,640]{2,1,0:T(8,128)} %all_to_all.25.parts_ref, f32[128,512]{1,0:T(8,128)} %constant.8.clone.spread_ref), custom_call_target="tpu_custom_call" | custom-call | tf_op jit(solution)/shard_map/combine/pallas_call | solution.py:300
  152.8 4.5 %all-to-all-start.4 = ((f32[8,8,512]{2,1,0:T(8,128)}), f32[8,8,512]{2,1,0:T(8,128)S(1)}, u32[]{:S(2)}, u32[]{:S(2)}) async-start(f32[8,8,512]{2,1,0:T(8,128)} %combine.1), calls=%async_computation.4 | async-start | bytes 262144 | tf_op jit(solution)/shard_map/all_to_all | solution.py:387
  157.3 0.6 pad_maximum_fusion.value_ref
  158.0 5.2 %all-to-all-done.4 = f32[8,8,512]{2,1,0:T(8,128)S(1)} async-done(((f32[8,8,512]{2,1,0:T(8,128)}), f32[8,8,512]{2,1,0:T(8,128)S(1)}, u32[]{:S(2)}, u32[]{:S(2)}) %all-to-all-start.4) | async-done | bytes 131104 | tf_op jit(solution)/shard_map/all_to_all | solution.py:387
  163.2 0.6 copy-done.5
  163.8 2.2 %valued.1 = f32[64,8,128]{2,1,0:T(8,128)} custom-call(f32[64,512]{1,0:T(8,128)} %bitcast.29, f32[128,128]{1,0:T(8,128)} %pad_maximum_fusion.value_ref), custom_call_target="tpu_custom_call" | custom-call | tf_op jit(solution)/shard_map/valued/pallas_call | solution.py:319
  (35 shorter events, 0.1 us)
Async XLA Ops:
  0.0 61.2 %copy-start = (f32[64,128]{1,0:T(8,128)S(1)}, f32[64,128]{1,0:T(8,128)}, u32[]{:S(2)}) copy-start(f32[64,128]{1,0:T(8,128)} %param.25) | copy-start | bytes 98308
  0.0 9.3 %copy-start.10 = (bf16[2,64,256]{2,1,0:T(8,128)(2,1)S(1)}, bf16[2,64,256]{2,1,0:T(8,128)(2,1)}, u32[]{:S(2)}) copy-start(bf16[2,64,256]{2,1,0:T(8,128)(2,1)} %param.15) | copy-start | bytes 196612
  1.7 43.3 %all-to-all-start = ((bf16[16,64,256]{2,1,0:T(8,128)(2,1)}), bf16[16,64,256]{2,1,0:T(8,128)(2,1)S(1)}, u32[]{:S(2)}, u32[]{:S(2)}) async-start(bf16[16,64,256]{2,1,0:T(8,128)(2,1)} %broadcast_in_dim.2), calls=%async_computation | async-start | bytes 1048576 | tf_op jit(solution)/shard_map/all_to_all | solution.py:366
  33.8 11.1 %copy-start.2 = (bf16[8,64,256]{2,1,0:T(8,128)(2,1)}, bf16[8,64,256]{2,1,0:T(8,128)(2,1)S(1)}, u32[]{:S(2)}) copy-start(bf16[8,64,256]{2,1,0:T(8,128)(2,1)S(1)} %all-gather) | copy-start | bytes 786436
  33.8 7.5 %collective-permute-start = (bf16[4,2,16,256]{3,2,1,0:T(8,128)(2,1)S(1)}, bf16[4,2,16,256]{3,2,1,0:T(8,128)(2,1)S(1)}, u32[]{:S(2)}, u32[]{:S(2)}) collective-permute-start(bf16[4,2,16,256]{3,2,1,0:T(8,128)(2,1)S(1)} %get-tuple-element.48), channel_id=1, source_target_pairs={{0,1},{1,2},{2,3},{3,4},{4,5},{5,6},{6,7},{8,9},{9,10},{10,11},{11... | collective-permute-start | bytes 196616 | tf_op jit(solution)/shard_map/ppermute | solution.py:371
  39.4 5.6 %collective-permute-start.1 = (bf16[4,2,16,256]{3,2,1,0:T(8,128)(2,1)S(1)}, bf16[4,2,16,256]{3,2,1,0:T(8,128)(2,1)S(1)}, u32[]{:S(2)}, u32[]{:S(2)}) collective-permute-start(bf16[4,2,16,256]{3,2,1,0:T(8,128)(2,1)S(1)} %get-tuple-element.47), channel_id=1, source_target_pairs={{1,0},{2,1},{3,2},{4,3},{5,4},{6,5},{7,6},{9,8},{10,9},{11,10},{12... | collective-permute-start | bytes 196616 | tf_op jit(solution)/shard_map/ppermute | solution.py:372
  41.3 3.7 %copy-start.7 = (bf16[4,2,16,256]{3,2,1,0:T(8,128)(2,1)}, bf16[4,2,16,256]{3,2,1,0:T(8,128)(2,1)S(1)}, u32[]{:S(2)}) copy-start(bf16[4,2,16,256]{3,2,1,0:T(8,128)(2,1)S(1)} %collective-permute-done.left_ref) | copy-start | bytes 196612
  44.9 0.6 copy-start.8
  45.6 0.8 copy-start.1
  48.9 6.8 %copy-start.16 = (f32[16]{0:T(128)S(1)}, f32[16]{0:T(128)}, u32[]{:S(2)}) copy-start(f32[16]{0:T(128)} %param.18) | copy-start | bytes 196
  48.9 7.5 %copy-start.17 = (f32[32]{0:T(128)S(1)}, f32[32]{0:T(128)}, u32[]{:S(2)}) copy-start(f32[32]{0:T(128)} %param.20) | copy-start | bytes 388
  48.9 8.2 %copy-start.18 = (f32[64]{0:T(128)S(1)}, f32[64]{0:T(128)}, u32[]{:S(2)}) copy-start(f32[64]{0:T(128)} %param.22) | copy-start | bytes 772
  48.9 8.8 %copy-start.14 = (bf16[6,6,1,16]{3,1,2,0:T(8,128)(2,1)S(1)}, bf16[6,6,1,16]{3,1,2,0:T(8,128)(2,1)}, u32[]{:S(2)}) copy-start(bf16[6,6,1,16]{3,1,2,0:T(8,128)(2,1)} %param.17) | copy-start | bytes 3460
  48.9 9.9 %copy-start.9 = (bf16[6,6,16,32]{3,2,1,0:T(8,128)(2,1)S(1)}, bf16[6,6,16,32]{3,2,1,0:T(8,128)(2,1)}, u32[]{:S(2)}) copy-start(bf16[6,6,16,32]{3,2,1,0:T(8,128)(2,1)} %param.19) | copy-start | bytes 110596
  48.9 20.3 %all-to-all-start.2 = ((bf16[16,32,768]{2,1,0:T(8,128)(2,1)}), bf16[16,32,768]{2,1,0:T(8,128)(2,1)S(1)}, u32[]{:S(2)}, u32[]{:S(2)}) async-start(bf16[16,32,768]{2,1,0:T(8,128)(2,1)} %cost_maps.3), calls=%async_computation.2 | async-start | bytes 1572864 | tf_op jit(solution)/shard_map/all_to_all | solution.py:379
  55.7 4.2 %copy-start.6 = (bf16[6,6,32,64]{3,2,1,0:T(8,128)(2,1)S(1)}, bf16[6,6,32,64]{3,2,1,0:T(8,128)(2,1)}, u32[]{:S(2)}) copy-start(bf16[6,6,32,64]{3,2,1,0:T(8,128)(2,1)} %param.21) | copy-start | bytes 442372
  60.0 1.2 copy-start.13
  60.0 1.3 copy-start.15
  60.1 1.6 copy-start.11
  69.2 7.4 %copy-start.3 = (bf16[16,32,768]{2,1,0:T(8,128)(2,1)}, bf16[16,32,768]{2,1,0:T(8,128)(2,1)S(1)}, u32[]{:S(2)}) copy-start(bf16[16,32,768]{2,1,0:T(8,128)(2,1)S(1)} %all-to-all-done.2.refs_0_) | copy-start | bytes 2359300
  69.2 39.4 %all-to-all-start.1 = ((bf16[16,32,768]{2,1,0:T(8,128)(2,1)}), bf16[16,32,768]{2,1,0:T(8,128)(2,1)S(1)}, u32[]{:S(2)}, u32[]{:S(2)}) async-start(bf16[16,32,768]{2,1,0:T(8,128)(2,1)} %cost_maps.2), calls=%async_computation.1 | async-start | bytes 1572864 | tf_op jit(solution)/shard_map/all_to_all | solution.py:381
  108.5 48.8 %copy-start.12 = (f32[64,128]{1,0:T(8,128)S(1)}, f32[64,128]{1,0:T(8,128)}, u32[]{:S(2)}) copy-start(f32[64,128]{1,0:T(8,128)} %param.26) | copy-start | bytes 98308
  108.6 0.9 copy-start.4
  152.8 10.4 %all-to-all-start.4 = ((f32[8,8,512]{2,1,0:T(8,128)}), f32[8,8,512]{2,1,0:T(8,128)S(1)}, u32[]{:S(2)}, u32[]{:S(2)}) async-start(f32[8,8,512]{2,1,0:T(8,128)} %combine.1), calls=%async_computation.4 | async-start | bytes 262144 | tf_op jit(solution)/shard_map/all_to_all | solution.py:387
  163.2 0.7 copy-start.5

commit v3 on v2

--- a/solution.py
+++ b/solution.py
@@ -19,6 +19,9 @@
 PAIRS = 64
 EDGE = 7
 VMEM = 56 * 1024 * 1024
+ROWS_ONE = 38
+ROWS_TWO = 18
+ROWS_THREE = 16
 
 
 def params():
@@ -136,7 +139,7 @@
     done = before_ref.shape[0] if before_ref is not None else 0
     blank = jnp.zeros((EDGE, count, 256), bf16)
     pairs[0:EDGE] = blank
-    pairs[EDGE + PAIRS :] = blank
+    pairs[EDGE + PAIRS : 2 * EDGE + PAIRS] = blank
 
     def place(i, _):
         for z in range(4):
@@ -149,13 +152,11 @@
 
     lax.fori_loop(0, GROUP, place, 0, unroll=2)
 
-    step = 4
-    flat = step * count
-
     def first(i, _):
+        step = ROWS_ONE
         h = i * step
         left = jnp.concatenate(
-            [pairs[pl.ds(h + j, step)].reshape(flat, 256) for j in range(3)], axis=1
+            [pairs[pl.ds(h + j, step)].reshape(step * count, 256) for j in range(3)], axis=1
         )
         for n in range(3):
             lanes = slice(256 * n, 256 * (n + 1))
@@ -165,85 +166,69 @@
             )
         return 0
 
-    lax.fori_loop(0, 76 // step, first, 0)
+    lax.fori_loop(0, pl.cdiv(76, ROWS_ONE), first, 0)
+
+    def taps(source, h, step, lanes):
+        parts = [
+            source[pl.ds(h + k // 2, step), k % 2, :, lanes].reshape(step * count, -1)
+            for k in range(6)
+        ]
+        return jnp.concatenate(parts, axis=1)
+
+    short = jnp.concatenate([two_ref[384 * k : 384 * k + 256, :128] for k in range(6)], axis=0)
 
     def second(i, _):
+        step = ROWS_TWO
         h = i * step
-
-        def left(lanes):
-            return jnp.concatenate(
-                [
-                    hidden_one[pl.ds(h + k // 2, step), k % 2, :, lanes].reshape(flat, -1)
-                    for k in range(6)
-                ],
-                axis=1,
-            )
-
-        def save(value, lanes):
+        for n in range(3):
+            lanes = slice(256 * n, min(256 * n + 384, 768))
+            right, bias = (two_ref[...], bias_two[...])
+            if n == 2:
+                right, bias = (short, bias_two[:, :128])
+            value = gelu(mm(taps(hidden_one, h, step, lanes), right) + bias)
+            lanes = slice(256 * n, 256 * n + value.shape[1])
             hidden_two[pl.ds(i * (step // 2), step // 2), :, :, lanes] = value.astype(bf16).reshape(
                 step // 2, 2, count, -1
             )
-
-        for n in range(2):
-            value = mm(left(slice(256 * n, 256 * n + 384)), two_ref[...])
-            save(gelu(value + bias_two[...]), slice(256 * n, 256 * (n + 1)))
-        short = jnp.concatenate([two_ref[384 * k : 384 * k + 256, :128] for k in range(6)], axis=0)
-        value = mm(left(slice(512, 768)), short)
-        save(gelu(value + bias_two[:, :128]), slice(512, 640))
         return 0
 
-    lax.fori_loop(0, 36 // step, second, 0)
+    lax.fori_loop(0, 36 // ROWS_TWO, second, 0)
 
     def third(i, _):
+        step = ROWS_THREE
         h = i * step
         for n in range(2):
-            left = jnp.concatenate(
-                [
-                    hidden_two[
-                        pl.ds(h + k // 2, step), k % 2, :, 256 * n : 256 * n + 384
-                    ].reshape(flat, 384)
-                    for k in range(6)
-                ],
-                axis=1,
-            )
+            left = taps(hidden_two, h, step, slice(256 * n, 256 * n + 384))
             value = mm(left, three_ref[...]) + bias_three[...]
             features[pl.ds(h, step), :, 256 * n : 256 * (n + 1)] = value.astype(bf16).reshape(
                 step, count, 256
             )
         return 0
 
-    lax.fori_loop(0, 16 // step, third, 0)
+    lax.fori_loop(0, 16 // ROWS_THREE, third, 0)
 
     scale = 1.0 / math.sqrt(128)
 
-    def score(h, peak):
-        value = (mm(features[h], query_ref[...]) + pos_ref[pl.ds(h, 1), :]) * scale
-        score_ref[h] = value
-        return jnp.maximum(peak, value)
-
-    peak = lax.fori_loop(0, 16, score, jnp.full((count, 128), -jnp.inf, f32), unroll=2)
+    value = mm(features[...].reshape(16 * count, 512), query_ref[...]).reshape(16, count, 128)
+    value = (value + pos_ref[...][:, None, :]) * scale
+    score_ref[...] = value
+    peak = jnp.max(value, axis=0)
     for k in (8, 16, 32):
         peak = jnp.maximum(peak, pltpu.roll(peak, k, 1))
     low = lax.broadcasted_iota(jnp.int32, (count, 128), 1) < 64
 
-    def weigh(h, total):
-        value = jnp.exp(score_ref[h] - peak)
-        head = value.astype(bf16).astype(f32)
-        score_ref[h] = jnp.where(low, head, value - head)
-        return total + value
-
-    total = lax.fori_loop(0, 16, weigh, jnp.zeros((count, 128), f32), unroll=2)
+    value = jnp.exp(score_ref[...] - peak)
+    total = jnp.sum(value, axis=0)
+    head = value.astype(bf16).astype(f32)
+    shares = jnp.where(low, head, value - head).astype(bf16).reshape(16 * count, 128)
     for k in (8, 16, 32):
         total = total + pltpu.roll(total, k, 1)
 
     def gather(latent):
         spread = spread_ref[:, 512 * latent : 512 * (latent + 1)]
 
-        def one(h, acc):
-            value = mm(score_ref[h].astype(bf16), spread)
-            return acc + value * features[h].astype(f32)
-
-        acc = lax.fori_loop(0, 16, one, jnp.zeros((count, 512), f32), unroll=2)
+        value = mm(shares, spread).reshape(16, count, 512)
+        acc = jnp.sum(value * features[...].astype(f32), axis=0)
         acc = (acc[:, :128] + acc[:, 128:256]) + (acc[:, 256:384] + acc[:, 384:])
         return acc + pltpu.roll(acc, 64, 1)
 
@@ -268,8 +253,8 @@
         body,
         out_shape=jax.ShapeDtypeStruct((whole, 640), f32),
         scratch_shapes=[
-            pltpu.VMEM((PAIRS + 2 * EDGE, count, 256), bf16),
-            pltpu.VMEM((38, 2, count, 768), bf16),
+            pltpu.VMEM((pl.cdiv(76, ROWS_ONE) * ROWS_ONE + 2, count, 256), bf16),
+            pltpu.VMEM((pl.cdiv(76, ROWS_ONE) * (ROWS_ONE // 2), 2, count, 768), bf16),
             pltpu.VMEM((18, 2, count, 640), bf16),
             pltpu.VMEM((16, count, 512), bf16),
             pltpu.VMEM((16, count, 128), f32),
@@ -370,17 +355,11 @@
     down = [(j, i) for i, j in up]
     left = lax.ppermute(rows[:, :, width - HALO :], "tile", up)
     right = lax.ppermute(rows[:, :, :HALO], "tile", down)
-    half = sources.shape[0] // 2
-    cost = cost_maps(rows, left, right, every, 0, half)
+    cost = cost_maps(rows, left, right, every, 0, sources.shape[0])
     weights = (kernel_one, kernel_two, kernel_three, latents, pos_key)
     cost, weights = lax.optimization_barrier((cost, weights))
     prepared = prepare(*weights, first_conv_bias, shift_two, shift_three, w_key)
-    other = cost_maps(rows, left, right, every, half, half)
-    cost = lax.all_to_all(cost, "xy", 0, 0)
-    other, prepared = lax.optimization_barrier((other, prepared))
-    other = lax.all_to_all(other, "xy", 0, 0)
-    parts = encode(cost, *prepared)
-    parts = encode(other, *prepared, parts)
+    parts = encode(lax.all_to_all(cost, "xy", 0, 0), *prepared)
     parts = lax.all_to_all(parts.reshape(tiles, -1, parts.shape[1]), "tile", 0, 0)
     latent = np.arange(128)[:, None]
     spread = jnp.asarray((latent == np.arange(512)[None, :] // 64).astype(np.float32))

time: 167 us -> 134 us (0.80)
  Pallas kernels: 76.7 us -> 38.2 us
  waiting for transfers between devices: 8.85 us -> 19.4 us
  starting transfers between devices: 33 us -> 26.3 us
  blocking collectives: 33.9 us -> 35.7 us
    pallas_call x2 -> x1, Pallas kernels: 63.9 us -> 27.2 us  [encode(): pl.pallas_call(body, out_shape=jax.ShapeDtypeStruct((whole, 640), f32), s...]
    all_to_all x2 -> x1, waiting for transfers between devices: 0.01 us -> 10.5 us  [on_device(): parts = encode(lax.all_to_all(cost, 'xy', 0, 0), *prepared)]
    all_to_all x2 -> x1, starting transfers between devices: 13.4 us -> 6.79 us  [on_device(): parts = encode(lax.all_to_all(cost, 'xy', 0, 0), *prepared)]
    pallas_call x2 -> x1, Pallas kernels: 4.99 us -> 2.98 us  [cost_maps(): pl.pallas_call(functools.partial(cost_body, first=first), out_shape=jax.S...]
    all_to_all x1, blocking collectives: 9.39 us -> 11.2 us  [on_device(): lax.all_to_all(parts.reshape(tiles, -1, parts.shape[1]), 'tile', 0, 0)]
  transfers between devices with their start and end apart: 6 -> 5, of which waited for: 2 -> 3; matrix products, arithmetic and copies ran while one was open for 5% -> 6% of each run, Pallas kernels for 23% -> 3%
where the time goes in v3:
time: 134 us; the launch traced here: 133 us
  Pallas kernels  38.2 us (29%)
  blocking collectives  35.7 us (27%)
  starting transfers between devices  26.3 us (20%)
  waiting for transfers between devices  19.4 us (14%)
  local copies, waits for them, and re-layouts  11.4 us (9%)
  other arithmetic  1.41 us (1%)
    pallas_call x1, Pallas kernels, encode(): pl.pallas_call(body, out_shape=jax.ShapeDtypeStruct((whole, 640), f32), s...  27.2 us
    all_gather x1, blocking collectives, on_device(): rows = lax.all_gather(target, 'zh', axis=0)  24.5 us
    all_to_all x1, blocking collectives, on_device(): lax.all_to_all(parts.reshape(tiles, -1, parts.shape[1]), 'tile', 0, 0)  11.2 us
    all_to_all x1, waiting for transfers between devices, on_device(): parts = encode(lax.all_to_all(cost, 'xy', 0, 0), *prepared)  10.5 us
    all_to_all x1, starting transfers between devices, on_device(): every = lax.all_to_all(copies, 'xy', 0, 0)  7.58 us
    all_to_all x1, starting transfers between devices, on_device(): parts = encode(lax.all_to_all(cost, 'xy', 0, 0), *prepared)  6.79 us
    ppermute x1, starting transfers between devices, on_device(): left = lax.ppermute(rows[:, :, width - HALO:], 'tile', up)  5.53 us
    all_to_all x1, waiting for transfers between devices, on_device(): attended = lax.all_to_all(combine(parts, spread), 'tile', 0, 0)  5.21 us
  transfers between devices with their start and end apart: 5, of which 3 were waited for; matrix products, arithmetic and copies ran while one was open for 6% of the time, Pallas kernels for 3%

profile of v3, /device:TPU:1, one launch (start us, length us, event | category | flops | bytes accessed | tf_op | source)
XLA Modules:
  0.0 133.4 jit_solution(10400360285556200902)
XLA Ops:
  0.0 1.7 %broadcast_in_dim.2 = bf16[16,64,256]{2,1,0:T(8,128)(2,1)} broadcast(bf16[64,256]{1,0:T(8,128)(2,1)} %param.16), dimensions={1,2} | broadcast | bytes 557056 | tf_op jit(solution)/shard_map/broadcast_in_dim | solution.py:349
  1.7 7.6 %all-to-all-start = ((bf16[16,64,256]{2,1,0:T(8,128)(2,1)}), bf16[16,64,256]{2,1,0:T(8,128)(2,1)S(1)}, u32[]{:S(2)}, u32[]{:S(2)}) async-start(bf16[16,64,256]{2,1,0:T(8,128)(2,1)} %broadcast_in_dim.2), calls=%async_computation | async-start | bytes 1048576 | tf_op jit(solution)/shard_map/all_to_all | solution.py:351
  9.3 24.5 %all-gather = bf16[8,64,256]{2,1,0:T(8,128)(2,1)S(1)} all-gather(bf16[2,64,256]{2,1,0:T(8,128)(2,1)S(1)} %copy-done.7), channel_id=2, replica_groups=mesh['zh'=4,'xy'=16,'tile'=8] {'zh'}, dimensions={0}, use_global_device_ids=true | all-gather | bytes 327680 | tf_op jit(solution)/shard_map/all_gather | solution.py:352
  33.8 5.5 %collective-permute-start = (bf16[4,2,16,256]{3,2,1,0:T(8,128)(2,1)S(1)}, bf16[4,2,16,256]{3,2,1,0:T(8,128)(2,1)S(1)}, u32[]{:S(2)}, u32[]{:S(2)}) collective-permute-start(bf16[4,2,16,256]{3,2,1,0:T(8,128)(2,1)S(1)} %get-tuple-element.28), channel_id=1, source_target_pairs={{0,1},{1,2},{2,3},{3,4},{4,5},{5,6},{6,7},{8,9},{9,10},{10,11},{11... | collective-permute-start | bytes 196616 | tf_op jit(solution)/shard_map/ppermute | solution.py:356
  39.4 1.9 %collective-permute-start.1 = (bf16[4,2,16,256]{3,2,1,0:T(8,128)(2,1)S(1)}, bf16[4,2,16,256]{3,2,1,0:T(8,128)(2,1)S(1)}, u32[]{:S(2)}, u32[]{:S(2)}) collective-permute-start(bf16[4,2,16,256]{3,2,1,0:T(8,128)(2,1)S(1)} %get-tuple-element.27), channel_id=1, source_target_pairs={{1,0},{2,1},{3,2},{4,3},{5,4},{6,5},{7,6},{9,8},{10,9},{11,10},{12... | collective-permute-start | bytes 196616 | tf_op jit(solution)/shard_map/ppermute | solution.py:357
  41.3 0.0 collective-permute-done.left_ref
  41.3 3.6 %collective-permute-done.1.right_ref = bf16[4,2,16,256]{3,2,1,0:T(8,128)(2,1)S(1)} collective-permute-done((bf16[4,2,16,256]{3,2,1,0:T(8,128)(2,1)S(1)}, bf16[4,2,16,256]{3,2,1,0:T(8,128)(2,1)S(1)}, u32[]{:S(2)}, u32[]{:S(2)}) %collective-permute-start.1) | collective-permute-done | bytes 65568 | tf_op jit(solution)/shard_map/ppermute | solution.py:357
  44.9 0.0 all-to-all-done.sources_ref
  45.0 0.6 copy-done.9
  45.5 0.8 copy-done.2
  46.3 3.0 %cost_maps.1 = bf16[16,64,768]{2,1,0:T(8,128)(2,1)} custom-call(bf16[4,2,64,256]{3,2,1,0:T(8,128)(2,1)} %bitcast.25, bf16[4,2,16,256]{3,2,1,0:T(8,128)(2,1)} %copy-done.8, bf16[4,2,16,256]{3,2,1,0:T(8,128)(2,1)} %copy-done.9, bf16[16,64,256]{2,1,0:T(8,128)(2,1)} %copy-done.2), custom_call_target="tpu_custom_call" | custom-call | tf_op jit(solution)/shard_map/cost_maps/pallas_call | solution.py:60
  49.3 0.0 copy-start.6
  49.3 6.8 %all-to-all-start.1 = ((bf16[16,64,768]{2,1,0:T(8,128)(2,1)}), bf16[16,64,768]{2,1,0:T(8,128)(2,1)S(1)}, u32[]{:S(2)}, u32[]{:S(2)}) async-start(bf16[16,64,768]{2,1,0:T(8,128)(2,1)} %cost_maps.1), calls=%async_computation.1 | async-start | bytes 3145728 | tf_op jit(solution)/shard_map/all_to_all | solution.py:362
  56.2 0.0 copy-start.5
  56.2 0.7 broadcast_in_dim_tile.9.refs_4_
  56.9 0.6 broadcast_in_dim_tile.10.refs_5_
  57.5 0.6 broadcast_in_dim_tile.11.refs_6_
  58.1 0.1 tile.49
  58.2 1.1 tile.50.one_ref
  59.3 0.1 copy.25
  59.4 0.1 tile.52
  59.5 0.9 copy.27.two_ref
  60.3 0.0 copy-done.5
  60.3 0.2 copy.26
  60.5 0.0 copy-start.12
  60.5 0.0 copy-start.14
  60.5 0.1 tile.55
  60.6 0.0 copy-start.10
  60.6 1.1 copy.28.three_ref
  61.7 0.1 fusion
  61.9 0.1 broadcast_multiply_fusion
  62.0 0.2 mul.23
  62.2 0.8 copy.32.refs_7_
  63.0 0.0 copy-done.10
  63.0 0.6 convolution_bitcast_fusion
  63.6 0.1 copy.30
  63.6 3.7 %bands.1 = (bf16[768,768]{1,0:T(8,128)(2,1)}, bf16[2304,256]{1,0:T(8,128)(2,1)}, bf16[2304,256]{1,0:T(8,128)(2,1)}) custom-call(bf16[6,6,768]{2,1,0:T(8,128)(2,1)} %tile.50.one_ref, bf16[6,96,256]{2,1,0:T(8,128)(2,1)} %copy.27.two_ref, bf16[6,192,256]{2,1,0:T(8,128)(2,1)} %copy.28.three_ref), custom_call_target="tpu_custom_call" | custom-call | tf_op jit(solution)/shard_map/bands/pallas_call | solution.py:107
  67.3 0.7 pad_maximum_fusion.1.refs_8_
  68.0 10.5 %all-to-all-done.1.refs_0_ = bf16[16,64,768]{2,1,0:T(8,128)(2,1)S(1)} async-done(((bf16[16,64,768]{2,1,0:T(8,128)(2,1)}), bf16[16,64,768]{2,1,0:T(8,128)(2,1)S(1)}, u32[]{:S(2)}, u32[]{:S(2)}) %all-to-all-start.1) | async-done | bytes 1572896 | tf_op jit(solution)/shard_map/all_to_all | solution.py:362
  78.5 1.2 copy-done.1
  79.7 27.2 %encode.1 = f32[64,640]{1,0:T(8,128)} custom-call(bf16[16,64,768]{2,1,0:T(8,128)(2,1)} %copy-done.1, bf16[768,768]{1,0:T(8,128)(2,1)} %get-tuple-element.22.refs_1_, bf16[2304,256]{1,0:T(8,128)(2,1)} %get-tuple-element.23.refs_2_, bf16[2304,256]{1,0:T(8,128)(2,1)} %get-tuple-element.24.refs_3_, f32[1,768]{1,0:T(1,128)} %broadcast_in_dim_tile.9.refs_4_, ...), custom_call_target="tpu_custom_call" | custom-call | tf_op jit(solution)/shard_map/encode/pallas_call | solution.py:252
  106.9 11.2 %all_to_all.20.parts_ref = f32[8,8,640]{2,1,0:T(8,128)} all-to-all(f32[8,8,640]{2,1,0:T(8,128)} %bitcast.27), channel_id=1, replica_groups=mesh['zh'=4,'xy'=16,'tile'=8] {'tile'}, dimensions={0} | all-to-all | bytes 327680 | tf_op jit(solution)/shard_map/all_to_all | solution.py:363
  118.1 2.0 %combine.1 = f32[8,8,512]{2,1,0:T(8,128)} custom-call(f32[8,8,640]{2,1,0:T(8,128)} %all_to_all.20.parts_ref, f32[128,512]{1,0:T(8,128)} %constant.8.clone.spread_ref), custom_call_target="tpu_custom_call" | custom-call | tf_op jit(solution)/shard_map/combine/pallas_call | solution.py:285
  120.1 4.5 %all-to-all-start.3 = ((f32[8,8,512]{2,1,0:T(8,128)}), f32[8,8,512]{2,1,0:T(8,128)S(1)}, u32[]{:S(2)}, u32[]{:S(2)}) async-start(f32[8,8,512]{2,1,0:T(8,128)} %combine.1), calls=%async_computation.3 | async-start | bytes 262144 | tf_op jit(solution)/shard_map/all_to_all | solution.py:366
  124.7 0.6 pad_maximum_fusion.value_ref
  125.3 5.2 %all-to-all-done.3 = f32[8,8,512]{2,1,0:T(8,128)S(1)} async-done(((f32[8,8,512]{2,1,0:T(8,128)}), f32[8,8,512]{2,1,0:T(8,128)S(1)}, u32[]{:S(2)}, u32[]{:S(2)}) %all-to-all-start.3) | async-done | bytes 131104 | tf_op jit(solution)/shard_map/all_to_all | solution.py:366
  130.5 0.6 copy-done.4
  131.2 2.2 %valued.1 = f32[64,8,128]{2,1,0:T(8,128)} custom-call(f32[64,512]{1,0:T(8,128)} %bitcast.28, f32[128,128]{1,0:T(8,128)} %pad_maximum_fusion.value_ref), custom_call_target="tpu_custom_call" | custom-call | tf_op jit(solution)/shard_map/valued/pallas_call | solution.py:304
  (29 shorter events, 0.1 us)
Async XLA Ops:
  0.0 61.7 %copy-start = (f32[64,128]{1,0:T(8,128)S(1)}, f32[64,128]{1,0:T(8,128)}, u32[]{:S(2)}) copy-start(f32[64,128]{1,0:T(8,128)} %param.25) | copy-start | bytes 98308
  0.0 9.2 %copy-start.7 = (bf16[2,64,256]{2,1,0:T(8,128)(2,1)S(1)}, bf16[2,64,256]{2,1,0:T(8,128)(2,1)}, u32[]{:S(2)}) copy-start(bf16[2,64,256]{2,1,0:T(8,128)(2,1)} %param.15) | copy-start | bytes 196612
  1.7 43.3 %all-to-all-start = ((bf16[16,64,256]{2,1,0:T(8,128)(2,1)}), bf16[16,64,256]{2,1,0:T(8,128)(2,1)S(1)}, u32[]{:S(2)}, u32[]{:S(2)}) async-start(bf16[16,64,256]{2,1,0:T(8,128)(2,1)} %broadcast_in_dim.2), calls=%async_computation | async-start | bytes 1048576 | tf_op jit(solution)/shard_map/all_to_all | solution.py:351
  33.8 11.1 %copy-start.3 = (bf16[8,64,256]{2,1,0:T(8,128)(2,1)}, bf16[8,64,256]{2,1,0:T(8,128)(2,1)S(1)}, u32[]{:S(2)}) copy-start(bf16[8,64,256]{2,1,0:T(8,128)(2,1)S(1)} %all-gather) | copy-start | bytes 786436
  33.8 7.5 %collective-permute-start = (bf16[4,2,16,256]{3,2,1,0:T(8,128)(2,1)S(1)}, bf16[4,2,16,256]{3,2,1,0:T(8,128)(2,1)S(1)}, u32[]{:S(2)}, u32[]{:S(2)}) collective-permute-start(bf16[4,2,16,256]{3,2,1,0:T(8,128)(2,1)S(1)} %get-tuple-element.28), channel_id=1, source_target_pairs={{0,1},{1,2},{2,3},{3,4},{4,5},{5,6},{6,7},{8,9},{9,10},{10,11},{11... | collective-permute-start | bytes 196616 | tf_op jit(solution)/shard_map/ppermute | solution.py:356
  39.4 5.6 %collective-permute-start.1 = (bf16[4,2,16,256]{3,2,1,0:T(8,128)(2,1)S(1)}, bf16[4,2,16,256]{3,2,1,0:T(8,128)(2,1)S(1)}, u32[]{:S(2)}, u32[]{:S(2)}) collective-permute-start(bf16[4,2,16,256]{3,2,1,0:T(8,128)(2,1)S(1)} %get-tuple-element.27), channel_id=1, source_target_pairs={{1,0},{2,1},{3,2},{4,3},{5,4},{6,5},{7,6},{9,8},{10,9},{11,10},{12... | collective-permute-start | bytes 196616 | tf_op jit(solution)/shard_map/ppermute | solution.py:357
  41.3 3.7 %copy-start.8 = (bf16[4,2,16,256]{3,2,1,0:T(8,128)(2,1)}, bf16[4,2,16,256]{3,2,1,0:T(8,128)(2,1)S(1)}, u32[]{:S(2)}) copy-start(bf16[4,2,16,256]{3,2,1,0:T(8,128)(2,1)S(1)} %collective-permute-done.left_ref) | copy-start | bytes 196612
  44.9 0.6 copy-start.9
  45.5 0.8 copy-start.2
  49.3 6.8 %copy-start.15 = (f32[16]{0:T(128)S(1)}, f32[16]{0:T(128)}, u32[]{:S(2)}) copy-start(f32[16]{0:T(128)} %param.18) | copy-start | bytes 196
  49.3 7.5 %copy-start.16 = (f32[32]{0:T(128)S(1)}, f32[32]{0:T(128)}, u32[]{:S(2)}) copy-start(f32[32]{0:T(128)} %param.20) | copy-start | bytes 388
  49.3 8.2 %copy-start.17 = (f32[64]{0:T(128)S(1)}, f32[64]{0:T(128)}, u32[]{:S(2)}) copy-start(f32[64]{0:T(128)} %param.22) | copy-start | bytes 772
  49.3 8.8 %copy-start.13 = (bf16[6,6,1,16]{3,1,2,0:T(8,128)(2,1)S(1)}, bf16[6,6,1,16]{3,1,2,0:T(8,128)(2,1)}, u32[]{:S(2)}) copy-start(bf16[6,6,1,16]{3,1,2,0:T(8,128)(2,1)} %param.17) | copy-start | bytes 3460
  49.3 9.9 %copy-start.6 = (bf16[6,6,16,32]{3,2,1,0:T(8,128)(2,1)S(1)}, bf16[6,6,16,32]{3,2,1,0:T(8,128)(2,1)}, u32[]{:S(2)}) copy-start(bf16[6,6,16,32]{3,2,1,0:T(8,128)(2,1)} %param.19) | copy-start | bytes 110596
  49.3 29.2 %all-to-all-start.1 = ((bf16[16,64,768]{2,1,0:T(8,128)(2,1)}), bf16[16,64,768]{2,1,0:T(8,128)(2,1)S(1)}, u32[]{:S(2)}, u32[]{:S(2)}) async-start(bf16[16,64,768]{2,1,0:T(8,128)(2,1)} %cost_maps.1), calls=%async_computation.1 | async-start | bytes 3145728 | tf_op jit(solution)/shard_map/all_to_all | solution.py:362
  56.2 4.2 %copy-start.5 = (bf16[6,6,32,64]{3,2,1,0:T(8,128)(2,1)S(1)}, bf16[6,6,32,64]{3,2,1,0:T(8,128)(2,1)}, u32[]{:S(2)}) copy-start(bf16[6,6,32,64]{3,2,1,0:T(8,128)(2,1)} %param.21) | copy-start | bytes 442372
  60.5 1.2 copy-start.12
  60.5 1.4 %copy-start.14 = (bf16[8,16]{0,1:T(8,128)(2,1)S(1)}, bf16[8,16]{0,1:T(8,128)(2,1)}, u32[]{:S(2)}) copy-start(bf16[8,16]{0,1:T(8,128)(2,1)} %constant.10) | copy-start | bytes 772
  60.6 2.4 %copy-start.10 = (f32[16,8,128]{2,1,0:T(8,128)S(1)}, f32[16,8,128]{2,1,0:T(8,128)}, u32[]{:S(2)}) copy-start(f32[16,8,128]{2,1,0:T(8,128)} %param.24) | copy-start | bytes 196612
  78.5 1.2 copy-start.1
  79.7 45.0 %copy-start.11 = (f32[64,128]{1,0:T(8,128)S(1)}, f32[64,128]{1,0:T(8,128)}, u32[]{:S(2)}) copy-start(f32[64,128]{1,0:T(8,128)} %param.26) | copy-start | bytes 98308
  120.1 10.4 %all-to-all-start.3 = ((f32[8,8,512]{2,1,0:T(8,128)}), f32[8,8,512]{2,1,0:T(8,128)S(1)}, u32[]{:S(2)}, u32[]{:S(2)}) async-start(f32[8,8,512]{2,1,0:T(8,128)} %combine.1), calls=%async_computation.3 | async-start | bytes 262144 | tf_op jit(solution)/shard_map/all_to_all | solution.py:366
  130.5 0.6 copy-start.4

commit v4 on v3

--- a/solution.py
+++ b/solution.py
@@ -18,14 +18,26 @@
 WIDE = 96
 PAIRS = 64
 EDGE = 7
-VMEM = 56 * 1024 * 1024
 ROWS_ONE = 38
 ROWS_TWO = 18
 ROWS_THREE = 16
 
 
-def params():
-    return pltpu.CompilerParams(vmem_limit_bytes=VMEM)
+def call(body, out_shape, operands, name, limit, scratch=()):
+    near = pl.BlockSpec(memory_space=pltpu.VMEM)
+    return pl.pallas_call(
+        body,
+        out_shape=out_shape,
+        in_specs=[near] * len(operands),
+        out_specs=jax.tree.map(lambda _: near, out_shape),
+        scratch_shapes=scratch,
+        compiler_params=pltpu.CompilerParams(vmem_limit_bytes=limit * 1024 * 1024),
+        name=name,
+    )(*(pltpu.with_memory_space_constraint(x, pltpu.VMEM) for x in operands))
+
+
+def vmem(shape, dtype):
+    return pltpu.VMEM(shape, dtype)
 
 
 def gelu(x):
@@ -57,12 +69,13 @@
 
 
 def cost_maps(rows, left, right, sources, first, count):
-    return pl.pallas_call(
+    return call(
         functools.partial(cost_body, first=first),
-        out_shape=jax.ShapeDtypeStruct((sources.shape[0], count, 2 * WIDE * rows.shape[0]), bf16),
-        compiler_params=params(),
-        name="cost_maps",
-    )(rows, left, right, sources)
+        vmem((sources.shape[0], count, 2 * WIDE * rows.shape[0]), bf16),
+        (rows, left, right, sources),
+        "cost_maps",
+        16,
+    )
 
 
 def band(kernel_ref, out_ref, step, block):
@@ -104,16 +117,8 @@
     one = jnp.tile(kernel_one.reshape(6, 6, 16), (1, 1, 48))
     two = jnp.tile(kernel_two.reshape(6, 96, 32), (1, 1, 8))
     three = jnp.tile(kernel_three.reshape(6, 192, 64), (1, 1, 4))
-    return pl.pallas_call(
-        band_body,
-        out_shape=(
-            jax.ShapeDtypeStruct((768, 768), bf16),
-            jax.ShapeDtypeStruct((2304, 256), bf16),
-            jax.ShapeDtypeStruct((2304, 256), bf16),
-        ),
-        compiler_params=params(),
-        name="bands",
-    )(one, two, three)
+    shapes = (vmem((768, 768), bf16), vmem((2304, 256), bf16), vmem((2304, 256), bf16))
+    return call(band_body, shapes, (one, two, three), "bands", 16)
 
 
 def encode_body(
@@ -249,19 +254,14 @@
 
     if before is not None:
         body, operands = (encode_body, operands + (before,))
-    return pl.pallas_call(
-        body,
-        out_shape=jax.ShapeDtypeStruct((whole, 640), f32),
-        scratch_shapes=[
-            pltpu.VMEM((pl.cdiv(76, ROWS_ONE) * ROWS_ONE + 2, count, 256), bf16),
-            pltpu.VMEM((pl.cdiv(76, ROWS_ONE) * (ROWS_ONE // 2), 2, count, 768), bf16),
-            pltpu.VMEM((18, 2, count, 640), bf16),
-            pltpu.VMEM((16, count, 512), bf16),
-            pltpu.VMEM((16, count, 128), f32),
-        ],
-        compiler_params=params(),
-        name="encode",
-    )(*operands)
+    scratch = [
+        vmem((pl.cdiv(76, ROWS_ONE) * ROWS_ONE + 2, count, 256), bf16),
+        vmem((pl.cdiv(76, ROWS_ONE) * (ROWS_ONE // 2), 2, count, 768), bf16),
+        vmem((18, 2, count, 640), bf16),
+        vmem((16, count, 512), bf16),
+        vmem((16, count, 128), f32),
+    ]
+    return call(body, vmem((whole, 640), f32), operands, "encode", 40, scratch)
 
 
 def combine_body(parts_ref, spread_ref, out_ref):
@@ -282,12 +282,9 @@
 
 
 def combine(parts, spread):
-    return pl.pallas_call(
-        combine_body,
-        out_shape=jax.ShapeDtypeStruct(parts.shape[:2] + (512,), f32),
-        compiler_params=params(),
-        name="combine",
-    )(parts, spread)
+    return call(
+        combine_body, vmem(parts.shape[:2] + (512,), f32), (parts, spread), "combine", 8
+    )
 
 
 def value_body(attended_ref, value_ref, out_ref):
@@ -301,12 +298,8 @@
 
 
 def valued(attended, value_weight):
-    return pl.pallas_call(
-        value_body,
-        out_shape=jax.ShapeDtypeStruct((attended.shape[0], 8, 128), f32),
-        compiler_params=params(),
-        name="valued",
-    )(attended, value_weight)
+    shape = jax.ShapeDtypeStruct((attended.shape[0], 8, 128), f32)
+    return call(value_body, shape, (attended, value_weight), "valued", 8)
 
 
 def prepare(

time: 134 us -> 128 us (0.955)
  Pallas kernels: 38.2 us -> 29.1 us
  waiting for transfers between devices: 19.4 us -> 22 us
  local copies, waits for them, and re-layouts: 11.4 us -> 13.1 us
    pallas_call x5, Pallas kernels: 38.2 us -> 29.1 us  [call(): pl.pallas_call(body, out_shape=out_shape, in_specs=[near] * len(operands)...]
    unnamed x36 -> x40, local copies, waits for them, and re-layouts: 3.27 us -> 8.03 us
    all_to_all x1, waiting for transfers between devices: 10.5 us -> 12.5 us  [on_device(): parts = encode(lax.all_to_all(cost, 'xy', 0, 0), *prepared)]
  transfers between devices with their start and end apart: 5 -> 5, of which waited for: 3 -> 3; matrix products, arithmetic and copies ran while one was open for 6% -> 3% of each run, Pallas kernels for 3% -> 1%
where the time goes in v4:
time: 128 us; the launch traced here: 127 us
  blocking collectives  35.4 us (28%)
  Pallas kernels  29.1 us (23%)
  starting transfers between devices  26.3 us (21%)
  waiting for transfers between devices  22 us (17%)
  local copies, waits for them, and re-layouts  13.1 us (10%)
    pallas_call x5, Pallas kernels, call(): pl.pallas_call(body, out_shape=out_shape, in_specs=[near] * len(operands)...  29.1 us
    all_gather x1, blocking collectives, on_device(): rows = lax.all_gather(target, 'zh', axis=0)  24.5 us
    all_to_all x1, waiting for transfers between devices, on_device(): parts = encode(lax.all_to_all(cost, 'xy', 0, 0), *prepared)  12.5 us
    all_to_all x1, blocking collectives, on_device(): lax.all_to_all(parts.reshape(tiles, -1, parts.shape[1]), 'tile', 0, 0)  10.9 us
    unnamed x40, local copies, waits for them, and re-layouts  8.03 us
    all_to_all x1, starting transfers between devices, on_device(): every = lax.all_to_all(copies, 'xy', 0, 0)  7.58 us
    all_to_all x1, starting transfers between devices, on_device(): parts = encode(lax.all_to_all(cost, 'xy', 0, 0), *prepared)  6.79 us
    all_to_all x1, waiting for transfers between devices, on_device(): attended = lax.all_to_all(combine(parts, spread), 'tile', 0, 0)  5.83 us
  transfers between devices with their start and end apart: 5, of which 3 were waited for; matrix products, arithmetic and copies ran while one was open for 3% of the time, Pallas kernels for 1%

profile of v4, /device:TPU:1, one launch (start us, length us, event | category | flops | bytes accessed | tf_op | source)
XLA Modules:
  0.0 127.0 jit_solution(17757333992996615978)
XLA Ops:
  0.0 1.6 %broadcast_in_dim.2 = bf16[16,64,256]{2,1,0:T(8,128)(2,1)} broadcast(bf16[64,256]{1,0:T(8,128)(2,1)} %param.16), dimensions={1,2} | broadcast | bytes 557056 | tf_op jit(solution)/shard_map/broadcast_in_dim | solution.py:342
  1.7 7.6 %all-to-all-start = ((bf16[16,64,256]{2,1,0:T(8,128)(2,1)}), bf16[16,64,256]{2,1,0:T(8,128)(2,1)S(1)}, u32[]{:S(2)}, u32[]{:S(2)}) async-start(bf16[16,64,256]{2,1,0:T(8,128)(2,1)} %broadcast_in_dim.2), calls=%async_computation | async-start | bytes 1048576 | tf_op jit(solution)/shard_map/all_to_all | solution.py:344
  9.3 24.5 %all-gather = bf16[8,64,256]{2,1,0:T(8,128)(2,1)S(1)} all-gather(bf16[2,64,256]{2,1,0:T(8,128)(2,1)S(1)} %copy-done.11), channel_id=2, replica_groups=mesh['zh'=4,'xy'=16,'tile'=8] {'zh'}, dimensions={0}, use_global_device_ids=true | all-gather | bytes 327680 | tf_op jit(solution)/shard_map/all_gather | solution.py:345
  33.8 5.5 %collective-permute-start = (bf16[4,2,16,256]{3,2,1,0:T(8,128)(2,1)S(1)}, bf16[4,2,16,256]{3,2,1,0:T(8,128)(2,1)S(1)}, u32[]{:S(2)}, u32[]{:S(2)}) collective-permute-start(bf16[4,2,16,256]{3,2,1,0:T(8,128)(2,1)S(1)} %get-tuple-element.28), channel_id=1, source_target_pairs={{0,1},{1,2},{2,3},{3,4},{4,5},{5,6},{6,7},{8,9},{9,10},{10,11},{11... | collective-permute-start | bytes 196616 | tf_op jit(solution)/shard_map/ppermute | solution.py:349
  39.3 1.9 %collective-permute-start.1 = (bf16[4,2,16,256]{3,2,1,0:T(8,128)(2,1)S(1)}, bf16[4,2,16,256]{3,2,1,0:T(8,128)(2,1)S(1)}, u32[]{:S(2)}, u32[]{:S(2)}) collective-permute-start(bf16[4,2,16,256]{3,2,1,0:T(8,128)(2,1)S(1)} %get-tuple-element.27), channel_id=1, source_target_pairs={{1,0},{2,1},{3,2},{4,3},{5,4},{6,5},{7,6},{9,8},{10,9},{11,10},{12... | collective-permute-start | bytes 196616 | tf_op jit(solution)/shard_map/ppermute | solution.py:350
  41.3 0.0 collective-permute-done.left_ref
  41.3 3.6 %collective-permute-done.1.right_ref = bf16[4,2,16,256]{3,2,1,0:T(8,128)(2,1)S(1)} collective-permute-done((bf16[4,2,16,256]{3,2,1,0:T(8,128)(2,1)S(1)}, bf16[4,2,16,256]{3,2,1,0:T(8,128)(2,1)S(1)}, u32[]{:S(2)}, u32[]{:S(2)}) %collective-permute-start.1) | collective-permute-done | bytes 65568 | tf_op jit(solution)/shard_map/ppermute | solution.py:350
  44.9 1.8 %cost_maps.1 = bf16[16,64,768]{2,1,0:T(8,128)(2,1)} custom-call(bf16[4,2,64,256]{3,2,1,0:T(8,128)(2,1)S(1)} %bitcast.24, bf16[4,2,16,256]{3,2,1,0:T(8,128)(2,1)S(1)} %collective-permute-done.left_ref, bf16[4,2,16,256]{3,2,1,0:T(8,128)(2,1)S(1)} %collective-permute-done.1.right_ref, bf16[16,64,256]{2,1,0:T(8,128)(2,1)S(1)} %all-to-all-done.sources_ref), custom_call_target="tpu_custom_call" | custom-call | tf_op jit(solution)/shard_map/cost_maps/pallas_call | solution.py:28
  46.8 0.0 copy-start.10
  46.8 6.8 %all-to-all-start.1 = ((bf16[16,64,768]{2,1,0:T(8,128)(2,1)}), bf16[16,64,768]{2,1,0:T(8,128)(2,1)S(1)}, u32[]{:S(2)}, u32[]{:S(2)}) async-start(bf16[16,64,768]{2,1,0:T(8,128)(2,1)} %cost_maps.1), calls=%async_computation.1 | async-start | bytes 3145728 | tf_op jit(solution)/shard_map/all_to_all | solution.py:355
  53.6 0.0 copy-start.9
  53.6 0.1 broadcast_in_dim_tile.9.refs_4_
  53.7 0.1 broadcast_in_dim_tile.10.refs_5_
  53.8 0.1 broadcast_in_dim_tile.11.refs_6_
  53.9 0.1 tile.49
  53.9 1.1 tile.50.one_ref
  55.0 0.1 copy.25
  55.1 0.1 tile.52
  55.2 0.9 copy.27.two_ref
  56.1 0.2 copy.26
  56.3 0.0 copy-start.14
  56.3 0.0 copy-start.16
  56.3 0.1 tile.55
  56.4 0.0 copy-start.12
  56.4 0.3 copy.28.three_ref
  56.7 0.3 copy-done.14
  57.0 0.1 fusion
  57.1 0.1 broadcast_multiply_fusion
  57.2 0.2 mul.23
  57.4 0.1 copy.32.refs_7_
  57.6 0.6 convolution_bitcast_fusion
  58.1 0.1 copy.30
  58.2 1.0 copy-done.5
  59.2 0.9 copy-done.7
  60.1 1.2 bands.1
  61.3 1.0 copy-done.1
  62.3 1.0 copy-done.3
  63.4 0.1 pad_maximum_fusion.1.refs_8_
  63.4 12.5 %all-to-all-done.1.refs_0_ = bf16[16,64,768]{2,1,0:T(8,128)(2,1)S(1)} async-done(((bf16[16,64,768]{2,1,0:T(8,128)(2,1)}), bf16[16,64,768]{2,1,0:T(8,128)(2,1)S(1)}, u32[]{:S(2)}, u32[]{:S(2)}) %all-to-all-start.1) | async-done | bytes 1572896 | tf_op jit(solution)/shard_map/all_to_all | solution.py:355
  75.9 1.3 copy-done.2
  77.2 1.3 copy-done.4
  78.5 1.2 copy-done.6
  79.7 23.8 %encode.1 = f32[64,640]{1,0:T(8,128)S(1)} custom-call(bf16[16,64,768]{2,1,0:T(8,128)(2,1)S(1)} %all-to-all-done.1.refs_0_, bf16[768,768]{1,0:T(8,128)(2,1)S(1)} %get-tuple-element.22.refs_1_, bf16[2304,256]{1,0:T(8,128)(2,1)S(1)} %copy-done.2, bf16[2304,256]{1,0:T(8,128)(2,1)S(1)} %copy-done.4, f32[1,768]{1,0:T(1,128)S(1)} %broadcast_in_dim_tile.9.refs_4_, ...), custom_call_target="tpu_custom_call" | custom-call | tf_op jit(solution)/shard_map/encode/pallas_call | solution.py:28
  103.5 10.9 %all_to_all.20.parts_ref = f32[8,8,640]{2,1,0:T(8,128)S(1)} all-to-all(f32[8,8,640]{2,1,0:T(8,128)S(1)} %bitcast.25), channel_id=1, replica_groups=mesh['zh'=4,'xy'=16,'tile'=8] {'tile'}, dimensions={0} | all-to-all | bytes 327680 | tf_op jit(solution)/shard_map/all_to_all | solution.py:356
  114.3 1.0 combine.1
  115.3 4.5 %all-to-all-start.3 = ((f32[8,8,512]{2,1,0:T(8,128)}), f32[8,8,512]{2,1,0:T(8,128)S(1)}, u32[]{:S(2)}, u32[]{:S(2)}) async-start(f32[8,8,512]{2,1,0:T(8,128)} %combine.1), calls=%async_computation.3 | async-start | bytes 262144 | tf_op jit(solution)/shard_map/all_to_all | solution.py:359
  119.8 5.8 %all-to-all-done.3 = f32[8,8,512]{2,1,0:T(8,128)S(1)} async-done(((f32[8,8,512]{2,1,0:T(8,128)}), f32[8,8,512]{2,1,0:T(8,128)S(1)}, u32[]{:S(2)}, u32[]{:S(2)}) %all-to-all-start.3) | async-done | bytes 131104 | tf_op jit(solution)/shard_map/all_to_all | solution.py:359
  125.7 1.3 %valued.1 = f32[64,8,128]{2,1,0:T(8,128)} custom-call(f32[64,512]{1,0:T(8,128)S(1)} %bitcast.26, f32[128,128]{1,0:T(8,128)S(1)} %pad_maximum_fusion.value_ref), custom_call_target="tpu_custom_call" | custom-call | tf_op jit(solution)/shard_map/valued/pallas_call | solution.py:28
  (33 shorter events, 0.1 us)
Async XLA Ops:
  0.0 56.7 %copy-start = (f32[64,128]{1,0:T(8,128)S(1)}, f32[64,128]{1,0:T(8,128)}, u32[]{:S(2)}) copy-start(f32[64,128]{1,0:T(8,128)} %param.25) | copy-start | bytes 98308
  0.0 9.2 %copy-start.11 = (bf16[2,64,256]{2,1,0:T(8,128)(2,1)S(1)}, bf16[2,64,256]{2,1,0:T(8,128)(2,1)}, u32[]{:S(2)}) copy-start(bf16[2,64,256]{2,1,0:T(8,128)(2,1)} %param.15) | copy-start | bytes 196612
  1.7 43.3 %all-to-all-start = ((bf16[16,64,256]{2,1,0:T(8,128)(2,1)}), bf16[16,64,256]{2,1,0:T(8,128)(2,1)S(1)}, u32[]{:S(2)}, u32[]{:S(2)}) async-start(bf16[16,64,256]{2,1,0:T(8,128)(2,1)} %broadcast_in_dim.2), calls=%async_computation | async-start | bytes 1048576 | tf_op jit(solution)/shard_map/all_to_all | solution.py:344
  33.8 7.5 %collective-permute-start = (bf16[4,2,16,256]{3,2,1,0:T(8,128)(2,1)S(1)}, bf16[4,2,16,256]{3,2,1,0:T(8,128)(2,1)S(1)}, u32[]{:S(2)}, u32[]{:S(2)}) collective-permute-start(bf16[4,2,16,256]{3,2,1,0:T(8,128)(2,1)S(1)} %get-tuple-element.28), channel_id=1, source_target_pairs={{0,1},{1,2},{2,3},{3,4},{4,5},{5,6},{6,7},{8,9},{9,10},{10,11},{11... | collective-permute-start | bytes 196616 | tf_op jit(solution)/shard_map/ppermute | solution.py:349
  39.3 5.6 %collective-permute-start.1 = (bf16[4,2,16,256]{3,2,1,0:T(8,128)(2,1)S(1)}, bf16[4,2,16,256]{3,2,1,0:T(8,128)(2,1)S(1)}, u32[]{:S(2)}, u32[]{:S(2)}) collective-permute-start(bf16[4,2,16,256]{3,2,1,0:T(8,128)(2,1)S(1)} %get-tuple-element.27), channel_id=1, source_target_pairs={{1,0},{2,1},{3,2},{4,3},{5,4},{6,5},{7,6},{9,8},{10,9},{11,10},{12... | collective-permute-start | bytes 196616 | tf_op jit(solution)/shard_map/ppermute | solution.py:350
  46.7 6.8 %copy-start.17 = (f32[16]{0:T(128)S(1)}, f32[16]{0:T(128)}, u32[]{:S(2)}) copy-start(f32[16]{0:T(128)} %param.18) | copy-start | bytes 196
  46.7 6.9 %copy-start.18 = (f32[32]{0:T(128)S(1)}, f32[32]{0:T(128)}, u32[]{:S(2)}) copy-start(f32[32]{0:T(128)} %param.20) | copy-start | bytes 388
  46.7 7.0 %copy-start.19 = (f32[64]{0:T(128)S(1)}, f32[64]{0:T(128)}, u32[]{:S(2)}) copy-start(f32[64]{0:T(128)} %param.22) | copy-start | bytes 772
  46.7 7.1 %copy-start.15 = (bf16[6,6,1,16]{3,1,2,0:T(8,128)(2,1)S(1)}, bf16[6,6,1,16]{3,1,2,0:T(8,128)(2,1)}, u32[]{:S(2)}) copy-start(bf16[6,6,1,16]{3,1,2,0:T(8,128)(2,1)} %param.17) | copy-start | bytes 3460
  46.8 8.2 %copy-start.10 = (bf16[6,6,16,32]{3,2,1,0:T(8,128)(2,1)S(1)}, bf16[6,6,16,32]{3,2,1,0:T(8,128)(2,1)}, u32[]{:S(2)}) copy-start(bf16[6,6,16,32]{3,2,1,0:T(8,128)(2,1)} %param.19) | copy-start | bytes 110596
  46.8 29.2 %all-to-all-start.1 = ((bf16[16,64,768]{2,1,0:T(8,128)(2,1)}), bf16[16,64,768]{2,1,0:T(8,128)(2,1)S(1)}, u32[]{:S(2)}, u32[]{:S(2)}) async-start(bf16[16,64,768]{2,1,0:T(8,128)(2,1)} %cost_maps.1), calls=%async_computation.1 | async-start | bytes 3145728 | tf_op jit(solution)/shard_map/all_to_all | solution.py:355
  53.6 2.5 %copy-start.9 = (bf16[6,6,32,64]{3,2,1,0:T(8,128)(2,1)S(1)}, bf16[6,6,32,64]{3,2,1,0:T(8,128)(2,1)}, u32[]{:S(2)}) copy-start(bf16[6,6,32,64]{3,2,1,0:T(8,128)(2,1)} %param.21) | copy-start | bytes 442372
  56.3 0.7 copy-start.14
  56.3 0.8 copy-start.16
  56.4 1.2 copy-start.12
  58.2 1.0 copy-start.5
  59.2 0.9 copy-start.7
  61.3 1.0 copy-start.1
  62.3 1.0 copy-start.3
  75.9 1.3 %copy-start.2 = (bf16[2304,256]{1,0:T(8,128)(2,1)S(1)}, bf16[2304,256]{1,0:T(8,128)(2,1)}, u32[]{:S(2)}) copy-start(bf16[2304,256]{1,0:T(8,128)(2,1)} %copy-done.1) | copy-start | bytes 3538948
  77.2 1.3 %copy-start.4 = (bf16[2304,256]{1,0:T(8,128)(2,1)S(1)}, bf16[2304,256]{1,0:T(8,128)(2,1)}, u32[]{:S(2)}) copy-start(bf16[2304,256]{1,0:T(8,128)(2,1)} %copy-done.3) | copy-start | bytes 3538948
  78.5 1.2 copy-start.6
  79.7 34.6 %copy-start.8 = (f32[128,512]{1,0:T(8,128)S(1)}, f32[128,512]{1,0:T(8,128)}, u32[]{:S(2)}) copy-start(f32[128,512]{1,0:T(8,128)} %constant.8.clone.spread_ref) | copy-start | bytes 786436
  79.7 40.1 %copy-start.13 = (f32[64,128]{1,0:T(8,128)S(1)}, f32[64,128]{1,0:T(8,128)}, u32[]{:S(2)}) copy-start(f32[64,128]{1,0:T(8,128)} %param.26) | copy-start | bytes 98308
  115.3 10.4 %all-to-all-start.3 = ((f32[8,8,512]{2,1,0:T(8,128)}), f32[8,8,512]{2,1,0:T(8,128)S(1)}, u32[]{:S(2)}, u32[]{:S(2)}) async-start(f32[8,8,512]{2,1,0:T(8,128)} %combine.1), calls=%async_computation.3 | async-start | bytes 262144 | tf_op jit(solution)/shard_map/all_to_all | solution.py:359

commit v5 on v4

--- a/solution.py
+++ b/solution.py
@@ -15,7 +15,7 @@
 
 GROUP = 16
 HALO = 16
-WIDE = 96
+OWN = 512
 PAIRS = 64
 EDGE = 7
 ROWS_ONE = 38
@@ -54,28 +54,35 @@
     return jnp.dot(a, b, preferred_element_type=f32)
 
 
-def cost_body(rows_ref, left_ref, right_ref, sources_ref, out_ref, *, first):
+def cost_of(sources_ref, window, out_ref, start):
+    groups, count, depth = sources_ref.shape
+    every = sources_ref[...].reshape(groups * count, depth)
+    for n in range(0, window.shape[0], 256):
+        value = nt_dot(every, window[n : n + 256]) * (1.0 / math.sqrt(depth))
+        out_ref[:, :, start + n : start + n + 256] = value.astype(bf16).reshape(groups, count, 256)
+
+
+def own_body(rows_ref, sources_ref, out_ref):
     parts = []
     for z in range(rows_ref.shape[0]):
+        for half in (slice(0, 32), slice(32, 64)):
+            parts += [rows_ref[z, 0, half], rows_ref[z, 1, half]]
+    cost_of(sources_ref, jnp.concatenate(parts, axis=0), out_ref, 0)
+
+
+def halo_body(left_ref, right_ref, sources_ref, own_ref, out_ref):
+    out_ref[:, :, :OWN] = own_ref[...]
+    parts = []
+    for z in range(left_ref.shape[0]):
         for r in range(2):
-            parts += [left_ref[z, r], rows_ref[z, r], right_ref[z, r]]
-    window = jnp.concatenate(parts, axis=0)
-    groups, count, width = out_ref.shape
-    depth = sources_ref.shape[-1]
-    mine = sources_ref[:, first : first + count].reshape(groups * count, depth)
-    for n in range(0, width, 256):
-        value = nt_dot(mine, window[n : n + 256]) * (1.0 / math.sqrt(depth))
-        out_ref[:, :, n : n + 256] = value.astype(bf16).reshape(groups, count, 256)
-
-
-def cost_maps(rows, left, right, sources, first, count):
-    return call(
-        functools.partial(cost_body, first=first),
-        vmem((sources.shape[0], count, 2 * WIDE * rows.shape[0]), bf16),
-        (rows, left, right, sources),
-        "cost_maps",
-        16,
-    )
+            parts += [left_ref[z, r], right_ref[z, r]]
+    cost_of(sources_ref, jnp.concatenate(parts, axis=0), out_ref, OWN)
+
+
+def cost_maps(rows, left, right, sources):
+    own = call(own_body, vmem(sources.shape[:2] + (OWN,), bf16), (rows, sources), "own_columns", 16)
+    shape = vmem(sources.shape[:2] + (OWN + OWN // 2,), bf16)
+    return call(halo_body, shape, (left, right, sources, own), "halo_columns", 16)
 
 
 def band(kernel_ref, out_ref, step, block):
@@ -98,26 +105,35 @@
 
 
 def band_body(one_ref, two_ref, three_ref, out_one, out_two, out_three):
-    lanes = one_ref.shape[-1]
-    row = lax.broadcasted_iota(jnp.int32, (WIDE, lanes), 0)
-    tap = row - 2 - 2 * (lax.broadcasted_iota(jnp.int32, (WIDE, lanes), 1) // 16)
-    for j in range(3):
-        for q in range(2):
-            total = jnp.zeros((WIDE, lanes), f32)
+    row = lax.broadcasted_iota(jnp.int32, (128, 256), 0)
+    place = lax.broadcasted_iota(jnp.int32, (128, 256), 1) // 16
+    odd = (row // 32) % 2 == 1
+    x = row % 32
+    upper = row >= 64
+    halo = jnp.where(x < 16, x - 16, x + 48)
+    columns = (
+        jnp.where(upper, halo, x),
+        jnp.where(upper, x + 32, x),
+        jnp.where(upper, x + 32, halo),
+    )
+    for n in range(3):
+        tap = columns[n] + 14 - 2 * (place + 16 * n)
+        for j in range(3):
+            total = jnp.zeros((128, 256), f32)
             for kw in range(6):
-                line = one_ref[2 * j + q, kw : kw + 1, :].astype(f32)
-                total = jnp.where(tap == kw, line, total)
-            out_one[256 * j + WIDE * q : 256 * j + WIDE * (q + 1), :] = total.astype(bf16)
-        out_one[256 * j + 2 * WIDE : 256 * (j + 1), :] = jnp.zeros((256 - 2 * WIDE, lanes), bf16)
+                first = one_ref[2 * j, kw : kw + 1, :].astype(f32)
+                second = one_ref[2 * j + 1, kw : kw + 1, :].astype(f32)
+                total = jnp.where(tap == kw, jnp.where(odd, second, first), total)
+            out_one[128 * j : 128 * (j + 1), 256 * n : 256 * (n + 1)] = total.astype(bf16)
     band(two_ref, out_two, 32, 32)
     band(three_ref, out_three, 64, 64)
 
 
 def bands(kernel_one, kernel_two, kernel_three):
-    one = jnp.tile(kernel_one.reshape(6, 6, 16), (1, 1, 48))
+    one = jnp.tile(kernel_one.reshape(6, 6, 16), (1, 1, 16))
     two = jnp.tile(kernel_two.reshape(6, 96, 32), (1, 1, 8))
     three = jnp.tile(kernel_three.reshape(6, 192, 64), (1, 1, 4))
-    shapes = (vmem((768, 768), bf16), vmem((2304, 256), bf16), vmem((2304, 256), bf16))
+    shapes = (vmem((384, 768), bf16), vmem((2304, 256), bf16), vmem((2304, 256), bf16))
     return call(band_body, shapes, (one, two, three), "bands", 16)
 
 
@@ -142,17 +158,17 @@
 ):
     count = cost_ref.shape[1]
     done = before_ref.shape[0] if before_ref is not None else 0
-    blank = jnp.zeros((EDGE, count, 256), bf16)
+    blank = jnp.zeros((EDGE, count, 384), bf16)
     pairs[0:EDGE] = blank
     pairs[EDGE + PAIRS : 2 * EDGE + PAIRS] = blank
 
     def place(i, _):
         for z in range(4):
-            start = 384 * (z // 2) + 128 * (z % 2)
-            value = cost_ref[i, :, start : start + 256]
-            if z % 2:
-                value = jnp.concatenate([value[:, 64:], value[:, :64]], axis=1)
-            pairs[EDGE + z * GROUP + i] = value
+            own = cost_ref[i, :, 128 * z : 128 * (z + 1)]
+            halo = cost_ref[i, :, OWN + 64 * z : OWN + 64 * (z + 1)]
+            pairs[EDGE + z * GROUP + i] = jnp.concatenate(
+                [own[:, :64], halo, own, halo, own[:, 64:]], axis=1
+            )
         return 0
 
     lax.fori_loop(0, GROUP, place, 0, unroll=2)
@@ -160,10 +176,12 @@
     def first(i, _):
         step = ROWS_ONE
         h = i * step
-        left = jnp.concatenate(
-            [pairs[pl.ds(h + j, step)].reshape(step * count, 256) for j in range(3)], axis=1
-        )
         for n in range(3):
+            lanes = slice(128 * n, 128 * (n + 1))
+            left = jnp.concatenate(
+                [pairs[pl.ds(h + j, step), :, lanes].reshape(step * count, 128) for j in range(3)],
+                axis=1,
+            )
             lanes = slice(256 * n, 256 * (n + 1))
             value = gelu(mm(left, one_ref[:, lanes]) + bias_one[:, lanes])
             hidden_one[pl.ds(i * (step // 2), step // 2), :, :, lanes] = value.astype(bf16).reshape(
@@ -255,7 +273,7 @@
     if before is not None:
         body, operands = (encode_body, operands + (before,))
     scratch = [
-        vmem((pl.cdiv(76, ROWS_ONE) * ROWS_ONE + 2, count, 256), bf16),
+        vmem((pl.cdiv(76, ROWS_ONE) * ROWS_ONE + 2, count, 384), bf16),
         vmem((pl.cdiv(76, ROWS_ONE) * (ROWS_ONE // 2), 2, count, 768), bf16),
         vmem((18, 2, count, 640), bf16),
         vmem((16, count, 512), bf16),
@@ -288,13 +306,20 @@
 
 
 def value_body(attended_ref, value_ref, out_ref):
-    low = lax.broadcasted_iota(jnp.int32, (attended_ref.shape[0], 128), 1) < 64
+    count = attended_ref.shape[0]
+    low = lax.broadcasted_iota(jnp.int32, (count, 128), 1) < 64
+    parts = []
     for latent in range(8):
         part = attended_ref[:, 128 * (latent // 2) : 128 * (latent // 2 + 1)]
-        part = jnp.where(low == (latent % 2 == 0), part, 0.0)
-        out_ref[:, latent, :] = jnp.dot(
-            part, value_ref[...], precision=exact, preferred_element_type=f32
-        )
+        parts.append(jnp.where(low == (latent % 2 == 0), part, 0.0))
+    value = jnp.dot(
+        jnp.concatenate(parts, axis=0),
+        value_ref[...],
+        precision=exact,
+        preferred_element_type=f32,
+    )
+    for latent in range(8):
+        out_ref[:, latent, :] = value[count * latent : count * (latent + 1)]
 
 
 def valued(attended, value_weight):
@@ -348,16 +373,17 @@
     down = [(j, i) for i, j in up]
     left = lax.ppermute(rows[:, :, width - HALO :], "tile", up)
     right = lax.ppermute(rows[:, :, :HALO], "tile", down)
-    cost = cost_maps(rows, left, right, every, 0, sources.shape[0])
+    cost = cost_maps(rows, left, right, every)
     weights = (kernel_one, kernel_two, kernel_three, latents, pos_key)
-    cost, weights = lax.optimization_barrier((cost, weights))
+    cost, weights, value_weight = lax.optimization_barrier((cost, weights, value_weight))
+    value_weight = jnp.concatenate([value_weight, value_weight], axis=0)
     prepared = prepare(*weights, first_conv_bias, shift_two, shift_three, w_key)
     parts = encode(lax.all_to_all(cost, "xy", 0, 0), *prepared)
+    parts, value_weight = lax.optimization_barrier((parts, value_weight))
     parts = lax.all_to_all(parts.reshape(tiles, -1, parts.shape[1]), "tile", 0, 0)
     latent = np.arange(128)[:, None]
     spread = jnp.asarray((latent == np.arange(512)[None, :] // 64).astype(np.float32))
     attended = lax.all_to_all(combine(parts, spread), "tile", 0, 0)
-    value_weight = jnp.concatenate([value_weight, value_weight], axis=0)
     return valued(attended.reshape(-1, attended.shape[-1]), value_weight)
 
 

time: 128 us -> 125 us (0.977)
  waiting for transfers between devices: 22 us -> 6.43 us
  blocking collectives: 35.4 us -> 45.2 us
  local copies, waits for them, and re-layouts: 13.1 us -> 18.8 us
  starting transfers between devices: 26.3 us -> 21.8 us
  other arithmetic: 0.2 us -> 3.19 us
  Pallas kernels: 29.1 us -> 26.3 us
  matrix products: 0.71 us -> 2.17 us
    all_to_all x0 -> x1, blocking collectives: none -> 9.79 us  [on_device(): attended = lax.all_to_all(combine(parts, spread), 'tile', 0, 0)]
    all_to_all x1, waiting for transfers between devices: 12.5 us -> 3.26 us  [on_device(): parts = encode(lax.all_to_all(cost, 'xy', 0, 0), *prepared)]
    all_to_all x1 -> x0, waiting for transfers between devices: 5.83 us -> none  [on_device(): attended = lax.all_to_all(combine(parts, spread), 'tile', 0, 0)]
    all_to_all x1 -> x0, starting transfers between devices: 4.51 us -> none  [on_device(): attended = lax.all_to_all(combine(parts, spread), 'tile', 0, 0)]
    mul x2, local copies, waits for them, and re-layouts: 0.33 us -> 3.47 us  [prepare(): query = query.T[None, :, None, :] * own[:, None, :, None].astype(bf16)]
    pallas_call x5 -> x6, Pallas kernels: 29.1 us -> 26.3 us  [call(): pl.pallas_call(body, out_shape=out_shape, in_specs=[near] * len(operands)...]
    another operation x3, local copies, waits for them, and re-layouts: 0.51 us -> 2.63 us  [bands(): three = jnp.tile(kernel_three.reshape(6, 192, 64), (1, 1, 4))]
    dot_general x1, matrix products: 0.57 us -> 2.03 us  [prepare(): jnp.einsum('ld,hwd->hwl', latents, pos_key, precision=exact).reshape(16, 64)]
  transfers between devices with their start and end apart: 5 -> 4, of which waited for: 3 -> 2; matrix products, arithmetic and copies ran while one was open for 3% -> 12% of each run, Pallas kernels for 1% -> 1%
where the time goes in v5:
time: 125 us; the launch traced here: 124 us
  blocking collectives  45.2 us (36%)
  Pallas kernels  26.3 us (21%)
  starting transfers between devices  21.8 us (17%)
  local copies, waits for them, and re-layouts  18.8 us (15%)
  waiting for transfers between devices  6.43 us (5%)
  other arithmetic  3.19 us (3%)
  matrix products  2.17 us (2%)
    pallas_call x6, Pallas kernels, call(): pl.pallas_call(body, out_shape=out_shape, in_specs=[near] * len(operands)...  26.3 us
    all_gather x1, blocking collectives, on_device(): rows = lax.all_gather(target, 'zh', axis=0)  24.5 us
    all_to_all x1, blocking collectives, on_device(): lax.all_to_all(parts.reshape(tiles, -1, parts.shape[1]), 'tile', 0, 0)  10.9 us
    all_to_all x1, blocking collectives, on_device(): attended = lax.all_to_all(combine(parts, spread), 'tile', 0, 0)  9.79 us
    unnamed x38, local copies, waits for them, and re-layouts  8.18 us
    all_to_all x1, starting transfers between devices, on_device(): every = lax.all_to_all(copies, 'xy', 0, 0)  7.58 us
    all_to_all x1, starting transfers between devices, on_device(): parts = encode(lax.all_to_all(cost, 'xy', 0, 0), *prepared)  6.81 us
    ppermute x1, starting transfers between devices, on_device(): left = lax.ppermute(rows[:, :, width - HALO:], 'tile', up)  5.53 us
  transfers between devices with their start and end apart: 4, of which 2 were waited for; matrix products, arithmetic and copies ran while one was open for 12% of the time, Pallas kernels for 1%

profile of v5, /device:TPU:1, one launch (start us, length us, event | category | flops | bytes accessed | tf_op | source)
XLA Modules:
  0.0 124.1 jit_solution(1101592253945365460)
XLA Ops:
  0.0 1.6 %broadcast_in_dim.2 = bf16[16,64,256]{2,1,0:T(8,128)(2,1)} broadcast(bf16[64,256]{1,0:T(8,128)(2,1)} %param.16), dimensions={1,2} | broadcast | bytes 557056 | tf_op jit(solution)/shard_map/broadcast_in_dim | solution.py:367
  1.6 7.6 %all-to-all-start = ((bf16[16,64,256]{2,1,0:T(8,128)(2,1)}), bf16[16,64,256]{2,1,0:T(8,128)(2,1)S(1)}, u32[]{:S(2)}, u32[]{:S(2)}) async-start(bf16[16,64,256]{2,1,0:T(8,128)(2,1)} %broadcast_in_dim.2), calls=%async_computation | async-start | bytes 1048576 | tf_op jit(solution)/shard_map/all_to_all | solution.py:369
  9.2 24.5 %all-gather = bf16[8,64,256]{2,1,0:T(8,128)(2,1)S(1)} all-gather(bf16[2,64,256]{2,1,0:T(8,128)(2,1)S(1)} %copy-done.13), channel_id=2, replica_groups=mesh['zh'=4,'xy'=16,'tile'=8] {'zh'}, dimensions={0}, use_global_device_ids=true | all-gather | bytes 327680 | tf_op jit(solution)/shard_map/all_gather | solution.py:370
  33.8 5.5 %collective-permute-start = (bf16[4,2,16,256]{3,2,1,0:T(8,128)(2,1)S(1)}, bf16[4,2,16,256]{3,2,1,0:T(8,128)(2,1)S(1)}, u32[]{:S(2)}, u32[]{:S(2)}) collective-permute-start(bf16[4,2,16,256]{3,2,1,0:T(8,128)(2,1)S(1)} %get-tuple-element.34), channel_id=1, source_target_pairs={{0,1},{1,2},{2,3},{3,4},{4,5},{5,6},{6,7},{8,9},{9,10},{10,11},{11... | collective-permute-start | bytes 196616 | tf_op jit(solution)/shard_map/ppermute | solution.py:374
  39.3 1.9 %collective-permute-start.1 = (bf16[4,2,16,256]{3,2,1,0:T(8,128)(2,1)S(1)}, bf16[4,2,16,256]{3,2,1,0:T(8,128)(2,1)S(1)}, u32[]{:S(2)}, u32[]{:S(2)}) collective-permute-start(bf16[4,2,16,256]{3,2,1,0:T(8,128)(2,1)S(1)} %get-tuple-element.33), channel_id=1, source_target_pairs={{1,0},{2,1},{3,2},{4,3},{5,4},{6,5},{7,6},{9,8},{10,9},{11,10},{12... | collective-permute-start | bytes 196616 | tf_op jit(solution)/shard_map/ppermute | solution.py:375
  41.3 0.0 all-to-all-done.sources_ref
  41.3 0.5 own_columns.1.own_ref
  41.8 0.0 collective-permute-done.left_ref
  41.8 3.2 %collective-permute-done.1.right_ref = bf16[4,2,16,256]{3,2,1,0:T(8,128)(2,1)S(1)} collective-permute-done((bf16[4,2,16,256]{3,2,1,0:T(8,128)(2,1)S(1)}, bf16[4,2,16,256]{3,2,1,0:T(8,128)(2,1)S(1)}, u32[]{:S(2)}, u32[]{:S(2)}) %collective-permute-start.1) | collective-permute-done | bytes 65568 | tf_op jit(solution)/shard_map/ppermute | solution.py:375
  44.9 1.5 %halo_columns.1 = bf16[16,64,768]{2,1,0:T(8,128)(2,1)} custom-call(bf16[4,2,16,256]{3,2,1,0:T(8,128)(2,1)S(1)} %collective-permute-done.left_ref, bf16[4,2,16,256]{3,2,1,0:T(8,128)(2,1)S(1)} %collective-permute-done.1.right_ref, bf16[16,64,256]{2,1,0:T(8,128)(2,1)S(1)} %all-to-all-done.sources_ref, bf16[16,64,512]{2,1,0:T(8,128)(2,1)S(1)} %own_columns.1.own_ref), custom_call_target="tpu_custom_call" | custom-call | tf_op jit(solution)/shard_map/halo_columns/pallas_call | solution.py:28
  46.4 0.0 copy-start.12
  46.5 6.8 %all-to-all-start.1 = ((bf16[16,64,768]{2,1,0:T(8,128)(2,1)}), bf16[16,64,768]{2,1,0:T(8,128)(2,1)S(1)}, u32[]{:S(2)}, u32[]{:S(2)}) async-start(bf16[16,64,768]{2,1,0:T(8,128)(2,1)} %halo_columns.1), calls=%async_computation.1 | async-start | bytes 3145728 | tf_op jit(solution)/shard_map/all_to_all | solution.py:381
  53.3 0.0 copy-start.11
  53.3 0.1 broadcast_in_dim_tile.9.refs_4_
  53.4 0.0 copy-done.17
  53.4 0.1 broadcast_in_dim_tile.10.refs_5_
  53.5 0.1 broadcast_in_dim_tile.11.refs_6_
  53.6 0.8 tile.50.one_ref
  54.4 0.1 copy.25
  54.5 0.1 tile.52
  54.6 0.2 copy.27.two_ref
  54.8 0.0 copy-start.14
  54.8 0.2 copy.26
  55.0 1.0 tile.55
  55.9 1.5 %copy.28.three_ref = bf16[6,192,256]{2,1,0:T(8,128)(2,1)S(1)} copy(bf16[6,192,256]{1,2,0:T(8,128)(2,1)} %bitcast.27) | data formatting | bytes 1179648 | tf_op jit(solution)/shard_map/tile | solution.py:135
  57.4 0.1 fusion
  57.6 1.5 %broadcast_multiply_fusion = bf16[8,64,16,8]{1,0,3,2:T(8,128)(2,1)} fusion(bf16[8,16]{0,1:T(8,128)(2,1)} %constant.10, bf16[64,8]{0,1:T(8,128)(2,1)S(1)} %fusion), kind=kLoop, calls=%fused_computation.3 | loop fusion | flops 65536 | bytes 132352 | tf_op jit(solution)/shard_map/mul | solution.py:336
  59.1 1.8 %mul.23 = bf16[512,128]{0,1:T(8,128)(2,1)} reshape(bf16[8,64,16,8]{1,0,3,2:T(8,128)(2,1)} %broadcast_multiply_fusion) | data formatting | bytes 262144 | tf_op jit(solution)/shard_map/mul | solution.py:336
  60.9 1.7 %copy.32.refs_7_ = bf16[512,128]{1,0:T(8,128)(2,1)} copy(bf16[512,128]{0,1:T(8,128)(2,1)} %mul.23) | data formatting | bytes 262144 | tf_op jit(solution)/shard_map/mul | solution.py:336
  62.6 2.0 %convolution_bitcast_fusion = f32[16,64]{0,1:T(8,128)} fusion(f32[16,8,128]{2,1,0:T(8,128)} %param.24, f32[8,128]{1,0:T(8,128)S(1)} %copy-done.14), kind=kOutput, calls=%fused_computation | convolution fusion | flops 1572864 | bytes 73728 | tf_op jit(solution)/shard_map/ld,hwd->hwl/dot_general | solution.py:338
  64.6 1.4 %copy.30 = f32[16,64]{1,0:T(8,128)} copy(f32[16,64]{0,1:T(8,128)} %convolution_bitcast_fusion) | data formatting | bytes 8192 | tf_op jit(solution)/shard_map/reshape | solution.py:338
  66.0 0.7 copy-done.10
  66.8 1.0 bands.1
  67.8 1.0 copy-done.1
  68.8 1.0 copy-done.3
  69.9 0.8 copy-done.6
  70.7 0.8 pad_maximum_fusion.1.refs_8_
  71.5 0.8 pad_maximum_fusion.value_ref
  72.4 3.3 %all-to-all-done.1.refs_0_ = bf16[16,64,768]{2,1,0:T(8,128)(2,1)S(1)} async-done(((bf16[16,64,768]{2,1,0:T(8,128)(2,1)}), bf16[16,64,768]{2,1,0:T(8,128)(2,1)S(1)}, u32[]{:S(2)}, u32[]{:S(2)}) %all-to-all-start.1) | async-done | bytes 1572896 | tf_op jit(solution)/shard_map/all_to_all | solution.py:381
  75.6 1.3 %copy-done.2 = bf16[2304,256]{1,0:T(8,128)(2,1)S(1)} copy-done((bf16[2304,256]{1,0:T(8,128)(2,1)S(1)}, bf16[2304,256]{1,0:T(8,128)(2,1)}, u32[]{:S(2)}) %copy-start.2) | copy-done | bytes 1179672
  76.9 1.3 %copy-done.4 = bf16[2304,256]{1,0:T(8,128)(2,1)S(1)} copy-done((bf16[2304,256]{1,0:T(8,128)(2,1)S(1)}, bf16[2304,256]{1,0:T(8,128)(2,1)}, u32[]{:S(2)}) %copy-start.4) | copy-done | bytes 1179672
  78.2 1.1 copy-done.7
  79.3 0.9 copy-done.8
  80.2 21.8 %encode.1 = f32[64,640]{1,0:T(8,128)S(1)} custom-call(bf16[16,64,768]{2,1,0:T(8,128)(2,1)S(1)} %all-to-all-done.1.refs_0_, bf16[384,768]{1,0:T(8,128)(2,1)S(1)} %copy-done.7, bf16[2304,256]{1,0:T(8,128)(2,1)S(1)} %copy-done.2, bf16[2304,256]{1,0:T(8,128)(2,1)S(1)} %copy-done.4, f32[1,768]{1,0:T(1,128)S(1)} %broadcast_in_dim_tile.9.refs_4_, ...), custom_call_target="tpu_custom_call" | custom-call | tf_op jit(solution)/shard_map/encode/pallas_call | solution.py:28
  102.0 10.9 %all_to_all.20.parts_ref = f32[8,8,640]{2,1,0:T(8,128)S(1)} all-to-all(f32[8,8,640]{2,1,0:T(8,128)S(1)} %bitcast.25), channel_id=1, replica_groups=mesh['zh'=4,'xy'=16,'tile'=8] {'tile'}, dimensions={0} | all-to-all | bytes 327680 | tf_op jit(solution)/shard_map/all_to_all | solution.py:383
  112.8 0.3 combine.1
  113.2 9.8 %all_to_all.21 = f32[8,8,512]{2,1,0:T(8,128)S(1)} all-to-all(f32[8,8,512]{2,1,0:T(8,128)S(1)} %combine.1), channel_id=1, replica_groups=mesh['zh'=4,'xy'=16,'tile'=8] {'tile'}, dimensions={0} | all-to-all | bytes 262144 | tf_op jit(solution)/shard_map/all_to_all | solution.py:386
  123.0 1.2 valued.1
  (31 shorter events, 0.1 us)
Async XLA Ops:
  0.0 57.4 %copy-start = (f32[64,128]{1,0:T(8,128)S(1)}, f32[64,128]{1,0:T(8,128)}, u32[]{:S(2)}) copy-start(f32[64,128]{1,0:T(8,128)} %param.25) | copy-start | bytes 98308
  0.0 9.2 %copy-start.13 = (bf16[2,64,256]{2,1,0:T(8,128)(2,1)S(1)}, bf16[2,64,256]{2,1,0:T(8,128)(2,1)}, u32[]{:S(2)}) copy-start(bf16[2,64,256]{2,1,0:T(8,128)(2,1)} %param.15) | copy-start | bytes 196612
  1.6 39.6 %all-to-all-start = ((bf16[16,64,256]{2,1,0:T(8,128)(2,1)}), bf16[16,64,256]{2,1,0:T(8,128)(2,1)S(1)}, u32[]{:S(2)}, u32[]{:S(2)}) async-start(bf16[16,64,256]{2,1,0:T(8,128)(2,1)} %broadcast_in_dim.2), calls=%async_computation | async-start | bytes 1048576 | tf_op jit(solution)/shard_map/all_to_all | solution.py:369
  33.8 8.0 %collective-permute-start = (bf16[4,2,16,256]{3,2,1,0:T(8,128)(2,1)S(1)}, bf16[4,2,16,256]{3,2,1,0:T(8,128)(2,1)S(1)}, u32[]{:S(2)}, u32[]{:S(2)}) collective-permute-start(bf16[4,2,16,256]{3,2,1,0:T(8,128)(2,1)S(1)} %get-tuple-element.34), channel_id=1, source_target_pairs={{0,1},{1,2},{2,3},{3,4},{4,5},{5,6},{6,7},{8,9},{9,10},{10,11},{11... | collective-permute-start | bytes 196616 | tf_op jit(solution)/shard_map/ppermute | solution.py:374
  39.3 5.6 %collective-permute-start.1 = (bf16[4,2,16,256]{3,2,1,0:T(8,128)(2,1)S(1)}, bf16[4,2,16,256]{3,2,1,0:T(8,128)(2,1)S(1)}, u32[]{:S(2)}, u32[]{:S(2)}) collective-permute-start(bf16[4,2,16,256]{3,2,1,0:T(8,128)(2,1)S(1)} %get-tuple-element.33), channel_id=1, source_target_pairs={{1,0},{2,1},{3,2},{4,3},{5,4},{6,5},{7,6},{9,8},{10,9},{11,10},{12... | collective-permute-start | bytes 196616 | tf_op jit(solution)/shard_map/ppermute | solution.py:375
  46.4 6.8 %copy-start.16 = (f32[16]{0:T(128)S(1)}, f32[16]{0:T(128)}, u32[]{:S(2)}) copy-start(f32[16]{0:T(128)} %param.18) | copy-start | bytes 196
  46.4 7.0 %copy-start.17 = (f32[32]{0:T(128)S(1)}, f32[32]{0:T(128)}, u32[]{:S(2)}) copy-start(f32[32]{0:T(128)} %param.20) | copy-start | bytes 388
  46.4 7.0 %copy-start.18 = (f32[64]{0:T(128)S(1)}, f32[64]{0:T(128)}, u32[]{:S(2)}) copy-start(f32[64]{0:T(128)} %param.22) | copy-start | bytes 772
  46.4 7.1 %copy-start.15 = (bf16[6,6,1,16]{3,1,2,0:T(8,128)(2,1)S(1)}, bf16[6,6,1,16]{3,1,2,0:T(8,128)(2,1)}, u32[]{:S(2)}) copy-start(bf16[6,6,1,16]{3,1,2,0:T(8,128)(2,1)} %param.17) | copy-start | bytes 3460
  46.4 7.9 %copy-start.12 = (bf16[6,6,16,32]{3,2,1,0:T(8,128)(2,1)S(1)}, bf16[6,6,16,32]{3,2,1,0:T(8,128)(2,1)}, u32[]{:S(2)}) copy-start(bf16[6,6,16,32]{3,2,1,0:T(8,128)(2,1)} %param.19) | copy-start | bytes 110596
  46.5 29.2 %all-to-all-start.1 = ((bf16[16,64,768]{2,1,0:T(8,128)(2,1)}), bf16[16,64,768]{2,1,0:T(8,128)(2,1)S(1)}, u32[]{:S(2)}, u32[]{:S(2)}) async-start(bf16[16,64,768]{2,1,0:T(8,128)(2,1)} %halo_columns.1), calls=%async_computation.1 | async-start | bytes 3145728 | tf_op jit(solution)/shard_map/all_to_all | solution.py:381
  53.3 1.5 %copy-start.11 = (bf16[6,6,32,64]{3,2,1,0:T(8,128)(2,1)S(1)}, bf16[6,6,32,64]{3,2,1,0:T(8,128)(2,1)}, u32[]{:S(2)}) copy-start(bf16[6,6,32,64]{3,2,1,0:T(8,128)(2,1)} %param.21) | copy-start | bytes 442372
  54.8 2.7 %copy-start.14 = (f32[8,128]{1,0:T(8,128)S(1)}, f32[8,128]{1,0:T(8,128)}, u32[]{:S(2)}) copy-start(f32[8,128]{1,0:T(8,128)} %param.23) | copy-start | bytes 12292
  55.9 19.7 %copy-start.5 = (bf16[128,4096]{1,0:T(8,128)(2,1)S(1)}, bf16[128,4096]{1,0:T(8,128)(2,1)}, u32[]{:S(2)}) copy-start(bf16[128,4096]{1,0:T(8,128)(2,1)} %constant.7.clone.refs_9_) | copy-start | bytes 3145732
  66.0 0.7 copy-start.10
  67.8 1.0 copy-start.1
  68.8 1.0 copy-start.3
  69.9 0.8 copy-start.6
  75.6 1.3 %copy-start.2 = (bf16[2304,256]{1,0:T(8,128)(2,1)S(1)}, bf16[2304,256]{1,0:T(8,128)(2,1)}, u32[]{:S(2)}) copy-start(bf16[2304,256]{1,0:T(8,128)(2,1)} %copy-done.1) | copy-start | bytes 3538948
  76.9 1.3 %copy-start.4 = (bf16[2304,256]{1,0:T(8,128)(2,1)S(1)}, bf16[2304,256]{1,0:T(8,128)(2,1)}, u32[]{:S(2)}) copy-start(bf16[2304,256]{1,0:T(8,128)(2,1)} %copy-done.3) | copy-start | bytes 3538948
  78.2 1.1 copy-start.7
  79.2 0.9 copy-start.8
  80.2 32.7 %copy-start.9 = (f32[128,512]{1,0:T(8,128)S(1)}, f32[128,512]{1,0:T(8,128)}, u32[]{:S(2)}) copy-start(f32[128,512]{1,0:T(8,128)} %constant.8.clone.spread_ref) | copy-start | bytes 786436

commit v6 on v5

--- a/solution.py
+++ b/solution.py
@@ -23,17 +23,22 @@
 ROWS_THREE = 16
 
 
-def call(body, out_shape, operands, name, limit, scratch=()):
+def call(body, out_shape, operands, name, limit, scratch=(), far=()):
     near = pl.BlockSpec(memory_space=pltpu.VMEM)
+    hbm = pl.BlockSpec(memory_space=pltpu.HBM)
+    operands = [
+        pltpu.with_memory_space_constraint(x, pltpu.HBM if i in far else pltpu.VMEM)
+        for i, x in enumerate(operands)
+    ]
     return pl.pallas_call(
         body,
         out_shape=out_shape,
-        in_specs=[near] * len(operands),
+        in_specs=[hbm if i in far else near for i in range(len(operands))],
         out_specs=jax.tree.map(lambda _: near, out_shape),
         scratch_shapes=scratch,
         compiler_params=pltpu.CompilerParams(vmem_limit_bytes=limit * 1024 * 1024),
         name=name,
-    )(*(pltpu.with_memory_space_constraint(x, pltpu.VMEM) for x in operands))
+    )(*operands)
 
 
 def vmem(shape, dtype):
@@ -85,13 +90,13 @@
     return call(halo_body, shape, (left, right, sources, own), "halo_columns", 16)
 
 
-def band(kernel_ref, out_ref, step, block):
-    _, depth, lanes = kernel_ref.shape
+def band(taps, out_ref, step, block):
+    depth = taps.shape[0] // 6
     rows = out_ref.shape[0] // 6
-    for t in range(lanes // 128):
+    for t in range(taps.shape[1] // 128):
         lane = lax.broadcasted_iota(jnp.int32, (depth, 128), 1) // block
         for kh in range(6):
-            tile = kernel_ref[kh, :, 128 * t : 128 * (t + 1)].astype(f32)
+            tile = taps[depth * kh : depth * (kh + 1), 128 * t : 128 * (t + 1)]
             total = jnp.zeros((rows, 128), f32)
             for b in range(128 // block):
                 top = step * (b + t * (128 // block))
@@ -104,7 +109,27 @@
             out_ref[kh * rows : (kh + 1) * rows, 128 * t : 128 * (t + 1)] = total.astype(bf16)
 
 
-def band_body(one_ref, two_ref, three_ref, out_one, out_two, out_three):
+def repeated(kernel_ref):
+    width = kernel_ref.shape[1]
+    row = lax.broadcasted_iota(jnp.int32, (width, 256), 0)
+    lane = lax.broadcasted_iota(jnp.int32, (width, 256), 1)
+    pick = jnp.where(lane % width == row, 1.0, 0.0).astype(bf16)
+    return mm(kernel_ref[...], pick)
+
+
+def band_body(
+    one_ref,
+    two_ref,
+    three_ref,
+    latents_ref,
+    key_ref,
+    pos_key_ref,
+    out_one,
+    out_two,
+    out_three,
+    out_query,
+    out_pos,
+):
     row = lax.broadcasted_iota(jnp.int32, (128, 256), 0)
     place = lax.broadcasted_iota(jnp.int32, (128, 256), 1) // 16
     odd = (row // 32) % 2 == 1
@@ -116,48 +141,89 @@
         jnp.where(upper, x + 32, x),
         jnp.where(upper, x + 32, halo),
     )
+    one = repeated(one_ref)
     for n in range(3):
         tap = columns[n] + 14 - 2 * (place + 16 * n)
         for j in range(3):
             total = jnp.zeros((128, 256), f32)
             for kw in range(6):
-                first = one_ref[2 * j, kw : kw + 1, :].astype(f32)
-                second = one_ref[2 * j + 1, kw : kw + 1, :].astype(f32)
+                first = one[12 * j + kw : 12 * j + kw + 1]
+                second = one[12 * j + 6 + kw : 12 * j + 7 + kw]
                 total = jnp.where(tap == kw, jnp.where(odd, second, first), total)
             out_one[128 * j : 128 * (j + 1), 256 * n : 256 * (n + 1)] = total.astype(bf16)
-    band(two_ref, out_two, 32, 32)
-    band(three_ref, out_three, 64, 64)
-
-
-def bands(kernel_one, kernel_two, kernel_three):
-    one = jnp.tile(kernel_one.reshape(6, 6, 16), (1, 1, 16))
-    two = jnp.tile(kernel_two.reshape(6, 96, 32), (1, 1, 8))
-    three = jnp.tile(kernel_three.reshape(6, 192, 64), (1, 1, 4))
-    shapes = (vmem((384, 768), bf16), vmem((2304, 256), bf16), vmem((2304, 256), bf16))
-    return call(band_body, shapes, (one, two, three), "bands", 16)
+    band(repeated(two_ref), out_two, 32, 32)
+    band(repeated(three_ref), out_three, 64, 64)
+
+    def exact_nt(a, b):
+        return lax.dot_general(
+            a, b, (((1,), (1,)), ((), ())), precision=exact, preferred_element_type=f32
+        )
+
+    latents = jnp.concatenate([latents_ref[...]] * 16, axis=0)
+    query = exact_nt(key_ref[...], latents)
+    patch = lax.broadcasted_iota(jnp.int32, (64, 128), 1) // 8 % 8
+    for w in range(8):
+        out_query[64 * w : 64 * (w + 1), :] = jnp.where(patch == w, query, 0.0).astype(bf16)
+    pos = exact_nt(pos_key_ref[...].reshape(128, 128), latents)
+    row = lax.broadcasted_iota(jnp.int32, (128, 128), 0)
+    patch = lax.broadcasted_iota(jnp.int32, (128, 128), 1) // 8
+    pos = jnp.where(patch % 8 == row % 8, pos, 0.0)
+    out_pos[...] = jnp.sum(pos.reshape(16, 8, 128), axis=1)
+
+
+def bands(kernel_one, kernel_two, kernel_three, latents, w_key, pos_key):
+    shapes = (
+        jax.ShapeDtypeStruct((384, 768), bf16),
+        jax.ShapeDtypeStruct((2304, 256), bf16),
+        jax.ShapeDtypeStruct((2304, 256), bf16),
+        jax.ShapeDtypeStruct((512, 128), bf16),
+        jax.ShapeDtypeStruct((16, 128), f32),
+    )
+    kernels = (
+        kernel_one.reshape(36, 16),
+        kernel_two.reshape(6 * 96, 32),
+        kernel_three.reshape(6 * 192, 64),
+    )
+    return call(band_body, shapes, kernels + (latents, w_key, pos_key), "bands", 16)
 
 
 def encode_body(
     cost_ref,
-    one_ref,
-    two_ref,
-    three_ref,
+    one_far,
+    two_far,
+    three_far,
+    query_ref,
+    pos_ref,
     bias_one,
     bias_two,
     bias_three,
-    query_ref,
-    pos_ref,
-    spread_ref,
-    before_ref,
+    spread_far,
     out_ref,
     pairs,
     hidden_one,
     hidden_two,
     features,
     score_ref,
+    one_ref,
+    two_ref,
+    three_ref,
+    spread_ref,
+    arrived,
 ):
     count = cost_ref.shape[1]
-    done = before_ref.shape[0] if before_ref is not None else 0
+    fetches = [
+        pltpu.make_async_copy(far, near, arrived.at[i])
+        for i, (far, near) in enumerate(
+            (
+                (one_far, one_ref),
+                (two_far, two_ref),
+                (three_far, three_ref),
+                (spread_far, spread_ref),
+            )
+        )
+    ]
+    for fetch in fetches:
+        fetch.start()
     blank = jnp.zeros((EDGE, count, 384), bf16)
     pairs[0:EDGE] = blank
     pairs[EDGE + PAIRS : 2 * EDGE + PAIRS] = blank
@@ -189,7 +255,9 @@
             )
         return 0
 
+    fetches[0].wait()
     lax.fori_loop(0, pl.cdiv(76, ROWS_ONE), first, 0)
+    fetches[1].wait()
 
     def taps(source, h, step, lanes):
         parts = [
@@ -228,7 +296,9 @@
             )
         return 0
 
+    fetches[2].wait()
     lax.fori_loop(0, 16 // ROWS_THREE, third, 0)
+    fetches[3].wait()
 
     scale = 1.0 / math.sqrt(128)
 
@@ -256,30 +326,27 @@
         return acc + pltpu.roll(acc, 64, 1)
 
     for k in range(4):
-        out_ref[done:, 128 * k : 128 * (k + 1)] = jnp.where(low, gather(2 * k), gather(2 * k + 1))
-    out_ref[done:, 512:] = jnp.where(low, peak, total)
-    if done:
-        out_ref[:done] = before_ref[...]
-
-
-def encode(cost, banded, biases, query, pos, spread, before=None):
+        out_ref[:, 128 * k : 128 * (k + 1)] = jnp.where(low, gather(2 * k), gather(2 * k + 1))
+    out_ref[:, 512:] = jnp.where(low, peak, total)
+
+
+def encode(cost, prepared, biases, spread):
     count = cost.shape[1]
-    whole = count + (0 if before is None else before.shape[0])
-    operands = (cost, *banded, *biases, query, pos, spread)
-
-    def body(*refs):
-        encode_body(*refs[:10], None, *refs[10:])
-
-    if before is not None:
-        body, operands = (encode_body, operands + (before,))
     scratch = [
         vmem((pl.cdiv(76, ROWS_ONE) * ROWS_ONE + 2, count, 384), bf16),
         vmem((pl.cdiv(76, ROWS_ONE) * (ROWS_ONE // 2), 2, count, 768), bf16),
         vmem((18, 2, count, 640), bf16),
         vmem((16, count, 512), bf16),
         vmem((16, count, 128), f32),
+        vmem((384, 768), bf16),
+        vmem((2304, 256), bf16),
+        vmem((2304, 256), bf16),
+        vmem((128, 4096), bf16),
+        pltpu.SemaphoreType.DMA((4,)),
     ]
-    return call(body, vmem((whole, 640), f32), operands, "encode", 40, scratch)
+    operands = (cost, *prepared, *biases, spread)
+    shape = vmem((count, 640), f32)
+    return call(encode_body, shape, operands, "encode", 40, scratch, far=(1, 2, 3, 9))
 
 
 def combine_body(parts_ref, spread_ref, out_ref):
@@ -330,13 +397,7 @@
 def prepare(
     kernel_one, kernel_two, kernel_three, latents, pos_key, first_conv_bias, shift_two, shift_three, w_key
 ):
-    banded = bands(kernel_one, kernel_two, kernel_three)
-    query = jnp.dot(latents, w_key.T, precision=exact, preferred_element_type=f32).astype(bf16)
-    own = np.arange(8)[:, None] == np.arange(16)[None, :] % 8
-    query = query.T[None, :, None, :] * own[:, None, :, None].astype(bf16)
-    query = query.reshape(512, 128)
-    pos = jnp.einsum("ld,hwd->hwl", latents, pos_key, precision=exact).reshape(16, 64)
-    pos = jnp.concatenate([pos, pos], axis=1)
+    prepared = bands(kernel_one, kernel_two, kernel_three, latents, w_key, pos_key)
     lane = np.arange(128)[:, None] % 64
     column = np.arange(8 * 512)[None, :]
     spread = jnp.asarray((lane == (column % 512) // 64 * 8 + column // 512).astype(bf16))
@@ -345,7 +406,7 @@
         jnp.tile(shift_two, 8)[None],
         jnp.tile(shift_three, 4)[None],
     )
-    return banded, biases, query, pos, spread
+    return prepared, biases, spread
 
 
 def on_device(

time: 125 us -> 121 us (0.968)
  waiting for transfers between devices: 6.43 us -> 21.1 us
  local copies, waits for them, and re-layouts: 18.8 us -> 4.86 us
  other arithmetic: 3.19 us -> 0.01 us
  matrix products: 2.17 us -> 0 us
    all_to_all x1, waiting for transfers between devices: 3.26 us -> 17.9 us  [on_device(): parts = encode(lax.all_to_all(cost, 'xy', 0, 0), *prepared)]
    unnamed x38 -> x30, local copies, waits for them, and re-layouts: 8.18 us -> 2.93 us
    another operation x8 -> x0, local copies, waits for them, and re-layouts: 3.79 us -> none  [the longest x3 2.63 us: bands(): three = jnp.tile(kernel_three.reshape(6, 192, 64), (1, 1, 4))]
    mul x2 -> x0, local copies, waits for them, and re-layouts: 3.47 us -> none  [prepare(): query = query.T[None, :, None, :] * own[:, None, :, None].astype(bf16)]
    dot_general x2 -> x0, matrix products: 2.17 us -> none  [the longest x1 2.03 us: prepare(): jnp.einsum('ld,hwd->hwl', latents, pos_key, precision=exact).reshape(16, 64)]
    mul x1 -> x0, other arithmetic: 1.51 us -> none  [prepare(): query = query.T[None, :, None, :] * own[:, None, :, None].astype(bf16)]
    reshape x1, local copies, waits for them, and re-layouts: 1.43 us -> 0.02 us  [bands(): kernel_one.reshape(36, 16)]
  transfers between devices with their start and end apart: 4 -> 4, of which waited for: 2 -> 2; matrix products, arithmetic and copies ran while one was open for 12% -> 0% of each run, Pallas kernels for 1% -> 1%
where the time goes in v6:
time: 121 us; the launch traced here: 120 us
  blocking collectives  45.2 us (37%)
  Pallas kernels  26.9 us (22%)
  starting transfers between devices  21.8 us (18%)
  waiting for transfers between devices  21.1 us (17%)
  local copies, waits for them, and re-layouts  4.86 us (4%)
    pallas_call x6, Pallas kernels, call(): pl.pallas_call(body, out_shape=out_shape, in_specs=[hbm if i in far else...  26.9 us
    all_gather x1, blocking collectives, on_device(): rows = lax.all_gather(target, 'zh', axis=0)  24.5 us
    all_to_all x1, waiting for transfers between devices, on_device(): parts = encode(lax.all_to_all(cost, 'xy', 0, 0), *prepared)  17.9 us
    all_to_all x1, blocking collectives, on_device(): lax.all_to_all(parts.reshape(tiles, -1, parts.shape[1]), 'tile', 0, 0)  10.9 us
    all_to_all x1, blocking collectives, on_device(): attended = lax.all_to_all(combine(parts, spread), 'tile', 0, 0)  9.79 us
    all_to_all x1, starting transfers between devices, on_device(): every = lax.all_to_all(copies, 'xy', 0, 0)  7.58 us
    all_to_all x1, starting transfers between devices, on_device(): parts = encode(lax.all_to_all(cost, 'xy', 0, 0), *prepared)  6.79 us
    ppermute x1, starting transfers between devices, on_device(): left = lax.ppermute(rows[:, :, width - HALO:], 'tile', up)  5.53 us
  transfers between devices with their start and end apart: 4, of which 2 were waited for; matrix products, arithmetic and copies ran while one was open for 0% of the time, Pallas kernels for 1%

profile of v6, /device:TPU:1, one launch (start us, length us, event | category | flops | bytes accessed | tf_op | source)
XLA Modules:
  0.0 120.1 jit_solution(2288724391628593258)
XLA Ops:
  0.0 0.0 copy-start.9
  0.0 1.6 %broadcast_in_dim.2 = bf16[16,64,256]{2,1,0:T(8,128)(2,1)} broadcast(bf16[64,256]{1,0:T(8,128)(2,1)} %param.15), dimensions={1,2} | broadcast | bytes 557056 | tf_op jit(solution)/shard_map/broadcast_in_dim | solution.py:428
  1.6 7.6 %all-to-all-start = ((bf16[16,64,256]{2,1,0:T(8,128)(2,1)}), bf16[16,64,256]{2,1,0:T(8,128)(2,1)S(1)}, u32[]{:S(2)}, u32[]{:S(2)}) async-start(bf16[16,64,256]{2,1,0:T(8,128)(2,1)} %broadcast_in_dim.2), calls=%async_computation | async-start | bytes 1048576 | tf_op jit(solution)/shard_map/all_to_all | solution.py:430
  9.2 0.0 copy-done.9
  9.3 24.5 %all-gather = bf16[8,64,256]{2,1,0:T(8,128)(2,1)S(1)} all-gather(bf16[2,64,256]{2,1,0:T(8,128)(2,1)S(1)} %copy-done.9), channel_id=2, replica_groups=mesh['zh'=4,'xy'=16,'tile'=8] {'zh'}, dimensions={0}, use_global_device_ids=true | all-gather | bytes 327680 | tf_op jit(solution)/shard_map/all_gather | solution.py:431
  33.8 5.5 %collective-permute-start = (bf16[4,2,16,256]{3,2,1,0:T(8,128)(2,1)S(1)}, bf16[4,2,16,256]{3,2,1,0:T(8,128)(2,1)S(1)}, u32[]{:S(2)}, u32[]{:S(2)}) collective-permute-start(bf16[4,2,16,256]{3,2,1,0:T(8,128)(2,1)S(1)} %get-tuple-element.38), channel_id=1, source_target_pairs={{0,1},{1,2},{2,3},{3,4},{4,5},{5,6},{6,7},{8,9},{9,10},{10,11},{11... | collective-permute-start | bytes 196616 | tf_op jit(solution)/shard_map/ppermute | solution.py:435
  39.3 1.9 %collective-permute-start.1 = (bf16[4,2,16,256]{3,2,1,0:T(8,128)(2,1)S(1)}, bf16[4,2,16,256]{3,2,1,0:T(8,128)(2,1)S(1)}, u32[]{:S(2)}, u32[]{:S(2)}) collective-permute-start(bf16[4,2,16,256]{3,2,1,0:T(8,128)(2,1)S(1)} %get-tuple-element.37), channel_id=1, source_target_pairs={{1,0},{2,1},{3,2},{4,3},{5,4},{6,5},{7,6},{9,8},{10,9},{11,10},{12... | collective-permute-start | bytes 196616 | tf_op jit(solution)/shard_map/ppermute | solution.py:436
  41.3 0.0 all-to-all-done.sources_ref
  41.3 0.5 own_columns.1.own_ref
  41.7 0.0 collective-permute-done.left_ref
  41.8 3.2 %collective-permute-done.1.right_ref = bf16[4,2,16,256]{3,2,1,0:T(8,128)(2,1)S(1)} collective-permute-done((bf16[4,2,16,256]{3,2,1,0:T(8,128)(2,1)S(1)}, bf16[4,2,16,256]{3,2,1,0:T(8,128)(2,1)S(1)}, u32[]{:S(2)}, u32[]{:S(2)}) %collective-permute-start.1) | collective-permute-done | bytes 65568 | tf_op jit(solution)/shard_map/ppermute | solution.py:436
  44.9 1.5 %halo_columns.1 = bf16[16,64,768]{2,1,0:T(8,128)(2,1)} custom-call(bf16[4,2,16,256]{3,2,1,0:T(8,128)(2,1)S(1)} %collective-permute-done.left_ref, bf16[4,2,16,256]{3,2,1,0:T(8,128)(2,1)S(1)} %collective-permute-done.1.right_ref, bf16[16,64,256]{2,1,0:T(8,128)(2,1)S(1)} %all-to-all-done.sources_ref, bf16[16,64,512]{2,1,0:T(8,128)(2,1)S(1)} %own_columns.1.own_ref), custom_call_target="tpu_custom_call" | custom-call | tf_op jit(solution)/shard_map/halo_columns/pallas_call | solution.py:33
  46.4 0.0 copy-start.12
  46.4 0.0 copy-start.13
  46.4 0.0 copy-start.14
  46.4 0.0 copy-start.11
  46.4 0.0 copy-start.3
  46.5 0.0 copy-start.5
  46.5 0.0 copy-start.6
  46.5 0.0 copy-start.7
  46.5 0.0 copy-start.8
  46.5 0.0 copy-start.10
  46.5 6.8 %all-to-all-start.1 = ((bf16[16,64,768]{2,1,0:T(8,128)(2,1)}), bf16[16,64,768]{2,1,0:T(8,128)(2,1)S(1)}, u32[]{:S(2)}, u32[]{:S(2)}) async-start(bf16[16,64,768]{2,1,0:T(8,128)(2,1)} %halo_columns.1), calls=%async_computation.1 | async-start | bytes 3145728 | tf_op jit(solution)/shard_map/all_to_all | solution.py:442
  53.3 0.0 copy-done.12
  53.3 0.1 broadcast_in_dim_tile.9.bias_one
  53.4 0.0 copy-done.13
  53.4 0.1 broadcast_in_dim_tile.10.bias_two
  53.5 0.0 copy-done.14
  53.5 0.1 broadcast_in_dim_tile.11.bias_three
  53.6 0.0 copy-done.11
  53.6 0.0 copy-done.3
  53.6 0.0 copy-done.5
  53.6 0.0 copy-done.6
  53.6 0.0 copy-done.7
  53.7 0.0 copy-done.8
  53.7 1.2 bands.1
  54.8 0.0 copy-start
  54.9 1.0 copy-done
  55.9 1.0 copy-done.1
  56.9 0.8 copy-done.2
  57.7 0.0 copy-done.10
  57.7 17.9 %all-to-all-done.1.cost_ref = bf16[16,64,768]{2,1,0:T(8,128)(2,1)S(1)} async-done(((bf16[16,64,768]{2,1,0:T(8,128)(2,1)}), bf16[16,64,768]{2,1,0:T(8,128)(2,1)S(1)}, u32[]{:S(2)}, u32[]{:S(2)}) %all-to-all-start.1) | async-done | bytes 1572896 | tf_op jit(solution)/shard_map/all_to_all | solution.py:442
  75.7 22.3 %encode.1 = f32[64,640]{1,0:T(8,128)S(1)} custom-call(bf16[16,64,768]{2,1,0:T(8,128)(2,1)S(1)} %all-to-all-done.1.cost_ref, bf16[384,768]{1,0:T(8,128)(2,1)} %copy-done.2, bf16[2304,256]{1,0:T(8,128)(2,1)} %copy-done, bf16[2304,256]{1,0:T(8,128)(2,1)} %copy-done.1, bf16[512,128]{1,0:T(8,128)(2,1)S(1)} %get-tuple-element.32.query_ref, ...), custom_call_target="tpu_custom_call" | custom-call | tf_op jit(solution)/shard_map/encode/pallas_call | solution.py:33
  98.0 10.9 %all_to_all.20.parts_ref = f32[8,8,640]{2,1,0:T(8,128)S(1)} all-to-all(f32[8,8,640]{2,1,0:T(8,128)S(1)} %bitcast.9), channel_id=1, replica_groups=mesh['zh'=4,'xy'=16,'tile'=8] {'tile'}, dimensions={0} | all-to-all | bytes 327680 | tf_op jit(solution)/shard_map/all_to_all | solution.py:444
  108.8 0.0 copy-done.4
  108.8 0.3 combine.1
  109.2 9.8 %all_to_all.21 = f32[8,8,512]{2,1,0:T(8,128)S(1)} all-to-all(f32[8,8,512]{2,1,0:T(8,128)S(1)} %combine.1), channel_id=1, replica_groups=mesh['zh'=4,'xy'=16,'tile'=8] {'tile'}, dimensions={0} | all-to-all | bytes 262144 | tf_op jit(solution)/shard_map/all_to_all | solution.py:447
  119.0 1.2 valued.1
  (9 shorter events, 0.0 us)
Async XLA Ops:
  0.0 9.2 %copy-start.9 = (bf16[2,64,256]{2,1,0:T(8,128)(2,1)S(1)}, bf16[2,64,256]{2,1,0:T(8,128)(2,1)}, u32[]{:S(2)}) copy-start(bf16[2,64,256]{2,1,0:T(8,128)(2,1)} %param.14) | copy-start | bytes 196612
  1.6 39.6 %all-to-all-start = ((bf16[16,64,256]{2,1,0:T(8,128)(2,1)}), bf16[16,64,256]{2,1,0:T(8,128)(2,1)S(1)}, u32[]{:S(2)}, u32[]{:S(2)}) async-start(bf16[16,64,256]{2,1,0:T(8,128)(2,1)} %broadcast_in_dim.2), calls=%async_computation | async-start | bytes 1048576 | tf_op jit(solution)/shard_map/all_to_all | solution.py:430
  33.8 7.9 %collective-permute-start = (bf16[4,2,16,256]{3,2,1,0:T(8,128)(2,1)S(1)}, bf16[4,2,16,256]{3,2,1,0:T(8,128)(2,1)S(1)}, u32[]{:S(2)}, u32[]{:S(2)}) collective-permute-start(bf16[4,2,16,256]{3,2,1,0:T(8,128)(2,1)S(1)} %get-tuple-element.38), channel_id=1, source_target_pairs={{0,1},{1,2},{2,3},{3,4},{4,5},{5,6},{6,7},{8,9},{9,10},{10,11},{11... | collective-permute-start | bytes 196616 | tf_op jit(solution)/shard_map/ppermute | solution.py:435
  39.3 5.6 %collective-permute-start.1 = (bf16[4,2,16,256]{3,2,1,0:T(8,128)(2,1)S(1)}, bf16[4,2,16,256]{3,2,1,0:T(8,128)(2,1)S(1)}, u32[]{:S(2)}, u32[]{:S(2)}) collective-permute-start(bf16[4,2,16,256]{3,2,1,0:T(8,128)(2,1)S(1)} %get-tuple-element.37), channel_id=1, source_target_pairs={{1,0},{2,1},{3,2},{4,3},{5,4},{6,5},{7,6},{9,8},{10,9},{11,10},{12... | collective-permute-start | bytes 196616 | tf_op jit(solution)/shard_map/ppermute | solution.py:436
  46.4 6.9 %copy-start.12 = (f32[16]{0:T(128)S(1)}, f32[16]{0:T(128)}, u32[]{:S(2)}) copy-start(f32[16]{0:T(128)} %param.17) | copy-start | bytes 196
  46.4 7.0 %copy-start.13 = (f32[32]{0:T(128)S(1)}, f32[32]{0:T(128)}, u32[]{:S(2)}) copy-start(f32[32]{0:T(128)} %param.19) | copy-start | bytes 388
  46.4 7.1 %copy-start.14 = (f32[64]{0:T(128)S(1)}, f32[64]{0:T(128)}, u32[]{:S(2)}) copy-start(f32[64]{0:T(128)} %param.21) | copy-start | bytes 772
  46.4 7.2 %copy-start.11 = (bf16[6,6,1,16]{3,1,2,0:T(8,128)(2,1)S(1)}, bf16[6,6,1,16]{3,1,2,0:T(8,128)(2,1)}, u32[]{:S(2)}) copy-start(bf16[6,6,1,16]{3,1,2,0:T(8,128)(2,1)} %param.16) | copy-start | bytes 3460
  46.4 7.2 %copy-start.3 = (bf16[6,6,32,64]{3,2,1,0:T(8,128)(2,1)S(1)}, bf16[6,6,32,64]{3,2,1,0:T(8,128)(2,1)}, u32[]{:S(2)}) copy-start(bf16[6,6,32,64]{3,2,1,0:T(8,128)(2,1)} %param.20) | copy-start | bytes 442372
  46.5 7.2 %copy-start.5 = (bf16[6,6,16,32]{3,2,1,0:T(8,128)(2,1)S(1)}, bf16[6,6,16,32]{3,2,1,0:T(8,128)(2,1)}, u32[]{:S(2)}) copy-start(bf16[6,6,16,32]{3,2,1,0:T(8,128)(2,1)} %param.18) | copy-start | bytes 110596
  46.5 7.2 %copy-start.6 = (f32[16,8,128]{2,1,0:T(8,128)S(1)}, f32[16,8,128]{2,1,0:T(8,128)}, u32[]{:S(2)}) copy-start(f32[16,8,128]{2,1,0:T(8,128)} %pos_key_ref) | copy-start | bytes 196612
  46.5 7.2 %copy-start.7 = (f32[64,128]{1,0:T(8,128)S(1)}, f32[64,128]{1,0:T(8,128)}, u32[]{:S(2)}) copy-start(f32[64,128]{1,0:T(8,128)} %key_ref.1) | copy-start | bytes 98308
  46.5 7.2 %copy-start.8 = (f32[8,128]{1,0:T(8,128)S(1)}, f32[8,128]{1,0:T(8,128)}, u32[]{:S(2)}) copy-start(f32[8,128]{1,0:T(8,128)} %latents_ref) | copy-start | bytes 12292
  46.5 11.2 %copy-start.10 = (f32[64,128]{1,0:T(8,128)S(1)}, f32[64,128]{1,0:T(8,128)}, u32[]{:S(2)}) copy-start(f32[64,128]{1,0:T(8,128)} %param.25) | copy-start | bytes 98308
  46.5 29.2 %all-to-all-start.1 = ((bf16[16,64,768]{2,1,0:T(8,128)(2,1)}), bf16[16,64,768]{2,1,0:T(8,128)(2,1)S(1)}, u32[]{:S(2)}, u32[]{:S(2)}) async-start(bf16[16,64,768]{2,1,0:T(8,128)(2,1)} %halo_columns.1), calls=%async_computation.1 | async-start | bytes 3145728 | tf_op jit(solution)/shard_map/all_to_all | solution.py:442
  54.8 1.0 copy-start
  55.9 1.0 copy-start.1
  56.9 0.8 copy-start.2
  75.7 33.2 %copy-start.4 = (f32[128,512]{1,0:T(8,128)S(1)}, f32[128,512]{1,0:T(8,128)}, u32[]{:S(2)}) copy-start(f32[128,512]{1,0:T(8,128)} %constant.5.clone.spread_ref) | copy-start | bytes 786436

commit v7 on v6

--- a/solution.py
+++ b/solution.py
@@ -45,10 +45,9 @@
     return pltpu.VMEM(shape, dtype)
 
 
-def gelu(x):
+def gelu_twice(x):
     inner = x * (math.sqrt(2.0 / math.pi) + (math.sqrt(2.0 / math.pi) * 0.044715) * (x * x))
-    half = 0.5 * x
-    return half + half * jnp.tanh(inner)
+    return x + x * jnp.tanh(inner)
 
 
 def nt_dot(a, b):
@@ -100,7 +99,7 @@
             total = jnp.zeros((rows, 128), f32)
             for b in range(128 // block):
                 top = step * (b + t * (128 // block))
-                piece = [jnp.where(lane == b, tile, 0.0)]
+                piece = [jnp.where(lane == b, 0.5 * tile, 0.0)]
                 if top:
                     piece = [jnp.zeros((top, 128), f32)] + piece
                 if rows - top - depth:
@@ -249,7 +248,7 @@
                 axis=1,
             )
             lanes = slice(256 * n, 256 * (n + 1))
-            value = gelu(mm(left, one_ref[:, lanes]) + bias_one[:, lanes])
+            value = gelu_twice(mm(left, one_ref[:, lanes]) + bias_one[:, lanes])
             hidden_one[pl.ds(i * (step // 2), step // 2), :, :, lanes] = value.astype(bf16).reshape(
                 step // 2, 2, count, 256
             )
@@ -276,7 +275,7 @@
             right, bias = (two_ref[...], bias_two[...])
             if n == 2:
                 right, bias = (short, bias_two[:, :128])
-            value = gelu(mm(taps(hidden_one, h, step, lanes), right) + bias)
+            value = gelu_twice(mm(taps(hidden_one, h, step, lanes), right) + bias)
             lanes = slice(256 * n, 256 * n + value.shape[1])
             hidden_two[pl.ds(i * (step // 2), step // 2), :, :, lanes] = value.astype(bf16).reshape(
                 step // 2, 2, count, -1

time: 121 us -> 119 us (0.983)
  no operation moved by 1% of the time
where the time goes in v7:
time: 119 us
  blocking collectives  45.2 us (38%)
  Pallas kernels  25.8 us (22%)
  starting transfers between devices  21.8 us (18%)
  waiting for transfers between devices  21.1 us (18%)
  local copies, waits for them, and re-layouts  4.86 us (4%)
    pallas_call x6, Pallas kernels, call(): pl.pallas_call(body, out_shape=out_shape, in_specs=[hbm if i in far else...  25.8 us
    all_gather x1, blocking collectives, on_device(): rows = lax.all_gather(target, 'zh', axis=0)  24.5 us
    all_to_all x1, waiting for transfers between devices, on_device(): parts = encode(lax.all_to_all(cost, 'xy', 0, 0), *prepared)  17.9 us
    all_to_all x1, blocking collectives, on_device(): lax.all_to_all(parts.reshape(tiles, -1, parts.shape[1]), 'tile', 0, 0)  10.9 us
    all_to_all x1, blocking collectives, on_device(): attended = lax.all_to_all(combine(parts, spread), 'tile', 0, 0)  9.79 us
    all_to_all x1, starting transfers between devices, on_device(): every = lax.all_to_all(copies, 'xy', 0, 0)  7.58 us
    all_to_all x1, starting transfers between devices, on_device(): parts = encode(lax.all_to_all(cost, 'xy', 0, 0), *prepared)  6.8 us
    ppermute x1, starting transfers between devices, on_device(): left = lax.ppermute(rows[:, :, width - HALO:], 'tile', up)  5.53 us
  transfers between devices with their start and end apart: 4, of which 2 were waited for; matrix products, arithmetic and copies ran while one was open for 0% of the time, Pallas kernels for 1%

profile of v7, /device:TPU:1, one launch (start us, length us, event | category | flops | bytes accessed | tf_op | source)
XLA Modules:
  0.0 119.0 jit_solution(4946702997761917863)
XLA Ops:
  0.0 0.0 copy-start.9
  0.0 1.6 %broadcast_in_dim.2 = bf16[16,64,256]{2,1,0:T(8,128)(2,1)} broadcast(bf16[64,256]{1,0:T(8,128)(2,1)} %param.15), dimensions={1,2} | broadcast | bytes 557056 | tf_op jit(solution)/shard_map/broadcast_in_dim | solution.py:427
  1.6 7.6 %all-to-all-start = ((bf16[16,64,256]{2,1,0:T(8,128)(2,1)}), bf16[16,64,256]{2,1,0:T(8,128)(2,1)S(1)}, u32[]{:S(2)}, u32[]{:S(2)}) async-start(bf16[16,64,256]{2,1,0:T(8,128)(2,1)} %broadcast_in_dim.2), calls=%async_computation | async-start | bytes 1048576 | tf_op jit(solution)/shard_map/all_to_all | solution.py:429
  9.2 0.0 copy-done.9
  9.3 24.5 %all-gather = bf16[8,64,256]{2,1,0:T(8,128)(2,1)S(1)} all-gather(bf16[2,64,256]{2,1,0:T(8,128)(2,1)S(1)} %copy-done.9), channel_id=2, replica_groups=mesh['zh'=4,'xy'=16,'tile'=8] {'zh'}, dimensions={0}, use_global_device_ids=true | all-gather | bytes 327680 | tf_op jit(solution)/shard_map/all_gather | solution.py:430
  33.8 5.5 %collective-permute-start = (bf16[4,2,16,256]{3,2,1,0:T(8,128)(2,1)S(1)}, bf16[4,2,16,256]{3,2,1,0:T(8,128)(2,1)S(1)}, u32[]{:S(2)}, u32[]{:S(2)}) collective-permute-start(bf16[4,2,16,256]{3,2,1,0:T(8,128)(2,1)S(1)} %get-tuple-element.38), channel_id=1, source_target_pairs={{0,1},{1,2},{2,3},{3,4},{4,5},{5,6},{6,7},{8,9},{9,10},{10,11},{11... | collective-permute-start | bytes 196616 | tf_op jit(solution)/shard_map/ppermute | solution.py:434
  39.3 1.9 %collective-permute-start.1 = (bf16[4,2,16,256]{3,2,1,0:T(8,128)(2,1)S(1)}, bf16[4,2,16,256]{3,2,1,0:T(8,128)(2,1)S(1)}, u32[]{:S(2)}, u32[]{:S(2)}) collective-permute-start(bf16[4,2,16,256]{3,2,1,0:T(8,128)(2,1)S(1)} %get-tuple-element.37), channel_id=1, source_target_pairs={{1,0},{2,1},{3,2},{4,3},{5,4},{6,5},{7,6},{9,8},{10,9},{11,10},{12... | collective-permute-start | bytes 196616 | tf_op jit(solution)/shard_map/ppermute | solution.py:435
  41.3 0.0 all-to-all-done.sources_ref
  41.3 0.5 own_columns.1.own_ref
  41.8 0.0 collective-permute-done.left_ref
  41.8 3.2 %collective-permute-done.1.right_ref = bf16[4,2,16,256]{3,2,1,0:T(8,128)(2,1)S(1)} collective-permute-done((bf16[4,2,16,256]{3,2,1,0:T(8,128)(2,1)S(1)}, bf16[4,2,16,256]{3,2,1,0:T(8,128)(2,1)S(1)}, u32[]{:S(2)}, u32[]{:S(2)}) %collective-permute-start.1) | collective-permute-done | bytes 65568 | tf_op jit(solution)/shard_map/ppermute | solution.py:435
  44.9 1.5 %halo_columns.1 = bf16[16,64,768]{2,1,0:T(8,128)(2,1)} custom-call(bf16[4,2,16,256]{3,2,1,0:T(8,128)(2,1)S(1)} %collective-permute-done.left_ref, bf16[4,2,16,256]{3,2,1,0:T(8,128)(2,1)S(1)} %collective-permute-done.1.right_ref, bf16[16,64,256]{2,1,0:T(8,128)(2,1)S(1)} %all-to-all-done.sources_ref, bf16[16,64,512]{2,1,0:T(8,128)(2,1)S(1)} %own_columns.1.own_ref), custom_call_target="tpu_custom_call" | custom-call | tf_op jit(solution)/shard_map/halo_columns/pallas_call | solution.py:33
  46.4 0.0 copy-start.12
  46.4 0.0 copy-start.13
  46.4 0.0 copy-start.14
  46.4 0.0 copy-start.11
  46.4 0.0 copy-start.3
  46.5 0.0 copy-start.5
  46.5 0.0 copy-start.6
  46.5 0.0 copy-start.7
  46.5 0.0 copy-start.8
  46.5 0.0 copy-start.10
  46.5 6.8 %all-to-all-start.1 = ((bf16[16,64,768]{2,1,0:T(8,128)(2,1)}), bf16[16,64,768]{2,1,0:T(8,128)(2,1)S(1)}, u32[]{:S(2)}, u32[]{:S(2)}) async-start(bf16[16,64,768]{2,1,0:T(8,128)(2,1)} %halo_columns.1), calls=%async_computation.1 | async-start | bytes 3145728 | tf_op jit(solution)/shard_map/all_to_all | solution.py:441
  53.3 0.0 copy-done.12
  53.3 0.1 broadcast_in_dim_tile.9.bias_one
  53.4 0.0 copy-done.13
  53.4 0.1 broadcast_in_dim_tile.10.bias_two
  53.5 0.0 copy-done.14
  53.5 0.1 broadcast_in_dim_tile.11.bias_three
  53.6 0.0 copy-done.11
  53.6 0.0 copy-done.3
  53.6 0.0 copy-done.5
  53.6 0.0 copy-done.6
  53.7 0.0 copy-done.7
  53.7 0.0 copy-done.8
  53.7 1.2 %bands.1 = (bf16[384,768]{1,0:T(8,128)(2,1)S(1)}, bf16[2304,256]{1,0:T(8,128)(2,1)S(1)}, bf16[2304,256]{1,0:T(8,128)(2,1)S(1)}, bf16[512,128]{1,0:T(8,128)(2,1)S(1)}, f32[16,128]{1,0:T(8,128)S(1)}) custom-call(bf16[36,16]{1,0:T(8,128)(2,1)S(1)} %reshape.19.one_ref, bf16[576,32]{1,0:T(8,128)(2,1)S(1)} %bitcast.12, bf16[1152,64]{1,0:T(8,128)(2,1)S(1)} %bitcast.11, ...), custom_call_target="tpu_custom_call" | custom-call | tf_op jit(solution)/shard_map/bands/pallas_call | solution.py:33
  54.9 0.0 copy-start
  54.9 1.0 copy-done
  55.9 1.0 copy-done.1
  57.0 0.8 copy-done.2
  57.8 0.0 copy-done.10
  57.8 17.9 %all-to-all-done.1.cost_ref = bf16[16,64,768]{2,1,0:T(8,128)(2,1)S(1)} async-done(((bf16[16,64,768]{2,1,0:T(8,128)(2,1)}), bf16[16,64,768]{2,1,0:T(8,128)(2,1)S(1)}, u32[]{:S(2)}, u32[]{:S(2)}) %all-to-all-start.1) | async-done | bytes 1572896 | tf_op jit(solution)/shard_map/all_to_all | solution.py:441
  75.7 21.1 %encode.1 = f32[64,640]{1,0:T(8,128)S(1)} custom-call(bf16[16,64,768]{2,1,0:T(8,128)(2,1)S(1)} %all-to-all-done.1.cost_ref, bf16[384,768]{1,0:T(8,128)(2,1)} %copy-done.2, bf16[2304,256]{1,0:T(8,128)(2,1)} %copy-done, bf16[2304,256]{1,0:T(8,128)(2,1)} %copy-done.1, bf16[512,128]{1,0:T(8,128)(2,1)S(1)} %get-tuple-element.32.query_ref, ...), custom_call_target="tpu_custom_call" | custom-call | tf_op jit(solution)/shard_map/encode/pallas_call | solution.py:33
  96.8 10.9 %all_to_all.20.parts_ref = f32[8,8,640]{2,1,0:T(8,128)S(1)} all-to-all(f32[8,8,640]{2,1,0:T(8,128)S(1)} %bitcast.9), channel_id=1, replica_groups=mesh['zh'=4,'xy'=16,'tile'=8] {'tile'}, dimensions={0} | all-to-all | bytes 327680 | tf_op jit(solution)/shard_map/all_to_all | solution.py:443
  107.7 0.0 copy-done.4
  107.7 0.3 combine.1
  108.0 9.8 %all_to_all.21 = f32[8,8,512]{2,1,0:T(8,128)S(1)} all-to-all(f32[8,8,512]{2,1,0:T(8,128)S(1)} %combine.1), channel_id=1, replica_groups=mesh['zh'=4,'xy'=16,'tile'=8] {'tile'}, dimensions={0} | all-to-all | bytes 262144 | tf_op jit(solution)/shard_map/all_to_all | solution.py:446
  117.8 1.2 valued.1
  (9 shorter events, 0.0 us)
Async XLA Ops:
  0.0 9.2 %copy-start.9 = (bf16[2,64,256]{2,1,0:T(8,128)(2,1)S(1)}, bf16[2,64,256]{2,1,0:T(8,128)(2,1)}, u32[]{:S(2)}) copy-start(bf16[2,64,256]{2,1,0:T(8,128)(2,1)} %param.14) | copy-start | bytes 196612
  1.6 39.6 %all-to-all-start = ((bf16[16,64,256]{2,1,0:T(8,128)(2,1)}), bf16[16,64,256]{2,1,0:T(8,128)(2,1)S(1)}, u32[]{:S(2)}, u32[]{:S(2)}) async-start(bf16[16,64,256]{2,1,0:T(8,128)(2,1)} %broadcast_in_dim.2), calls=%async_computation | async-start | bytes 1048576 | tf_op jit(solution)/shard_map/all_to_all | solution.py:429
  33.8 8.0 %collective-permute-start = (bf16[4,2,16,256]{3,2,1,0:T(8,128)(2,1)S(1)}, bf16[4,2,16,256]{3,2,1,0:T(8,128)(2,1)S(1)}, u32[]{:S(2)}, u32[]{:S(2)}) collective-permute-start(bf16[4,2,16,256]{3,2,1,0:T(8,128)(2,1)S(1)} %get-tuple-element.38), channel_id=1, source_target_pairs={{0,1},{1,2},{2,3},{3,4},{4,5},{5,6},{6,7},{8,9},{9,10},{10,11},{11... | collective-permute-start | bytes 196616 | tf_op jit(solution)/shard_map/ppermute | solution.py:434
  39.3 5.6 %collective-permute-start.1 = (bf16[4,2,16,256]{3,2,1,0:T(8,128)(2,1)S(1)}, bf16[4,2,16,256]{3,2,1,0:T(8,128)(2,1)S(1)}, u32[]{:S(2)}, u32[]{:S(2)}) collective-permute-start(bf16[4,2,16,256]{3,2,1,0:T(8,128)(2,1)S(1)} %get-tuple-element.37), channel_id=1, source_target_pairs={{1,0},{2,1},{3,2},{4,3},{5,4},{6,5},{7,6},{9,8},{10,9},{11,10},{12... | collective-permute-start | bytes 196616 | tf_op jit(solution)/shard_map/ppermute | solution.py:435
  46.4 6.9 %copy-start.12 = (f32[16]{0:T(128)S(1)}, f32[16]{0:T(128)}, u32[]{:S(2)}) copy-start(f32[16]{0:T(128)} %param.17) | copy-start | bytes 196
  46.4 7.0 %copy-start.13 = (f32[32]{0:T(128)S(1)}, f32[32]{0:T(128)}, u32[]{:S(2)}) copy-start(f32[32]{0:T(128)} %param.19) | copy-start | bytes 388
  46.4 7.1 %copy-start.14 = (f32[64]{0:T(128)S(1)}, f32[64]{0:T(128)}, u32[]{:S(2)}) copy-start(f32[64]{0:T(128)} %param.21) | copy-start | bytes 772
  46.4 7.2 %copy-start.11 = (bf16[6,6,1,16]{3,1,2,0:T(8,128)(2,1)S(1)}, bf16[6,6,1,16]{3,1,2,0:T(8,128)(2,1)}, u32[]{:S(2)}) copy-start(bf16[6,6,1,16]{3,1,2,0:T(8,128)(2,1)} %param.16) | copy-start | bytes 3460
  46.4 7.2 %copy-start.3 = (bf16[6,6,32,64]{3,2,1,0:T(8,128)(2,1)S(1)}, bf16[6,6,32,64]{3,2,1,0:T(8,128)(2,1)}, u32[]{:S(2)}) copy-start(bf16[6,6,32,64]{3,2,1,0:T(8,128)(2,1)} %param.20) | copy-start | bytes 442372
  46.5 7.2 %copy-start.5 = (bf16[6,6,16,32]{3,2,1,0:T(8,128)(2,1)S(1)}, bf16[6,6,16,32]{3,2,1,0:T(8,128)(2,1)}, u32[]{:S(2)}) copy-start(bf16[6,6,16,32]{3,2,1,0:T(8,128)(2,1)} %param.18) | copy-start | bytes 110596
  46.5 7.2 %copy-start.6 = (f32[16,8,128]{2,1,0:T(8,128)S(1)}, f32[16,8,128]{2,1,0:T(8,128)}, u32[]{:S(2)}) copy-start(f32[16,8,128]{2,1,0:T(8,128)} %pos_key_ref) | copy-start | bytes 196612
  46.5 7.2 %copy-start.7 = (f32[64,128]{1,0:T(8,128)S(1)}, f32[64,128]{1,0:T(8,128)}, u32[]{:S(2)}) copy-start(f32[64,128]{1,0:T(8,128)} %key_ref.1) | copy-start | bytes 98308
  46.5 7.2 %copy-start.8 = (f32[8,128]{1,0:T(8,128)S(1)}, f32[8,128]{1,0:T(8,128)}, u32[]{:S(2)}) copy-start(f32[8,128]{1,0:T(8,128)} %latents_ref) | copy-start | bytes 12292
  46.5 11.3 %copy-start.10 = (f32[64,128]{1,0:T(8,128)S(1)}, f32[64,128]{1,0:T(8,128)}, u32[]{:S(2)}) copy-start(f32[64,128]{1,0:T(8,128)} %param.25) | copy-start | bytes 98308
  46.5 29.2 %all-to-all-start.1 = ((bf16[16,64,768]{2,1,0:T(8,128)(2,1)}), bf16[16,64,768]{2,1,0:T(8,128)(2,1)S(1)}, u32[]{:S(2)}, u32[]{:S(2)}) async-start(bf16[16,64,768]{2,1,0:T(8,128)(2,1)} %halo_columns.1), calls=%async_computation.1 | async-start | bytes 3145728 | tf_op jit(solution)/shard_map/all_to_all | solution.py:441
  54.9 1.0 copy-start
  55.9 1.0 copy-start.1
  57.0 0.8 copy-start.2
  75.7 32.0 %copy-start.4 = (f32[128,512]{1,0:T(8,128)S(1)}, f32[128,512]{1,0:T(8,128)}, u32[]{:S(2)}) copy-start(f32[128,512]{1,0:T(8,128)} %constant.5.clone.spread_ref) | copy-start | bytes 786436

commit v8 on v7

--- a/solution.py
+++ b/solution.py
@@ -74,19 +74,36 @@
     cost_of(sources_ref, jnp.concatenate(parts, axis=0), out_ref, 0)
 
 
-def halo_body(left_ref, right_ref, sources_ref, own_ref, out_ref):
-    out_ref[:, :, :OWN] = own_ref[...]
+def halo_body(left_ref, right_ref, sources_ref, _, out_ref, near, sent):
     parts = []
     for z in range(left_ref.shape[0]):
         for r in range(2):
             parts += [left_ref[z, r], right_ref[z, r]]
-    cost_of(sources_ref, jnp.concatenate(parts, axis=0), out_ref, OWN)
+    cost_of(sources_ref, jnp.concatenate(parts, axis=0), near, 0)
+    store = pltpu.make_async_copy(near, out_ref.at[:, :, pl.ds(OWN, OWN // 2)], sent)
+    store.start()
+    store.wait()
 
 
 def cost_maps(rows, left, right, sources):
-    own = call(own_body, vmem(sources.shape[:2] + (OWN,), bf16), (rows, sources), "own_columns", 16)
-    shape = vmem(sources.shape[:2] + (OWN + OWN // 2,), bf16)
-    return call(halo_body, shape, (left, right, sources, own), "halo_columns", 16)
+    shape = jax.ShapeDtypeStruct(sources.shape[:2] + (OWN + OWN // 2,), bf16)
+    own = call(own_body, shape, (rows, sources), "own_columns", 16)
+    near = pl.BlockSpec(memory_space=pltpu.VMEM)
+    hbm = pl.BlockSpec(memory_space=pltpu.HBM)
+    operands = [pltpu.with_memory_space_constraint(x, pltpu.VMEM) for x in (left, right, sources)]
+    return pl.pallas_call(
+        halo_body,
+        out_shape=shape,
+        in_specs=[near, near, near, hbm],
+        out_specs=hbm,
+        scratch_shapes=[
+            vmem(sources.shape[:2] + (OWN // 2,), bf16),
+            pltpu.SemaphoreType.DMA(()),
+        ],
+        input_output_aliases={3: 0},
+        compiler_params=pltpu.CompilerParams(vmem_limit_bytes=16 * 1024 * 1024),
+        name="halo_columns",
+    )(*operands, pltpu.with_memory_space_constraint(own, pltpu.HBM))
 
 
 def band(taps, out_ref, step, block):

time: 119 us -> 119 us (level)
  waiting for transfers between devices: 21.1 us -> 19.9 us
    pallas_call x6 -> x5, Pallas kernels: 25.8 us -> 24.3 us  [call(): pl.pallas_call(body, out_shape=out_shape, in_specs=[hbm if i in far else...]
    pallas_call x0 -> x1, Pallas kernels: none -> 1.23 us  [cost_maps(): pl.pallas_call(halo_body, out_shape=shape, in_specs=[near, near, near, hb...]
    unnamed x30 -> x32, local copies, waits for them, and re-layouts: 2.93 us -> 4.08 us
where the time goes in v8:
time: 119 us
  blocking collectives  45.2 us (38%)
  Pallas kernels  25.5 us (21%)
  starting transfers between devices  21.8 us (18%)
  waiting for transfers between devices  19.9 us (17%)
  local copies, waits for them, and re-layouts  6 us (5%)
    all_gather x1, blocking collectives, on_device(): rows = lax.all_gather(target, 'zh', axis=0)  24.5 us
    pallas_call x5, Pallas kernels, call(): pl.pallas_call(body, out_shape=out_shape, in_specs=[hbm if i in far else...  24.3 us
    all_to_all x1, waiting for transfers between devices, on_device(): parts = encode(lax.all_to_all(cost, 'xy', 0, 0), *prepared)  17.9 us
    all_to_all x1, blocking collectives, on_device(): lax.all_to_all(parts.reshape(tiles, -1, parts.shape[1]), 'tile', 0, 0)  10.9 us
    all_to_all x1, blocking collectives, on_device(): attended = lax.all_to_all(combine(parts, spread), 'tile', 0, 0)  9.79 us
    all_to_all x1, starting transfers between devices, on_device(): every = lax.all_to_all(copies, 'xy', 0, 0)  7.58 us
    all_to_all x1, starting transfers between devices, on_device(): parts = encode(lax.all_to_all(cost, 'xy', 0, 0), *prepared)  6.79 us
    ppermute x1, starting transfers between devices, on_device(): left = lax.ppermute(rows[:, :, width - HALO:], 'tile', up)  5.53 us
  transfers between devices with their start and end apart: 4, of which 2 were waited for; matrix products, arithmetic and copies ran while one was open for 0% of the time, Pallas kernels for 1%

profile of v8, /device:TPU:1, one launch (start us, length us, event | category | flops | bytes accessed | tf_op | source)
XLA Modules:
  0.0 118.8 jit_solution(5260978549141929781)
XLA Ops:
  0.0 1.6 %broadcast_in_dim.2 = bf16[16,64,256]{2,1,0:T(8,128)(2,1)} broadcast(bf16[64,256]{1,0:T(8,128)(2,1)} %param.15), dimensions={1,2} | broadcast | bytes 557056 | tf_op jit(solution)/shard_map/broadcast_in_dim | solution.py:444
  1.6 7.6 %all-to-all-start = ((bf16[16,64,256]{2,1,0:T(8,128)(2,1)}), bf16[16,64,256]{2,1,0:T(8,128)(2,1)S(1)}, u32[]{:S(2)}, u32[]{:S(2)}) async-start(bf16[16,64,256]{2,1,0:T(8,128)(2,1)} %broadcast_in_dim.2), calls=%async_computation | async-start | bytes 1048576 | tf_op jit(solution)/shard_map/all_to_all | solution.py:446
  9.2 0.0 copy-done.10
  9.2 24.5 %all-gather = bf16[8,64,256]{2,1,0:T(8,128)(2,1)S(1)} all-gather(bf16[2,64,256]{2,1,0:T(8,128)(2,1)S(1)} %copy-done.10), channel_id=2, replica_groups=mesh['zh'=4,'xy'=16,'tile'=8] {'zh'}, dimensions={0}, use_global_device_ids=true | all-gather | bytes 327680 | tf_op jit(solution)/shard_map/all_gather | solution.py:447
  33.8 5.5 %collective-permute-start = (bf16[4,2,16,256]{3,2,1,0:T(8,128)(2,1)S(1)}, bf16[4,2,16,256]{3,2,1,0:T(8,128)(2,1)S(1)}, u32[]{:S(2)}, u32[]{:S(2)}) collective-permute-start(bf16[4,2,16,256]{3,2,1,0:T(8,128)(2,1)S(1)} %get-tuple-element.38), channel_id=1, source_target_pairs={{0,1},{1,2},{2,3},{3,4},{4,5},{5,6},{6,7},{8,9},{9,10},{10,11},{11... | collective-permute-start | bytes 196616 | tf_op jit(solution)/shard_map/ppermute | solution.py:451
  39.3 1.9 %collective-permute-start.1 = (bf16[4,2,16,256]{3,2,1,0:T(8,128)(2,1)S(1)}, bf16[4,2,16,256]{3,2,1,0:T(8,128)(2,1)S(1)}, u32[]{:S(2)}, u32[]{:S(2)}) collective-permute-start(bf16[4,2,16,256]{3,2,1,0:T(8,128)(2,1)S(1)} %get-tuple-element.37), channel_id=1, source_target_pairs={{1,0},{2,1},{3,2},{4,3},{5,4},{6,5},{7,6},{9,8},{10,9},{11,10},{12... | collective-permute-start | bytes 196616 | tf_op jit(solution)/shard_map/ppermute | solution.py:452
  41.3 0.0 all-to-all-done.sources_ref
  41.3 0.5 own_columns.1._
  41.7 0.0 copy-start
  41.8 1.2 copy-done
  42.9 0.0 collective-permute-done.left_ref
  42.9 2.0 %collective-permute-done.1.right_ref = bf16[4,2,16,256]{3,2,1,0:T(8,128)(2,1)S(1)} collective-permute-done((bf16[4,2,16,256]{3,2,1,0:T(8,128)(2,1)S(1)}, bf16[4,2,16,256]{3,2,1,0:T(8,128)(2,1)S(1)}, u32[]{:S(2)}, u32[]{:S(2)}) %collective-permute-start.1) | collective-permute-done | bytes 65568 | tf_op jit(solution)/shard_map/ppermute | solution.py:452
  44.9 1.2 %halo_columns.1 = bf16[16,64,768]{2,1,0:T(8,128)(2,1)} custom-call(bf16[4,2,16,256]{3,2,1,0:T(8,128)(2,1)S(1)} %collective-permute-done.left_ref, bf16[4,2,16,256]{3,2,1,0:T(8,128)(2,1)S(1)} %collective-permute-done.1.right_ref, bf16[16,64,256]{2,1,0:T(8,128)(2,1)S(1)} %all-to-all-done.sources_ref, ...), custom_call_target="tpu_custom_call", output_to_operand_aliasing={{}: (3, {})} | custom-call | tf_op jit(solution)/shard_map/halo_columns/pallas_call | solution.py:94
  46.2 0.0 copy-start.13
  46.2 0.0 copy-start.14
  46.2 0.0 copy-start.15
  46.2 0.0 copy-start.12
  46.2 0.0 copy-start.4
  46.2 0.0 copy-start.6
  46.2 0.0 copy-start.7
  46.2 0.0 copy-start.8
  46.3 0.0 copy-start.9
  46.3 0.0 copy-start.11
  46.3 6.8 %all-to-all-start.1 = ((bf16[16,64,768]{2,1,0:T(8,128)(2,1)}), bf16[16,64,768]{2,1,0:T(8,128)(2,1)S(1)}, u32[]{:S(2)}, u32[]{:S(2)}) async-start(bf16[16,64,768]{2,1,0:T(8,128)(2,1)} %halo_columns.1), calls=%async_computation.1 | async-start | bytes 3145728 | tf_op jit(solution)/shard_map/all_to_all | solution.py:458
  53.1 0.0 copy-done.13
  53.1 0.1 broadcast_in_dim_tile.9.bias_one
  53.2 0.0 copy-done.14
  53.2 0.1 broadcast_in_dim_tile.10.bias_two
  53.3 0.0 copy-done.15
  53.3 0.1 broadcast_in_dim_tile.11.bias_three
  53.4 0.0 copy-done.12
  53.4 0.0 copy-done.4
  53.4 0.0 copy-done.6
  53.4 0.0 copy-done.7
  53.4 0.0 copy-done.8
  53.4 0.0 copy-done.9
  53.4 1.2 %bands.1 = (bf16[384,768]{1,0:T(8,128)(2,1)S(1)}, bf16[2304,256]{1,0:T(8,128)(2,1)S(1)}, bf16[2304,256]{1,0:T(8,128)(2,1)S(1)}, bf16[512,128]{1,0:T(8,128)(2,1)S(1)}, f32[16,128]{1,0:T(8,128)S(1)}) custom-call(bf16[36,16]{1,0:T(8,128)(2,1)S(1)} %reshape.19.one_ref, bf16[576,32]{1,0:T(8,128)(2,1)S(1)} %bitcast.12, bf16[1152,64]{1,0:T(8,128)(2,1)S(1)} %bitcast.11, ...), custom_call_target="tpu_custom_call" | custom-call | tf_op jit(solution)/shard_map/bands/pallas_call | solution.py:33
  54.6 0.0 copy-start.1
  54.7 1.0 copy-done.1
  55.7 1.0 copy-done.2
  56.7 0.8 copy-done.3
  57.5 0.0 copy-done.11
  57.5 17.9 %all-to-all-done.1.cost_ref = bf16[16,64,768]{2,1,0:T(8,128)(2,1)S(1)} async-done(((bf16[16,64,768]{2,1,0:T(8,128)(2,1)}), bf16[16,64,768]{2,1,0:T(8,128)(2,1)S(1)}, u32[]{:S(2)}, u32[]{:S(2)}) %all-to-all-start.1) | async-done | bytes 1572896 | tf_op jit(solution)/shard_map/all_to_all | solution.py:458
  75.4 21.1 %encode.1 = f32[64,640]{1,0:T(8,128)S(1)} custom-call(bf16[16,64,768]{2,1,0:T(8,128)(2,1)S(1)} %all-to-all-done.1.cost_ref, bf16[384,768]{1,0:T(8,128)(2,1)} %copy-done.3, bf16[2304,256]{1,0:T(8,128)(2,1)} %copy-done.1, bf16[2304,256]{1,0:T(8,128)(2,1)} %copy-done.2, bf16[512,128]{1,0:T(8,128)(2,1)S(1)} %get-tuple-element.32.query_ref, ...), custom_call_target="tpu_custom_call" | custom-call | tf_op jit(solution)/shard_map/encode/pallas_call | solution.py:33
  96.6 10.9 %all_to_all.20.parts_ref = f32[8,8,640]{2,1,0:T(8,128)S(1)} all-to-all(f32[8,8,640]{2,1,0:T(8,128)S(1)} %bitcast.9), channel_id=1, replica_groups=mesh['zh'=4,'xy'=16,'tile'=8] {'tile'}, dimensions={0} | all-to-all | bytes 327680 | tf_op jit(solution)/shard_map/all_to_all | solution.py:460
  107.5 0.3 combine.1
  107.8 9.8 %all_to_all.21 = f32[8,8,512]{2,1,0:T(8,128)S(1)} all-to-all(f32[8,8,512]{2,1,0:T(8,128)S(1)} %combine.1), channel_id=1, replica_groups=mesh['zh'=4,'xy'=16,'tile'=8] {'tile'}, dimensions={0} | all-to-all | bytes 262144 | tf_op jit(solution)/shard_map/all_to_all | solution.py:463
  117.6 1.2 valued.1
  (11 shorter events, 0.0 us)
Async XLA Ops:
  0.0 9.2 %copy-start.10 = (bf16[2,64,256]{2,1,0:T(8,128)(2,1)S(1)}, bf16[2,64,256]{2,1,0:T(8,128)(2,1)}, u32[]{:S(2)}) copy-start(bf16[2,64,256]{2,1,0:T(8,128)(2,1)} %param.14) | copy-start | bytes 196612
  1.6 39.6 %all-to-all-start = ((bf16[16,64,256]{2,1,0:T(8,128)(2,1)}), bf16[16,64,256]{2,1,0:T(8,128)(2,1)S(1)}, u32[]{:S(2)}, u32[]{:S(2)}) async-start(bf16[16,64,256]{2,1,0:T(8,128)(2,1)} %broadcast_in_dim.2), calls=%async_computation | async-start | bytes 1048576 | tf_op jit(solution)/shard_map/all_to_all | solution.py:446
  33.8 9.1 %collective-permute-start = (bf16[4,2,16,256]{3,2,1,0:T(8,128)(2,1)S(1)}, bf16[4,2,16,256]{3,2,1,0:T(8,128)(2,1)S(1)}, u32[]{:S(2)}, u32[]{:S(2)}) collective-permute-start(bf16[4,2,16,256]{3,2,1,0:T(8,128)(2,1)S(1)} %get-tuple-element.38), channel_id=1, source_target_pairs={{0,1},{1,2},{2,3},{3,4},{4,5},{5,6},{6,7},{8,9},{9,10},{10,11},{11... | collective-permute-start | bytes 196616 | tf_op jit(solution)/shard_map/ppermute | solution.py:451
  39.3 5.6 %collective-permute-start.1 = (bf16[4,2,16,256]{3,2,1,0:T(8,128)(2,1)S(1)}, bf16[4,2,16,256]{3,2,1,0:T(8,128)(2,1)S(1)}, u32[]{:S(2)}, u32[]{:S(2)}) collective-permute-start(bf16[4,2,16,256]{3,2,1,0:T(8,128)(2,1)S(1)} %get-tuple-element.37), channel_id=1, source_target_pairs={{1,0},{2,1},{3,2},{4,3},{5,4},{6,5},{7,6},{9,8},{10,9},{11,10},{12... | collective-permute-start | bytes 196616 | tf_op jit(solution)/shard_map/ppermute | solution.py:452
  41.7 1.2 copy-start
  46.2 6.9 %copy-start.13 = (f32[16]{0:T(128)S(1)}, f32[16]{0:T(128)}, u32[]{:S(2)}) copy-start(f32[16]{0:T(128)} %param.17) | copy-start | bytes 196
  46.2 7.0 %copy-start.14 = (f32[32]{0:T(128)S(1)}, f32[32]{0:T(128)}, u32[]{:S(2)}) copy-start(f32[32]{0:T(128)} %param.19) | copy-start | bytes 388
  46.2 7.1 %copy-start.15 = (f32[64]{0:T(128)S(1)}, f32[64]{0:T(128)}, u32[]{:S(2)}) copy-start(f32[64]{0:T(128)} %param.21) | copy-start | bytes 772
  46.2 7.2 %copy-start.12 = (bf16[6,6,1,16]{3,1,2,0:T(8,128)(2,1)S(1)}, bf16[6,6,1,16]{3,1,2,0:T(8,128)(2,1)}, u32[]{:S(2)}) copy-start(bf16[6,6,1,16]{3,1,2,0:T(8,128)(2,1)} %param.16) | copy-start | bytes 3460
  46.2 7.2 %copy-start.4 = (bf16[6,6,32,64]{3,2,1,0:T(8,128)(2,1)S(1)}, bf16[6,6,32,64]{3,2,1,0:T(8,128)(2,1)}, u32[]{:S(2)}) copy-start(bf16[6,6,32,64]{3,2,1,0:T(8,128)(2,1)} %param.20) | copy-start | bytes 442372
  46.2 7.2 %copy-start.6 = (bf16[6,6,16,32]{3,2,1,0:T(8,128)(2,1)S(1)}, bf16[6,6,16,32]{3,2,1,0:T(8,128)(2,1)}, u32[]{:S(2)}) copy-start(bf16[6,6,16,32]{3,2,1,0:T(8,128)(2,1)} %param.18) | copy-start | bytes 110596
  46.2 7.2 %copy-start.7 = (f32[16,8,128]{2,1,0:T(8,128)S(1)}, f32[16,8,128]{2,1,0:T(8,128)}, u32[]{:S(2)}) copy-start(f32[16,8,128]{2,1,0:T(8,128)} %pos_key_ref) | copy-start | bytes 196612
  46.2 7.2 %copy-start.8 = (f32[64,128]{1,0:T(8,128)S(1)}, f32[64,128]{1,0:T(8,128)}, u32[]{:S(2)}) copy-start(f32[64,128]{1,0:T(8,128)} %key_ref.1) | copy-start | bytes 98308
  46.3 7.2 %copy-start.9 = (f32[8,128]{1,0:T(8,128)S(1)}, f32[8,128]{1,0:T(8,128)}, u32[]{:S(2)}) copy-start(f32[8,128]{1,0:T(8,128)} %latents_ref) | copy-start | bytes 12292
  46.3 11.3 %copy-start.11 = (f32[64,128]{1,0:T(8,128)S(1)}, f32[64,128]{1,0:T(8,128)}, u32[]{:S(2)}) copy-start(f32[64,128]{1,0:T(8,128)} %param.25) | copy-start | bytes 98308
  46.3 29.2 %all-to-all-start.1 = ((bf16[16,64,768]{2,1,0:T(8,128)(2,1)}), bf16[16,64,768]{2,1,0:T(8,128)(2,1)S(1)}, u32[]{:S(2)}, u32[]{:S(2)}) async-start(bf16[16,64,768]{2,1,0:T(8,128)(2,1)} %halo_columns.1), calls=%async_computation.1 | async-start | bytes 3145728 | tf_op jit(solution)/shard_map/all_to_all | solution.py:458
  54.6 1.0 copy-start.1
  55.7 1.0 copy-start.2
  56.7 0.8 copy-start.3
  75.4 32.0 %copy-start.5 = (f32[128,512]{1,0:T(8,128)S(1)}, f32[128,512]{1,0:T(8,128)}, u32[]{:S(2)}) copy-start(f32[128,512]{1,0:T(8,128)} %constant.5.clone.spread_ref) | copy-start | bytes 786436
